TPU v7x, 512 devices: a whole 4x4x16 slice. The times are simulated.
512 devices in a mesh: seq: 64 (over z, x), head: 8 (over y, core).
Axes of the slice: x: 4, y: 4, z: 16, core: 2. Of those that a mesh axis runs over, the one named last changes fastest.
Arguments:
- x_in: bfloat16 [16384, 2048], P('seq', 'head'), may hold values from -45 to 45
- gate_in: bfloat16 [16384, 2048], P('seq', 'head'), may hold values from -6 to 6
- b_in: bfloat16 [16384, 128], P('seq'), may hold values from -0.375 to 0.375
- c_in: bfloat16 [16384, 128], P('seq'), may hold values from -0.375 to 0.375
- decay_fwd: float32 [32, 16384], P('head', 'seq'), may hold values from -1 to 0
- decay_bwd: float32 [32, 16384], P('head', 'seq'), may hold values from -1 to 0
- skip_gain: float32 [32], P('head'), may hold values from 0.5 to 1.5
- norm_gain: float32 [2048], P('head'), may hold values from 0.1 to 1.9
- w_out: bfloat16 [2048, 1024], P('head'), may hold values from -0.125 to 0.125
- d_out: bfloat16 [16384, 1024], P('seq'), may hold values from -6 to 6
Outputs:
- grad_x: bfloat16 [16384, 2048], P('seq', 'head')
- grad_z: bfloat16 [16384, 2048], P('seq', 'head')
- grad_b: float32 [16384, 128], P('seq')
- grad_c: float32 [16384, 128], P('seq')
- grad_w: float32 [2048, 1024], P('head')
All inputs are finite; a program needn't handle non-finite values.
Results may differ from a plain program's by a relative error of at most 0.0029.
Values sent between devices are 32-bit elements; how exact they have to be, the bound alone decides.
No kernel may reach another device: no remote copies, remote signals or barrier semaphores. Data moves between devices by JAX's collectives and lax.ppermute only.
A program may use at most 64 MiB of HBM per device.

v0:
```python
import jax
import jax.numpy as jnp
from jax import lax
from jax.sharding import PartitionSpec as P

HEAD_DIM = 64
INNER = 2048


exact_mode = lax.Precision.HIGHEST
eps_norm = 1e-05
weight_scale = 0.0078125


def prefix(shard, axis, combine, identity, reverse):
    devices, index = (lax.axis_size(axis), lax.axis_index(axis))
    everything = jax.tree.map(lambda part: lax.all_gather(part, axis), shard)
    start = jax.tree.map(
        lambda part, zero: jnp.broadcast_to(jnp.asarray(zero, part.dtype), part.shape),
        shard,
        identity,
    )

    def step(k, before):
        at = devices - 1 - k if reverse else k
        reached = at > index if reverse else at < index
        new = combine(before, jax.tree.map(lambda part: part[at], everything))
        return jax.tree.map(lambda a, b: jnp.where(reached, a, b), new, before)

    return lax.fori_loop(0, devices, step, start)


def link_states(earlier, after_one):
    return (after_one[0] + after_one[1][:, None, None] * earlier[0], earlier[1] * after_one[1])


def carry_up(local_state, decay_total):
    identity = (jnp.zeros_like(local_state), jnp.ones_like(decay_total))
    return prefix((local_state, decay_total), "seq", link_states, identity, False)[0]


def carry_down(local_state, decay_total):
    identity = (jnp.zeros_like(local_state), jnp.ones_like(decay_total))
    return prefix((local_state, decay_total), "seq", link_states, identity, True)[0]


def body(x_in, gate_in, b_in, c_in, decay_fwd, decay_bwd, skip_gain, norm_gain, w_out, d_out):
    frames = x_in.shape[0]
    head_count = decay_fwd.shape[0]
    signal = x_in.astype(jnp.float32).reshape(frames, head_count, HEAD_DIM)
    b_rows = b_in.astype(jnp.float32)
    c_rows = c_in.astype(jnp.float32)
    fwd_cumul = jnp.cumsum(decay_fwd, axis=1)
    bwd_cumul = jnp.cumsum(decay_bwd, axis=1)
    bwd_excl = bwd_cumul - decay_bwd
    fwd_end = fwd_cumul[:, -1:]
    bwd_end = bwd_cumul[:, -1:]
    positions = jnp.arange(frames)
    causal_mask = positions[:, None] >= positions[None, :]
    anti_mask = positions[:, None] <= positions[None, :]
    weights = jnp.exp(
        jnp.where(causal_mask[None], fwd_cumul[:, :, None] - fwd_cumul[:, None, :], -jnp.inf)
    )
    weights = weights + jnp.exp(
        jnp.where(anti_mask[None], bwd_excl[:, None, :] - bwd_excl[:, :, None], -jnp.inf)
    )
    scores = jnp.dot(c_rows, b_rows.T, precision=exact_mode)
    pair_weights = weights * scores[None]
    within = jnp.einsum("hts,shp->thp", pair_weights, signal, precision=exact_mode)
    tail_f = jnp.exp(fwd_end - fwd_cumul)
    lead_b = jnp.exp(bwd_excl)
    rise_f = jnp.exp(fwd_cumul)
    rise_b = jnp.exp(bwd_end - bwd_excl)
    state_f = jnp.einsum("hs,shp,sn->hpn", tail_f, signal, b_rows, precision=exact_mode)
    state_b = jnp.einsum("hs,shp,sn->hpn", lead_b, signal, b_rows, precision=exact_mode)
    decay_f = jnp.exp(fwd_end[:, 0])
    decay_b = jnp.exp(bwd_end[:, 0])
    entry_f = carry_up(state_f, decay_f)
    entry_b = carry_down(state_b, decay_b)
    across = jnp.einsum("tn,hpn,ht->thp", c_rows, entry_f, rise_f, precision=exact_mode)
    across = across + jnp.einsum("tn,hpn,ht->thp", c_rows, entry_b, rise_b, precision=exact_mode)
    merged = (within + across + skip_gain[None, :, None] * signal).reshape(
        frames, head_count * HEAD_DIM
    )
    gate_rows = gate_in.astype(jnp.float32)
    sigmoid_z = jax.nn.sigmoid(gate_rows)
    gated_y = merged * gate_rows * sigmoid_z
    grad_n = lax.dot_general(
        d_out, w_out, (((1,), (1,)), ((), ())), preferred_element_type=jnp.float32
    )
    scaled = grad_n * norm_gain
    square_sum, cross_sum = lax.psum(
        (jnp.sum(gated_y * gated_y, axis=1), jnp.sum(gated_y * scaled, axis=1)), "head"
    )
    inv_rms = lax.rsqrt(square_sum / INNER + eps_norm)[:, None]
    normed = gated_y * inv_rms * norm_gain
    local_w = lax.dot_general(
        normed.astype(jnp.bfloat16),
        d_out,
        (((0,), (0,)), ((), ())),
        preferred_element_type=jnp.float32,
    )
    grad_g = inv_rms * scaled - gated_y * inv_rms * inv_rms * inv_rms * (cross_sum / INNER)[:, None]
    grad_y = grad_g * gate_rows * sigmoid_z
    grad_z = grad_g * merged * sigmoid_z * (1.0 + gate_rows * (1.0 - sigmoid_z))
    grad_rows = grad_y.reshape(frames, head_count, HEAD_DIM)
    back_f_local = jnp.einsum("ht,thp,tn->hpn", rise_f, grad_rows, c_rows, precision=exact_mode)
    back_b_local = jnp.einsum("ht,thp,tn->hpn", rise_b, grad_rows, c_rows, precision=exact_mode)
    dot_pairs = jnp.einsum("thp,shp->hts", grad_rows, signal, precision=exact_mode)
    pair_sum = jnp.sum(weights * dot_pairs, axis=0)
    grad_c_near = jnp.dot(pair_sum, b_rows, precision=exact_mode)
    grad_b_near = jnp.dot(pair_sum.T, c_rows, precision=exact_mode)
    exit_f = carry_down(back_f_local, decay_f)
    exit_b = carry_up(back_b_local, decay_b)
    grad_sig = jnp.einsum("hts,thp->shp", pair_weights, grad_rows, precision=exact_mode)
    grad_sig = grad_sig + jnp.einsum("hpn,sn,hs->shp", exit_f, b_rows, tail_f, precision=exact_mode)
    grad_sig = grad_sig + jnp.einsum("hpn,sn,hs->shp", exit_b, b_rows, lead_b, precision=exact_mode)
    grad_x = (grad_sig + skip_gain[None, :, None] * grad_rows).reshape(
        frames, head_count * HEAD_DIM
    )
    grad_b_far = jnp.einsum("hs,shp,hpn->sn", tail_f, signal, exit_f, precision=exact_mode)
    grad_b_far = grad_b_far + jnp.einsum(
        "hs,shp,hpn->sn", lead_b, signal, exit_b, precision=exact_mode
    )
    grad_c_far = jnp.einsum("ht,thp,hpn->tn", rise_f, grad_rows, entry_f, precision=exact_mode)
    grad_c_far = grad_c_far + jnp.einsum(
        "ht,thp,hpn->tn", rise_b, grad_rows, entry_b, precision=exact_mode
    )
    grad_b, grad_c = lax.psum((grad_b_near + grad_b_far, grad_c_near + grad_c_far), "head")
    grad_w = lax.psum(local_w, "seq") * weight_scale
    return (grad_x.astype(jnp.bfloat16), grad_z.astype(jnp.bfloat16), grad_b, grad_c, grad_w)


def solution(mesh):
    in_specs = (
        P("seq", "head"),
        P("seq", "head"),
        P("seq", None),
        P("seq", None),
        P("head", "seq"),
        P("head", "seq"),
        P("head"),
        P("head"),
        P("head", None),
        P("seq", None),
    )
    out_specs = (
        P("seq", "head"),
        P("seq", "head"),
        P("seq", None),
        P("seq", None),
        P("head", None),
    )
    return jax.shard_map(body, mesh=mesh, in_specs=in_specs, out_specs=out_specs, check_vma=False)
```

profile of v0, /device:TPU:1, one launch (start us, length us, event | category | flops | bytes accessed | tf_op | source)
XLA Modules:
  0.0 1138.6 jit_solution(3195038183309739660)
XLA Ops:
  7.3 1.1 copy.37
  9.1 1.2 reduce-window.14
  10.9 1.8 fusion.37
  13.5 1.2 reduce-window.16
  16.0 1.8 fusion.38
  18.0 1.0 copy.39
  19.0 1.1 fusion.78
  20.1 1.3 dynamic-slice
  22.3 123.3 %all-reduce.2 = (f32[256]{0:T(256)S(1)}, f32[256]{0:T(256)S(1)}) all-reduce(f32[256]{0:T(256)S(1)} %bitcast_dynamic-update-slice_fusion, f32[256]{0:T(256)S(1)} %dynamic-update-slice.1), channel_id=3, replica_groups=mesh['seq'=64,'head'=8] {'seq'}, use_global_device_ids=true, to_apply=%add | all-reduce | flops 512 | bytes 4096
  145.8 1.1 convolution_bitcast_fusion.5
  147.0 21.2 %all-gather.11.cloned.1.call-done = f32[256,64,128]{2,1,0:T(8,128)} async-done(((f32[4,64,128]{2,1,0:T(8,128)}), f32[256,64,128]{2,1,0:T(8,128)}) %all-gather.11.cloned.1.call-update) | async-done | bytes 8388624 | tf_op jit(solution)/shard_map/all_gather | solution.py:17
  168.2 66.5 %while.60 = (s32[]{:T(128)}, f32[4,64,128]{2,1,0:T(8,128)S(1)}, s32[]{:T(128)}, f32[64,4,64,128]{3,2,1,0:T(8,128)}, f32[64,4]{1,0:T(8,128)S(1)}, /*index=5*/s32[]{:T(128)}, s32[]{:T(128)}) while((s32[]{:T(128)}, f32[4,64,128]{2,1,0:T(8,128)S(1)}, s32[]{:T(128)}, f32[64,4,64,128]{3,2,1,0:T(8,128)}, f32[64,4]{1,0:T(8,128)S(1)}, ...), condition=%wide.region_5.6_spmd.clone, body=%wide.region_4.5_spmd.clone.sunk | while | flops 131076 | bytes 393377 | solution.py:30
  196.2 1.0 fusion.104
  202.5 1.0 fusion.104
  205.6 1.0 fusion.104
  234.7 88.8 %all-gather.13.cloned.1.call-done = f32[256,64,128]{2,1,0:T(8,128)} async-done(((f32[4,64,128]{2,1,0:T(8,128)}), f32[256,64,128]{2,1,0:T(8,128)}) %all-gather.13.cloned.1.call-update) | async-done | bytes 8388624 | tf_op jit(solution)/shard_map/all_gather | solution.py:17
  323.5 66.9 %while.61 = (s32[]{:T(128)}, f32[4,64,128]{2,1,0:T(8,128)S(1)}, s32[]{:T(128)}, f32[64,4,64,128]{3,2,1,0:T(8,128)}, f32[64,4]{1,0:T(8,128)S(1)}, /*index=5*/s32[]{:T(128)}, s32[]{:T(128)}, s32[]{:T(128)}, s32[]{:T(128)}) while((s32[]{:T(128)}, f32[4,64,128]{2,1,0:T(8,128)S(1)}, s32[]{:T(128)}, f32[64,4,64,128]{3,2,1,0:T(8,128)}, ...), condition=%wide.region_7.8_spmd.clone, body=%wide.region_6.7_spmd.clone.sunk | while | flops 131080 | bytes 393439 | solution.py:30
  391.4 20.3 %all-reduce.3 = (f32[256]{0:T(256)S(1)}, f32[256]{0:T(256)S(1)}) all-reduce(f32[256]{0:T(256)S(1)} %get-tuple-element.549, f32[256]{0:T(256)S(1)} %get-tuple-element.548), channel_id=1, replica_groups=mesh['seq'=64,'head'=8] {'head'}, use_global_device_ids=true, to_apply=%region_11.12 | all-reduce | flops 512 | bytes 4096 | tf_op jit(solution)/shard_map/psum | solution.py:92
  411.6 1.3 fusion.54
  415.6 1.0 fusion.4
  418.2 1.2 convolution_bitcast_fusion.2
  420.4 248.6 %all-reduce.8.cloned.1.call-done = f32[256,1024]{1,0:T(8,128)} async-done(((f32[256,1024]{1,0:T(8,128)}), f32[256,1024]{1,0:T(8,128)}) %all-reduce.8.cloned.1.call-update) | async-done | bytes 1048592 | tf_op jit(solution)/shard_map/psum | solution.py:130
  669.0 2.3 broadcast_multiply_fusion
  671.3 155.6 %all-gather.15.cloned.1.call-done = f32[256,64,128]{2,1,0:T(8,128)} async-done(((f32[4,64,128]{2,1,0:T(8,128)}), f32[256,64,128]{2,1,0:T(8,128)}) %all-gather.15.cloned.1.call-update) | async-done | bytes 8388624 | tf_op jit(solution)/shard_map/all_gather | solution.py:17
  826.9 66.9 %while.62 = (s32[]{:T(128)}, f32[4,64,128]{2,1,0:T(8,128)S(1)}, s32[]{:T(128)}, f32[64,4,64,128]{3,2,1,0:T(8,128)}, f32[64,4]{1,0:T(8,128)S(1)}, /*index=5*/s32[]{:T(128)}, s32[]{:T(128)}, s32[]{:T(128)}, s32[]{:T(128)}) while((s32[]{:T(128)}, f32[4,64,128]{2,1,0:T(8,128)S(1)}, s32[]{:T(128)}, f32[64,4,64,128]{3,2,1,0:T(8,128)}, ...), condition=%wide.region_13.14_spmd.clone, body=%wide.region_12.13_spmd.clone.sunk | while | flops 131080 | bytes 393439 | solution.py:30
  849.9 1.0 fusion.106
  893.8 89.0 %all-gather.17.cloned.1.call-done = f32[256,64,128]{2,1,0:T(8,128)} async-done(((f32[4,64,128]{2,1,0:T(8,128)}), f32[256,64,128]{2,1,0:T(8,128)}) %all-gather.17.cloned.1.call-update) | async-done | bytes 8388624 | tf_op jit(solution)/shard_map/all_gather | solution.py:17
  982.8 66.5 %while.63 = (s32[]{:T(128)}, f32[4,64,128]{2,1,0:T(8,128)S(1)}, s32[]{:T(128)}, f32[64,4,64,128]{3,2,1,0:T(8,128)}, f32[64,4]{1,0:T(8,128)S(1)}, /*index=5*/s32[]{:T(128)}, s32[]{:T(128)}) while((s32[]{:T(128)}, f32[4,64,128]{2,1,0:T(8,128)S(1)}, s32[]{:T(128)}, f32[64,4,64,128]{3,2,1,0:T(8,128)}, f32[64,4]{1,0:T(8,128)S(1)}, ...), condition=%wide.region_15.16_spmd.clone, body=%wide.region_14.15_spmd.clone.sunk | while | flops 131076 | bytes 393377 | solution.py:30
  1050.7 1.0 convolution_add_fusion.1
  1052.8 75.8 %all-reduce.10.cloned.1.call-done = (f32[256,128]{1,0:T(8,128)}, f32[256,128]{1,0:T(8,128)}) async-done(((f32[256,128]{1,0:T(8,128)}, f32[256,128]{1,0:T(8,128)}), (f32[256,128]{1,0:T(8,128)}, f32[256,128]{1,0:T(8,128)})) %all-reduce.10.cloned.1.call-update) | async-done | bytes 262160 | tf_op jit(solution)/shard_map/psum | solution.py:129
  1128.6 1.6 copy.89
  1130.2 1.6 copy.90
  (582 shorter events, 265.9 us)
Async XLA Ops:
  7.2 383.8 %copy-start = (bf16[256,1024]{1,0:T(8,128)(2,1)S(1)}, bf16[256,1024]{1,0:T(8,128)(2,1)}, u32[]{:S(2)}) copy-start(bf16[256,1024]{1,0:T(8,128)(2,1)} %param.27) | copy-start | bytes 1572868
  7.2 383.2 %copy-start.1 = (bf16[256,128]{1,0:T(8,128)(2,1)S(1)}, bf16[256,128]{1,0:T(8,128)(2,1)}, u32[]{:S(2)}) copy-start(bf16[256,128]{1,0:T(8,128)(2,1)} %param.21) | copy-start | bytes 196612
  7.2 383.5 %copy-start.3 = (f32[4]{0:T(128)S(1)}, f32[4]{0:T(128)}, u32[]{:S(2)}) copy-start(f32[4]{0:T(128)} %param.24) | copy-start | bytes 52
  7.2 383.8 %copy-start.4 = (f32[256]{0:T(256)S(1)}, f32[256]{0:T(256)}, u32[]{:S(2)}) copy-start(f32[256]{0:T(256)} %param.25) | copy-start | bytes 3076
  7.2 383.8 %copy-start.5 = (bf16[256,1024]{1,0:T(8,128)(2,1)S(1)}, bf16[256,1024]{1,0:T(8,128)(2,1)}, u32[]{:S(2)}) copy-start(bf16[256,1024]{1,0:T(8,128)(2,1)} %param.26) | copy-start | bytes 1572868
  7.2 161.0 %all-gather.11.cloned.1.call-start = ((), (), s32[]{:S(2)}) async-start(), calls=%async_computation.1 | async-start | bytes 8519680 | tf_op jit(solution)/shard_map/all_gather | solution.py:17
  12.7 310.8 %all-gather.13.cloned.1.call-start = ((), (), s32[]{:S(2)}) async-start(), calls=%async_computation.2 | async-start | bytes 8519680 | tf_op jit(solution)/shard_map/all_gather | solution.py:17
  17.8 651.2 %all-reduce.8.cloned.1.call-start = ((), (), s32[]{:S(2)}) async-start(), calls=%async_computation | async-start | bytes 2097152 | tf_op jit(solution)/shard_map/psum | solution.py:130
  390.7 28.8 %copy-start.2 = (bf16[256,128]{1,0:T(8,128)(2,1)S(1)}, bf16[256,128]{1,0:T(8,128)(2,1)}, u32[]{:S(2)}) copy-start(bf16[256,128]{1,0:T(8,128)(2,1)} %param.20) | copy-start | bytes 196612
  413.0 413.9 %all-gather.15.cloned.1.call-start = ((), (), s32[]{:S(2)}) async-start(), calls=%async_computation.3 | async-start | bytes 8519680 | tf_op jit(solution)/shard_map/all_gather | solution.py:17
  414.2 568.6 %all-gather.17.cloned.1.call-start = ((), (), s32[]{:S(2)}) async-start(), calls=%async_computation.4 | async-start | bytes 8519680 | tf_op jit(solution)/shard_map/all_gather | solution.py:17
  419.4 709.2 %all-reduce.10.cloned.1.call-start = ((), (), s32[]{:S(2)}) async-start(), calls=%async_computation.5 | async-start | bytes 524288 | tf_op jit(solution)/shard_map/psum | solution.py:129
Sparse Core Ops, SparseCore 0:
  12.8 155.3 all-gather.10
  171.7 151.7 all-gather.12
  413.1 255.8 all-reduce.7
  672.8 154.0 all-gather.14
  830.7 152.0 all-gather.16
  1051.9 76.6 all-reduce.9
where the time goes:
time: 1140 us
  waiting for transfers between devices  679 us (60%)
  other arithmetic  261 us (23%)
  blocking collectives  144 us (13%)
  matrix products  17 us (1%)
  between operations  15.1 us (1%)
  local copies, waits for them, and re-layouts  13.4 us (1%)
    all_gather x4, waiting for transfers between devices, prefix(): everything = jax.tree.map(lambda part: lax.all_gather(part, axis), shard)  355 us
    select_n x256, other arithmetic, step(): return jax.tree.map(lambda a, b: jnp.where(reached, a, b), new, before)  255 us
    psum x1, waiting for transfers between devices, body(): grad_w = lax.psum(local_w, 'seq') * weight_scale  249 us
    unnamed x1, blocking collectives  123 us
    psum x1, waiting for transfers between devices, body(): lax.psum((grad_b_near + grad_b_far, grad_c_near + grad_c_far), 'head')  75.8 us
  transfers between devices with their start and end apart: 6, of which 6 were waited for; matrix products, arithmetic and copies ran while one was open for 13% of the time, Pallas kernels for 0%

commit v1 on v0

v1 whole, which is shorter than its diff:
```python
import jax
import jax.numpy as jnp
from jax import lax
from jax.experimental import pallas as pl
from jax.experimental.pallas import tpu as pltpu
from jax.sharding import Mesh, PartitionSpec as P

HEADS = 4
HEAD_DIM = 64
STATE = 128
FRAMES = 256
WIDTH = HEADS * HEAD_DIM
LANES = 128
EPS_NORM = 1e-05
WEIGHT_SCALE = 0.0078125
F32, BF16 = jnp.float32, jnp.bfloat16


def dot(a, b, ca, cb):
    return lax.dot_general(a, b, (((ca,), (cb,)), ((), ())), preferred_element_type=F32)


def halves(a):
    high = a.astype(BF16)
    return high, (a - high.astype(F32)).astype(BF16)


def dot_left(a, b, ca, cb):
    ah, al = halves(a)
    return dot(ah, b, ca, cb) + dot(al, b, ca, cb)


def dot_right(a, b, ca, cb):
    bh, bl = halves(b)
    return dot(a, bh, ca, cb) + dot(a, bl, ca, cb)


def dot_both(a, b, ca, cb):
    ah, al = halves(a)
    bh, bl = halves(b)
    return dot(ah, bh, ca, cb) + (dot(ah, bl, ca, cb) + dot(al, bh, ca, cb))


def dot_exact(a, b, ca, cb):
    return lax.dot_general(
        a, b, (((ca,), (cb,)), ((), ())), precision=lax.Precision.HIGHEST, preferred_element_type=F32
    )


def places():
    row = lax.broadcasted_iota(jnp.int32, (FRAMES, FRAMES), 0)
    col = lax.broadcasted_iota(jnp.int32, (FRAMES, FRAMES), 1)
    return row, col


def columns(df, db):
    row, col = places()
    upto = (col <= row).astype(F32)
    before = (col < row).astype(F32)
    cf = dot_exact(upto, df, 1, 1)
    be = dot_exact(before, db, 1, 1)
    end_f = cf[FRAMES - 1 :, :]
    end_b = dot_exact(jnp.ones((8, FRAMES), F32), db, 1, 1)[:1, :]
    return cf, be, end_f, end_b


def rows(df, db):
    row, col = places()
    upto = (row <= col).astype(F32)
    before = (row < col).astype(F32)
    return dot_exact(df, upto, 1, 0), dot_exact(db, before, 1, 0)


def spread(cols):
    lane = lax.broadcasted_iota(jnp.int32, (cols.shape[0], LANES), 1)
    pairs = [
        jnp.where(lane < HEAD_DIM, cols[:, 2 * g : 2 * g + 1], cols[:, 2 * g + 1 : 2 * g + 2])
        for g in range(HEADS // 2)
    ]
    return jnp.concatenate(pairs, axis=1)


def pair_decay(h, cf, be, cf_row, be_row, row, col):
    gap = jnp.where(
        row > col,
        cf[:, h : h + 1] - cf_row[h : h + 1, :],
        be_row[h : h + 1, :] - be[:, h : h + 1],
    )
    return jnp.where(row == col, 2.0, jnp.exp(jnp.minimum(gap, 0.0)))


def own_lanes(pair, hh):
    lane = lax.broadcasted_iota(jnp.int32, pair.shape, 1)
    mine = lane < HEAD_DIM if hh == 0 else lane >= HEAD_DIM
    return jnp.where(mine, pair, jnp.zeros_like(pair))


def stack(ref, start):
    return jnp.concatenate([ref[j, start : start + HEAD_DIM, :] for j in range(HEADS)], axis=0)


def local_states(x_ref, b_ref, df_ref, db_ref, out_ref):
    cf, be, end_f, end_b = columns(df_ref[...], db_ref[...])
    x = x_ref[...].astype(F32)
    b = b_ref[...]
    state_f = dot_left(x * spread(jnp.exp(end_f - cf)), b, 0, 0)
    state_b = dot_left(x * spread(jnp.exp(be)), b, 0, 0)
    total_f = jnp.exp(end_f)
    total_b = jnp.exp(end_b)
    for j in range(HEADS):
        at = slice(j * HEAD_DIM, (j + 1) * HEAD_DIM)
        out_ref[j, 0:64, :] = state_f[at, :]
        out_ref[j, 64:128, :] = state_b[at, :]
        out_ref[j, 128:136, :] = jnp.broadcast_to(total_f[:, j : j + 1], (8, LANES))
        out_ref[j, 136:144, :] = jnp.broadcast_to(total_b[:, j : j + 1], (8, LANES))


def tiles(a):
    return a.reshape(a.shape[0] // 8, 8, LANES)


def chain(order, states, totals):
    acc = states[order[0]]
    for i in order[1:]:
        acc = totals[i][None] * acc + states[i]
    return acc


def row_parts(dec_ref, rec_ref, n_x):
    state_f = [tiles(rec_ref[i, 0:64, :]) for i in range(n_x)]
    state_b = [tiles(rec_ref[i, 64:128, :]) for i in range(n_x)]
    total_f = [dec_ref[i, 128:136, :] for i in range(n_x)]
    total_b = [dec_ref[i, 136:144, :] for i in range(n_x)]
    return state_f, state_b, total_f, total_b


def product(parts):
    out = parts[0]
    for part in parts[1:]:
        out = out * part
    return out


def row_totals_first(rec_ref, out_ref):
    n_x, n_z = rec_ref.shape[0], out_ref.shape[0]
    state_f, state_b, total_f, total_b = row_parts(rec_ref, rec_ref, n_x)
    up = list(range(n_x))
    sum_f = chain(up, state_f, total_f)
    sum_b = chain(up[::-1], state_b, total_b)
    both = jnp.concatenate([sum_f, sum_b], axis=0).reshape(2 * HEAD_DIM, LANES)
    span = 2 * HEAD_DIM // n_z
    for k in range(n_z):
        out_ref[k, 0:span, :] = both[k * span : (k + 1) * span, :]
        out_ref[k, span : span + 8, :] = product(total_f if 2 * k < n_z else total_b)


def row_totals_second(rec1_ref, rec_ref, out_ref):
    n_x, n_z = rec_ref.shape[0], out_ref.shape[0]
    state_f, state_b, total_f, total_b = row_parts(rec1_ref, rec_ref, n_x)
    up = list(range(n_x))
    sum_f = chain(up[::-1], state_f, total_f)
    sum_b = chain(up, state_b, total_b)
    both = jnp.concatenate([sum_f, sum_b], axis=0).reshape(2 * HEAD_DIM, LANES)
    span = 2 * HEAD_DIM // n_z
    size = 512 // n_z
    for k in range(n_z):
        out_ref[k, 0:span, :] = both[k * span : (k + 1) * span, :]
        at = slice(128 + k * size, 128 + (k + 1) * size)
        out_ref[k, span:, :] = sum(rec_ref[i, at, :] for i in range(1, n_x)) + rec_ref[0, at, :]


def scan_up(states, totals, n):
    out, acc = [], jnp.zeros_like(states[0])
    for i in range(n):
        out.append(acc)
        acc = totals[i][None] * acc + states[i]
    return out


def scan_both(up_ref, data_ref, dec_ref, span, n_z):
    states = [tiles(data_ref[i, 0:span, :]) for i in range(n_z)]
    totals = [dec_ref[i, span : span + 8, :] for i in range(n_z)]
    up = scan_up(states, totals, n_z)
    down = scan_up(states[::-1], totals[::-1], n_z)[::-1]
    upward = up_ref[0] == 1
    return [jnp.where(upward, u, d).reshape(span, LANES) for u, d in zip(up, down)]


def scan_first(up_ref, rec_ref, out_ref):
    n_z, span = out_ref.shape[0], out_ref.shape[1]
    for i, entry in enumerate(scan_both(up_ref, rec_ref, rec_ref, span, n_z)):
        out_ref[i, :, :] = entry


def scan_second(up_ref, dec_ref, rec_ref, out_ref):
    n_z = out_ref.shape[0]
    span = 2 * HEAD_DIM // n_z
    entries = scan_both(up_ref, rec_ref, dec_ref, span, n_z)
    weight = rec_ref[0, span:, :]
    for i in range(1, n_z):
        weight = weight + rec_ref[i, span:, :]
    for i in range(n_z):
        out_ref[i, 0:span, :] = entries[i]
        out_ref[i, span:, :] = weight


def entries_of(back_ref, span, n_z):
    half = n_z // 2
    entry_f = jnp.concatenate([tiles(back_ref[k, 0:span, :]) for k in range(half)], axis=0)
    entry_b = jnp.concatenate([tiles(back_ref[k, 0:span, :]) for k in range(half, n_z)], axis=0)
    return entry_f, entry_b


def put_entries(out_ref, order, entry, states, totals, at):
    for i in order:
        out_ref[i, at : at + HEAD_DIM, :] = entry.reshape(HEAD_DIM, LANES)
        entry = totals[i][None] * entry + states[i]


def row_entries_first(back_ref, rec_ref, out_ref):
    n_z, span = back_ref.shape[0], back_ref.shape[1]
    n_x = rec_ref.shape[0]
    state_f, state_b, total_f, total_b = row_parts(rec_ref, rec_ref, n_x)
    entry_f, entry_b = entries_of(back_ref, span, n_z)
    up = list(range(n_x))
    put_entries(out_ref, up, entry_f, state_f, total_f, 0)
    put_entries(out_ref, up[::-1], entry_b, state_b, total_b, HEAD_DIM)


def row_entries_second(back_ref, rec1_ref, rec_ref, out_ref):
    n_z = back_ref.shape[0]
    n_x = rec_ref.shape[0]
    span, size = 2 * HEAD_DIM // n_z, 512 // n_z
    state_f, state_b, total_f, total_b = row_parts(rec1_ref, rec_ref, n_x)
    entry_f, entry_b = entries_of(back_ref, span, n_z)
    up = list(range(n_x))
    put_entries(out_ref, up[::-1], entry_f, state_f, total_f, 0)
    put_entries(out_ref, up, entry_b, state_b, total_b, HEAD_DIM)
    for k in range(n_z):
        weight = back_ref[k, span:, :]
        for i in range(n_x):
            out_ref[i, 128 + k * size : 128 + (k + 1) * size, :] = weight


def across_rows(cols):
    lane = lax.broadcasted_iota(jnp.int32, (LANES, LANES), 1)
    grid = jnp.zeros((LANES, LANES), F32)
    for i, col in enumerate(cols):
        for part in range(FRAMES // LANES):
            at = i * (FRAMES // LANES) + part
            grid = jnp.where(lane == at, col[part * LANES : (part + 1) * LANES, :], grid)
    return jnp.transpose(grid)[0:8, :]


def outputs(
    skip_ref, x_ref, z_ref, b_ref, c_ref, df_ref, db_ref, gain_ref, w_ref, do_ref, ent_ref,
    y_ref, m_ref, sums_ref,
):
    df, db = df_ref[...], db_ref[...]
    cf, be, end_f, end_b = columns(df, db)
    cf_row, be_row = rows(df, db)
    row, col = places()
    c = c_ref[...]
    scores = dot(c, b_ref[...], 1, 1)
    far = spread(jnp.exp(cf)) * dot_right(c, stack(ent_ref, 0), 1, 1)
    far = far + spread(jnp.exp(end_b - be)) * dot_right(c, stack(ent_ref, HEAD_DIM), 1, 1)
    near = []
    lane = lax.broadcasted_iota(jnp.int32, (1, LANES), 1)
    for g in range(HEADS // 2):
        pair = x_ref[:, g * LANES : (g + 1) * LANES]
        acc = jnp.where(lane < HEAD_DIM, skip_ref[2 * g], skip_ref[2 * g + 1]) * pair.astype(F32)
        for hh in range(2):
            weights = scores * pair_decay(2 * g + hh, cf, be, cf_row, be_row, row, col)
            acc = acc + dot_left(weights, own_lanes(pair, hh), 1, 0)
        near.append(acc)
    y = far + jnp.concatenate(near, axis=1)
    z = z_ref[...].astype(F32)
    u = y * z * jax.nn.sigmoid(z)
    m = dot(do_ref[...], w_ref[...], 1, 1) * gain_ref[...]
    y_ref[...] = y
    m_ref[...] = m
    sums = across_rows([jnp.sum(u * u, axis=1, keepdims=True), jnp.sum(u * m, axis=1, keepdims=True)])
    for i in range(sums_ref.shape[0]):
        sums_ref[i, :, :] = sums


def gradients(
    sums_ref, y_ref, m_ref, z_ref, c_ref, df_ref, db_ref, gain_ref, do_ref,
    dy_ref, gz_ref, out_ref, *, inner,
):
    total = sums_ref[0, :, :]
    for i in range(1, sums_ref.shape[0]):
        total = total + sums_ref[i, :, :]
    grid = jnp.transpose(jnp.concatenate([total, jnp.zeros((LANES - 8, LANES), F32)], axis=0))
    square = jnp.concatenate([grid[:, 0:1], grid[:, 1:2]], axis=0) / inner
    cross = jnp.concatenate([grid[:, 2:3], grid[:, 3:4]], axis=0) / inner
    q = lax.rsqrt(square + EPS_NORM)
    y, m, z = y_ref[...], m_ref[...], z_ref[...].astype(F32)
    sig = jax.nn.sigmoid(z)
    silu = z * sig
    u = y * z * sig
    normed = (u * q * gain_ref[...]).astype(BF16)
    du = q * m - u * (q * q * q * cross)
    dy = du * silu
    gz_ref[...] = (du * y * sig * (1.0 + z * (1.0 - sig))).astype(BF16)
    dy_ref[...] = dy
    cf, be, end_f, end_b = columns(df_ref[...], db_ref[...])
    c = c_ref[...]
    back_f = dot_left(dy * spread(jnp.exp(cf)), c, 0, 0)
    back_b = dot_left(dy * spread(jnp.exp(end_b - be)), c, 0, 0)
    weight = dot(normed, do_ref[...], 0, 0)
    for j in range(HEADS):
        at = slice(j * HEAD_DIM, (j + 1) * HEAD_DIM)
        out_ref[j, 0:64, :] = back_f[at, :]
        out_ref[j, 64:128, :] = back_b[at, :]
        for block in range(weight.shape[1] // LANES):
            out_ref[j, 128 + block * 64 : 192 + block * 64, :] = weight[
                at, block * LANES : (block + 1) * LANES
            ]


def finish(
    skip_ref, x_ref, b_ref, c_ref, df_ref, db_ref, dy_ref, ent_ref, exit_ref,
    gx_ref, gw_ref, out_ref,
):
    df, db = df_ref[...], db_ref[...]
    cf, be, end_f, end_b = columns(df, db)
    cf_row, be_row = rows(df, db)
    row, col = places()
    b, c, dy = b_ref[...], c_ref[...], dy_ref[...]
    x = x_ref[...].astype(F32)
    scores = dot(c, b, 1, 1)
    pair_sum = jnp.zeros((FRAMES, FRAMES), F32)
    near = []
    lane = lax.broadcasted_iota(jnp.int32, (1, LANES), 1)
    for g in range(HEADS // 2):
        at = slice(g * LANES, (g + 1) * LANES)
        acc = jnp.where(lane < HEAD_DIM, skip_ref[2 * g], skip_ref[2 * g + 1]) * dy[:, at]
        for hh in range(2):
            decay = pair_decay(2 * g + hh, cf, be, cf_row, be_row, row, col)
            dy_own = own_lanes(dy[:, at], hh)
            pair_sum = pair_sum + decay * dot_left(dy_own, x_ref[:, at], 1, 1)
            acc = acc + dot_both(scores * decay, dy_own, 0, 0)
        near.append(acc)
    rise_f, rise_b = spread(jnp.exp(cf)), spread(jnp.exp(end_b - be))
    tail_f, lead_b = spread(jnp.exp(end_f - cf)), spread(jnp.exp(be))
    entry_f, entry_b = stack(ent_ref, 0), stack(ent_ref, HEAD_DIM)
    exit_f, exit_b = stack(exit_ref, 0), stack(exit_ref, HEAD_DIM)
    gx = jnp.concatenate(near, axis=1)
    gx = gx + tail_f * dot_right(b, exit_f, 1, 1) + lead_b * dot_right(b, exit_b, 1, 1)
    gx_ref[...] = gx.astype(BF16)
    grad_c = dot_left(pair_sum, b, 1, 0)
    grad_c = grad_c + dot_both(dy * rise_f, entry_f, 1, 0) + dot_both(dy * rise_b, entry_b, 1, 0)
    grad_b = dot_left(pair_sum, c, 0, 0)
    grad_b = grad_b + dot_both(x * tail_f, exit_f, 1, 0) + dot_both(x * lead_b, exit_b, 1, 0)
    n = out_ref.shape[0]
    size = FRAMES // n
    for i in range(n):
        out_ref[i, 0:size, :] = grad_b[i * size : (i + 1) * size, :]
        out_ref[i, size : 2 * size, :] = grad_c[i * size : (i + 1) * size, :]
    for j in range(HEADS):
        for block in range(gw_ref.shape[1] // LANES):
            gw_ref[j * 64 : (j + 1) * 64, block * LANES : (block + 1) * LANES] = (
                exit_ref[j, 128 + block * 64 : 192 + block * 64, :] * WEIGHT_SCALE
            )


def add_up(rec_ref, out_ref):
    n = rec_ref.shape[0]
    total = rec_ref[0, :, :]
    for i in range(1, n):
        total = total + rec_ref[i, :, :]
    for i in range(n):
        out_ref[i, :, :] = total


def deal_out(rec_ref, gb_ref, gc_ref):
    n = rec_ref.shape[0]
    size = FRAMES // n
    for i in range(n):
        gb_ref[i * size : (i + 1) * size, :] = rec_ref[i, 0:size, :]
        gc_ref[i * size : (i + 1) * size, :] = rec_ref[i, size : 2 * size, :]


VMEM = pl.BlockSpec(memory_space=pltpu.VMEM)
SMEM = pl.BlockSpec(memory_space=pltpu.SMEM)


def call(kernel, name, out, *args, scalars=0):
    shapes = [jax.ShapeDtypeStruct(shape, dtype) for shape, dtype in out]
    single = len(shapes) == 1
    return pl.pallas_call(
        kernel,
        name=name,
        out_shape=shapes[0] if single else tuple(shapes),
        in_specs=[SMEM] * scalars + [VMEM] * (len(args) - scalars),
        out_specs=VMEM if single else tuple(VMEM for _ in shapes),
        compiler_params=pltpu.CompilerParams(vmem_limit_bytes=48 * 1024 * 1024),
    )(*args)


def exchange(a, axis):
    return lax.all_to_all(a, axis, 0, 0, tiled=True)


def body(x_in, gate_in, b_in, c_in, decay_fwd, decay_bwd, skip_gain, norm_gain, w_out, d_out):
    n_z, n_x, n_h = lax.axis_size("z"), lax.axis_size("x"), lax.axis_size("head")
    gain = norm_gain.reshape(1, WIDTH)
    span = 2 * HEAD_DIM // n_z
    size = 512 // n_z
    first_half = (2 * lax.axis_index("z") < n_z).astype(jnp.int32).reshape(1)

    sent = call(local_states, "local_states", [((n_x, 144, LANES), F32)], x_in, b_in, decay_fwd, decay_bwd)
    rec1 = exchange(sent, "x")
    sent = call(row_totals_first, "row_totals_first", [((n_z, span + 8, LANES), F32)], rec1)
    recz1 = exchange(sent, "z")
    sent = call(scan_first, "scan_first", [((n_z, span, LANES), F32)], first_half, recz1, scalars=1)
    back = exchange(sent, "z")
    sent = call(row_entries_first, "row_entries_first", [((n_x, 128, LANES), F32)], back, rec1)
    entries = exchange(sent, "x")

    y, m, sums = call(
        outputs, "outputs",
        [((FRAMES, WIDTH), F32), ((FRAMES, WIDTH), F32), ((n_h, 8, LANES), F32)],
        skip_gain, x_in, gate_in, b_in, c_in, decay_fwd, decay_bwd, gain, w_out, d_out, entries,
        scalars=1,
    )
    sums = exchange(sums, "head")

    def gradients_here(*refs):
        gradients(*refs, inner=WIDTH * n_h)

    dy, grad_z, sent = call(
        gradients_here, "gradients",
        [((FRAMES, WIDTH), F32), ((FRAMES, WIDTH), BF16), ((n_x, 640, LANES), F32)],
        sums, y, m, gate_in, c_in, decay_fwd, decay_bwd, gain, d_out,
    )
    rec2 = exchange(sent, "x")
    sent = call(row_totals_second, "row_totals_second", [((n_z, span + size, LANES), F32)], rec1, rec2)
    recz2 = exchange(sent, "z")
    sent = call(
        scan_second, "scan_second", [((n_z, span + size, LANES), F32)],
        1 - first_half, recz1, recz2, scalars=1,
    )
    back = exchange(sent, "z")
    sent = call(row_entries_second, "row_entries_second", [((n_x, 640, LANES), F32)], back, rec1, rec2)
    exits = exchange(sent, "x")

    chunk = 2 * FRAMES // n_h
    grad_x, grad_w, sent = call(
        finish, "finish",
        [((FRAMES, WIDTH), BF16), ((WIDTH, d_out.shape[1]), F32), ((n_h, chunk, LANES), F32)],
        skip_gain, x_in, b_in, c_in, decay_fwd, decay_bwd, dy, entries, exits,
        scalars=1,
    )
    rec = exchange(sent, "head")
    sent = call(add_up, "add_up", [((n_h, chunk, LANES), F32)], rec)
    rec = exchange(sent, "head")
    grad_b, grad_c = call(deal_out, "deal_out", [((FRAMES, STATE), F32)] * 2, rec)
    return grad_x, grad_z, grad_b, grad_c, grad_w


def solution(mesh):
    n_seq, n_head = mesh.devices.shape
    split = Mesh(mesh.devices.reshape(n_seq // HEADS, HEADS, n_head), ("z", "x", "head"))
    seq = ("z", "x")
    in_specs = (
        P(seq, "head"),
        P(seq, "head"),
        P(seq, None),
        P(seq, None),
        P("head", seq),
        P("head", seq),
        P("head"),
        P("head"),
        P("head", None),
        P(seq, None),
    )
    out_specs = (
        P(seq, "head"),
        P(seq, "head"),
        P(seq, None),
        P(seq, None),
        P("head", None),
    )
    return jax.shard_map(body, mesh=split, in_specs=in_specs, out_specs=out_specs, check_vma=False)
```

time: 1140 us -> 200 us (0.18)
  waiting for transfers between devices: 679 us -> 26 us
  other arithmetic: 261 us -> 0 us
  starting transfers between devices: 0.25 us -> 18.6 us
  matrix products: 17 us -> 0 us
  between operations: 15.1 us -> 0.84 us
  Pallas kernels: 0 us -> 11.8 us
    all_gather x4 -> x0, waiting for transfers between devices: 355 us -> none  [prefix(): everything = jax.tree.map(lambda part: lax.all_gather(part, axis), shard)]
    psum x2 -> x0, waiting for transfers between devices: 324 us -> none  [the longest x1 249 us: body(): grad_w = lax.psum(local_w, 'seq') * weight_scale]
    select_n x256 -> x0, other arithmetic: 255 us -> none  [step(): return jax.tree.map(lambda a, b: jnp.where(reached, a, b), new, before)]
    all_to_all x0 -> x9, blocking collectives: none -> 136 us  [exchange(): return lax.all_to_all(a, axis, 0, 0, tiled=True)]
    unnamed x1 -> x0, blocking collectives: 123 us -> none
    all_to_all x0 -> x2, waiting for transfers between devices: none -> 26 us  [exchange(): return lax.all_to_all(a, axis, 0, 0, tiled=True)]
    psum x1 -> x0, blocking collectives: 20.3 us -> none  [body(): lax.psum((jnp.sum(gated_y * gated_y, axis=1), jnp.sum(gated_y * scaled, a...]
    all_to_all x0 -> x2, starting transfers between devices: none -> 18.6 us  [exchange(): return lax.all_to_all(a, axis, 0, 0, tiled=True)]
  transfers between devices with their start and end apart: 6 -> 2, of which waited for: 6 -> 2; matrix products, arithmetic and copies ran while one was open for 13% -> 0% of each run, Pallas kernels for 0% -> 0%
where the time goes in v1:
time: 200 us; the launch traced here: 196 us
  blocking collectives  136 us (68%)
  waiting for transfers between devices  26 us (13%)
  starting transfers between devices  18.6 us (9%)
  Pallas kernels  11.8 us (6%)
  local copies, waits for them, and re-layouts  3.17 us (2%)
    all_to_all x9, blocking collectives, exchange(): return lax.all_to_all(a, axis, 0, 0, tiled=True)  136 us
    all_to_all x2, waiting for transfers between devices, exchange(): return lax.all_to_all(a, axis, 0, 0, tiled=True)  26 us
    all_to_all x2, starting transfers between devices, exchange(): return lax.all_to_all(a, axis, 0, 0, tiled=True)  18.6 us
    pallas_call x12, Pallas kernels, call(): pl.pallas_call(kernel, name=name, out_shape=shapes[0] if single else tupl...  11.8 us
  transfers between devices with their start and end apart: 2, of which 2 were waited for; matrix products, arithmetic and copies ran while one was open for 0% of the time, Pallas kernels for 0%

profile of v1, /device:TPU:1, one launch (start us, length us, event | category | flops | bytes accessed | tf_op | source)
XLA Modules:
  0.0 196.0 jit_solution(17625576607024614590)
XLA Ops:
  0.6 0.0 copy-start.1
  0.6 0.9 copy-done.1
  1.5 0.8 copy-done.3
  2.4 0.7 copy-done.8
  3.1 0.7 copy-done.10
  3.8 1.2 local_states.1
  5.0 0.0 copy-start.2
  5.0 0.0 copy-start.4
  5.1 0.0 copy-start.7
  5.1 0.0 copy-start.9
  5.1 0.0 copy-start.12
  5.1 0.0 copy-start.13
  5.1 10.5 %all_to_all.55.rec_ref.rec1_ref = f32[4,144,128]{2,1,0:T(8,128)S(1)} all-to-all(f32[4,144,128]{2,1,0:T(8,128)S(1)} %local_states.1), channel_id=1, replica_groups=mesh['z'=16,'x'=4,'head'=8] {'x'}, dimensions={0} | all-to-all | bytes 589824 | tf_op jit(solution)/shard_map/all_to_all | solution.py:403
  15.6 0.7 row_totals_first.1
  16.3 15.0 %all-to-all-start.1 = ((f32[16,16,128]{2,1,0:T(8,128)}), f32[16,16,128]{2,1,0:T(8,128)S(1)}, u32[]{:S(2)}, u32[]{:S(2)}) async-start(f32[16,16,128]{2,1,0:T(8,128)} %row_totals_first.1), calls=%async_computation.1 | async-start | bytes 262144 | tf_op jit(solution)/shard_map/all_to_all | solution.py:403
  31.3 12.0 %all-to-all-done.1.rec_ref.dec_ref = f32[16,16,128]{2,1,0:T(8,128)S(1)} async-done(((f32[16,16,128]{2,1,0:T(8,128)}), f32[16,16,128]{2,1,0:T(8,128)S(1)}, u32[]{:S(2)}, u32[]{:S(2)}) %all-to-all-start.1) | async-done | bytes 131104 | tf_op jit(solution)/shard_map/all_to_all | solution.py:403
  43.3 15.4 %all_to_all.56.back_ref = f32[16,8,128]{2,1,0:T(8,128)S(1)} all-to-all(f32[16,8,128]{2,1,0:T(8,128)S(1)} %scan_first.1), channel_id=1, replica_groups=mesh['z'=16,'x'=4,'head'=8] {'z'}, dimensions={0} | all-to-all | bytes 131072 | tf_op jit(solution)/shard_map/all_to_all | solution.py:403
  58.7 8.0 %all_to_all.57.ent_ref = f32[4,128,128]{2,1,0:T(8,128)S(1)} all-to-all(f32[4,128,128]{2,1,0:T(8,128)S(1)} %row_entries_first.1), channel_id=1, replica_groups=mesh['z'=16,'x'=4,'head'=8] {'x'}, dimensions={0} | all-to-all | bytes 524288 | tf_op jit(solution)/shard_map/all_to_all | solution.py:403
  66.8 2.4 %outputs.1 = (f32[256,256]{1,0:T(8,128)S(1)}, f32[256,256]{1,0:T(8,128)S(1)}, f32[8,8,128]{2,1,0:T(8,128)S(1)}) custom-call(f32[4]{0:T(128)S(1)} %copy-done.13, bf16[256,256]{1,0:T(8,128)(2,1)S(1)} %copy-done.2, bf16[256,256]{1,0:T(8,128)(2,1)S(1)} %copy-done.7, bf16[256,128]{1,0:T(8,128)(2,1)S(1)} %copy-done.4, bf16[256,128]{1,0:T(8,128)(2,1)S(1)} %copy-done.5, ...), custom_call_target="tpu_custom_call" | custom-call | tf_op jit(solution)/shard_map/outputs/pallas_call | solution.py:392
  69.2 14.9 %all_to_all.58.refs_0_ = f32[8,8,128]{2,1,0:T(8,128)S(1)} all-to-all(f32[8,8,128]{2,1,0:T(8,128)S(1)} %get-tuple-element.16), channel_id=1, replica_groups=mesh['z'=16,'x'=4,'head'=8] {'head'}, dimensions={0} | all-to-all | bytes 65536 | tf_op jit(solution)/shard_map/all_to_all | solution.py:403
  84.2 1.4 gradients.1
  85.6 19.4 %all_to_all.59.rec_ref = f32[4,640,128]{2,1,0:T(8,128)S(1)} all-to-all(f32[4,640,128]{2,1,0:T(8,128)S(1)} %get-tuple-element.20), channel_id=1, replica_groups=mesh['z'=16,'x'=4,'head'=8] {'x'}, dimensions={0} | all-to-all | bytes 2621440 | tf_op jit(solution)/shard_map/all_to_all | solution.py:403
  105.0 0.8 row_totals_second.1
  105.8 3.5 %all-to-all-start.6 = ((f32[16,40,128]{2,1,0:T(8,128)}), f32[16,40,128]{2,1,0:T(8,128)S(1)}, u32[]{:S(2)}, u32[]{:S(2)}) async-start(f32[16,40,128]{2,1,0:T(8,128)} %row_totals_second.1), calls=%async_computation.6 | async-start | bytes 655360 | tf_op jit(solution)/shard_map/all_to_all | solution.py:403
  109.3 14.0 %all-to-all-done.6.rec_ref = f32[16,40,128]{2,1,0:T(8,128)S(1)} async-done(((f32[16,40,128]{2,1,0:T(8,128)}), f32[16,40,128]{2,1,0:T(8,128)S(1)}, u32[]{:S(2)}, u32[]{:S(2)}) %all-to-all-start.6) | async-done | bytes 327712 | tf_op jit(solution)/shard_map/all_to_all | solution.py:403
  123.4 26.1 %all_to_all.60.back_ref = f32[16,40,128]{2,1,0:T(8,128)S(1)} all-to-all(f32[16,40,128]{2,1,0:T(8,128)S(1)} %scan_second.1), channel_id=1, replica_groups=mesh['z'=16,'x'=4,'head'=8] {'z'}, dimensions={0} | all-to-all | bytes 655360 | tf_op jit(solution)/shard_map/all_to_all | solution.py:403
  149.4 0.1 row_entries_second.1
  149.5 13.6 %all_to_all.61.exit_ref = f32[4,640,128]{2,1,0:T(8,128)S(1)} all-to-all(f32[4,640,128]{2,1,0:T(8,128)S(1)} %row_entries_second.1), channel_id=1, replica_groups=mesh['z'=16,'x'=4,'head'=8] {'x'}, dimensions={0} | all-to-all | bytes 2621440 | tf_op jit(solution)/shard_map/all_to_all | solution.py:403
  163.1 4.3 %finish.1 = (bf16[256,256]{1,0:T(8,128)(2,1)}, f32[256,1024]{1,0:T(8,128)}, f32[8,64,128]{2,1,0:T(8,128)S(1)}) custom-call(f32[4]{0:T(128)S(1)} %copy-done.13, bf16[256,256]{1,0:T(8,128)(2,1)S(1)} %copy-done.2, bf16[256,128]{1,0:T(8,128)(2,1)S(1)} %copy-done.4, bf16[256,128]{1,0:T(8,128)(2,1)S(1)} %copy-done.5, f32[4,256]{1,0:T(4,128)S(1)} %copy-done.9, ...), custom_call_target="tpu_custom_call" | custom-call | tf_op jit(solution)/shard_map/finish/pallas_call | solution.py:392
  167.4 18.0 %all_to_all.62.rec_ref = f32[8,64,128]{2,1,0:T(8,128)S(1)} all-to-all(f32[8,64,128]{2,1,0:T(8,128)S(1)} %get-tuple-element.23), channel_id=1, replica_groups=mesh['z'=16,'x'=4,'head'=8] {'head'}, dimensions={0} | all-to-all | bytes 524288 | tf_op jit(solution)/shard_map/all_to_all | solution.py:403
  185.4 9.9 %all_to_all.63.rec_ref = f32[8,64,128]{2,1,0:T(8,128)S(1)} all-to-all(f32[8,64,128]{2,1,0:T(8,128)S(1)} %add_up.1), channel_id=1, replica_groups=mesh['z'=16,'x'=4,'head'=8] {'head'}, dimensions={0} | all-to-all | bytes 524288 | tf_op jit(solution)/shard_map/all_to_all | solution.py:403
  195.3 0.7 deal_out.1
  (21 shorter events, 0.2 us)
Async XLA Ops:
  0.6 0.9 copy-start.1
  1.5 0.8 copy-start.3
  2.4 0.7 copy-start.8
  3.1 0.7 copy-start.10
  5.0 61.7 %copy-start = (bf16[256,1024]{1,0:T(8,128)(2,1)S(1)}, bf16[256,1024]{1,0:T(8,128)(2,1)}, u32[]{:S(2)}) copy-start(bf16[256,1024]{1,0:T(8,128)(2,1)} %refs_8_.1) | copy-start | bytes 1572868
  5.0 61.7 %copy-start.2 = (bf16[256,256]{1,0:T(8,128)(2,1)S(1)}, bf16[256,256]{1,0:T(8,128)(2,1)}, u32[]{:S(2)}) copy-start(bf16[256,256]{1,0:T(8,128)(2,1)} %x_ref.5) | copy-start | bytes 393220
  5.0 61.7 %copy-start.4 = (bf16[256,128]{1,0:T(8,128)(2,1)S(1)}, bf16[256,128]{1,0:T(8,128)(2,1)}, u32[]{:S(2)}) copy-start(bf16[256,128]{1,0:T(8,128)(2,1)} %b_ref.5) | copy-start | bytes 196612
  5.0 61.7 %copy-start.5 = (bf16[256,128]{1,0:T(8,128)(2,1)S(1)}, bf16[256,128]{1,0:T(8,128)(2,1)}, u32[]{:S(2)}) copy-start(bf16[256,128]{1,0:T(8,128)(2,1)} %c_ref.3) | copy-start | bytes 196612
  5.0 61.7 %copy-start.6 = (bf16[256,1024]{1,0:T(8,128)(2,1)S(1)}, bf16[256,1024]{1,0:T(8,128)(2,1)}, u32[]{:S(2)}) copy-start(bf16[256,1024]{1,0:T(8,128)(2,1)} %w_ref.1) | copy-start | bytes 1572868
  5.1 61.7 %copy-start.7 = (bf16[256,256]{1,0:T(8,128)(2,1)S(1)}, bf16[256,256]{1,0:T(8,128)(2,1)}, u32[]{:S(2)}) copy-start(bf16[256,256]{1,0:T(8,128)(2,1)} %refs_3_.1) | copy-start | bytes 393220
  5.1 61.7 %copy-start.9 = (f32[4,256]{1,0:T(4,128)S(1)}, f32[4,256]{1,0:T(4,128)}, u32[]{:S(2)}) copy-start(f32[4,256]{1,0:T(4,128)} %df_ref.5) | copy-start | bytes 12292
  5.1 61.7 %copy-start.11 = (f32[4,256]{1,0:T(4,128)S(1)}, f32[4,256]{1,0:T(4,128)}, u32[]{:S(2)}) copy-start(f32[4,256]{1,0:T(4,128)} %db_ref.5) | copy-start | bytes 12292
  5.1 61.7 %copy-start.12 = (f32[256]{0:T(256)S(1)}, f32[256]{0:T(256)}, u32[]{:S(2)}) copy-start(f32[256]{0:T(256)} %param.17) | copy-start | bytes 3076
  5.1 61.7 %copy-start.13 = (f32[4]{0:T(128)S(1)}, f32[4]{0:T(128)}, u32[]{:S(2)}) copy-start(f32[4]{0:T(128)} %skip_ref.3) | copy-start | bytes 52
  16.3 27.0 %all-to-all-start.1 = ((f32[16,16,128]{2,1,0:T(8,128)}), f32[16,16,128]{2,1,0:T(8,128)S(1)}, u32[]{:S(2)}, u32[]{:S(2)}) async-start(f32[16,16,128]{2,1,0:T(8,128)} %row_totals_first.1), calls=%async_computation.1 | async-start | bytes 262144 | tf_op jit(solution)/shard_map/all_to_all | solution.py:403
  105.8 17.6 %all-to-all-start.6 = ((f32[16,40,128]{2,1,0:T(8,128)}), f32[16,40,128]{2,1,0:T(8,128)S(1)}, u32[]{:S(2)}, u32[]{:S(2)}) async-start(f32[16,40,128]{2,1,0:T(8,128)} %row_totals_second.1), calls=%async_computation.6 | async-start | bytes 655360 | tf_op jit(solution)/shard_map/all_to_all | solution.py:403

commit v2 on v1

v2 whole, which is shorter than its diff:
```python
import functools

import jax
import jax.numpy as jnp
from jax import lax
from jax.experimental import pallas as pl
from jax.experimental.pallas import tpu as pltpu
from jax.sharding import Mesh, PartitionSpec as P

HEADS = 4
HEAD_DIM = 64
STATE = 128
FRAMES = 256
WIDTH = HEADS * HEAD_DIM
LANES = 128
EPS_NORM = 1e-05
WEIGHT_SCALE = 0.0078125
F32, BF16 = jnp.float32, jnp.bfloat16


def dot(a, b, ca, cb):
    return lax.dot_general(a, b, (((ca,), (cb,)), ((), ())), preferred_element_type=F32)


def halves(a):
    high = a.astype(BF16)
    return high, (a - high.astype(F32)).astype(BF16)


def dot_left(a, b, ca, cb):
    ah, al = halves(a)
    return dot(ah, b, ca, cb) + dot(al, b, ca, cb)


def dot_right(a, b, ca, cb):
    bh, bl = halves(b)
    return dot(a, bh, ca, cb) + dot(a, bl, ca, cb)


def dot_both(a, b, ca, cb):
    ah, al = halves(a)
    bh, bl = halves(b)
    return dot(ah, bh, ca, cb) + (dot(ah, bl, ca, cb) + dot(al, bh, ca, cb))


def dot_exact(a, b, ca, cb):
    return lax.dot_general(
        a, b, (((ca,), (cb,)), ((), ())), precision=lax.Precision.HIGHEST, preferred_element_type=F32
    )


def places():
    row = lax.broadcasted_iota(jnp.int32, (FRAMES, FRAMES), 0)
    col = lax.broadcasted_iota(jnp.int32, (FRAMES, FRAMES), 1)
    return row, col


def columns(df, db):
    row, col = places()
    upto = (col <= row).astype(F32)
    before = (col < row).astype(F32)
    cf = dot_exact(upto, df, 1, 1)
    be = dot_exact(before, db, 1, 1)
    end_f = cf[FRAMES - 1 :, :]
    end_b = dot_exact(jnp.ones((8, FRAMES), F32), db, 1, 1)[:1, :]
    return cf, be, end_f, end_b


def rows(df, db):
    row, col = places()
    upto = (row <= col).astype(F32)
    before = (row < col).astype(F32)
    return dot_exact(df, upto, 1, 0), dot_exact(db, before, 1, 0)


def spread(cols):
    lane = lax.broadcasted_iota(jnp.int32, (cols.shape[0], LANES), 1)
    pairs = [
        jnp.where(lane < HEAD_DIM, cols[:, 2 * g : 2 * g + 1], cols[:, 2 * g + 1 : 2 * g + 2])
        for g in range(HEADS // 2)
    ]
    return jnp.concatenate(pairs, axis=1)


def pair_decay(h, cf, be, cf_row, be_row, row, col):
    gap = jnp.where(
        row > col,
        cf[:, h : h + 1] - cf_row[h : h + 1, :],
        be_row[h : h + 1, :] - be[:, h : h + 1],
    )
    return jnp.where(row == col, 2.0, jnp.exp(jnp.minimum(gap, 0.0)))


def own_lanes(pair, hh):
    lane = lax.broadcasted_iota(jnp.int32, pair.shape, 1)
    mine = lane < HEAD_DIM if hh == 0 else lane >= HEAD_DIM
    return jnp.where(mine, pair, jnp.zeros_like(pair))


def put_slices(out_ref, forward, backward):
    n = out_ref.shape[0]
    size = WIDTH // n
    for i in range(n):
        at = slice(i * size, (i + 1) * size)
        out_ref[i, 0:size, :] = forward[at, :]
        out_ref[i, size : 2 * size, :] = backward[at, :]


def take_slices(ref):
    n = ref.shape[0]
    size = WIDTH // n
    forward = jnp.concatenate([ref[i, 0:size, :] for i in range(n)], axis=0)
    backward = jnp.concatenate([ref[i, size : 2 * size, :] for i in range(n)], axis=0)
    return forward, backward


def local_states(x_ref, b_ref, df_ref, db_ref, out_ref):
    cf, be, end_f, end_b = columns(df_ref[...], db_ref[...])
    x = x_ref[...].astype(F32)
    b = b_ref[...]
    state_f = dot_left(x * spread(jnp.exp(end_f - cf)), b, 0, 0)
    state_b = dot_left(x * spread(jnp.exp(be)), b, 0, 0)
    put_slices(out_ref, state_f, state_b)
    n = out_ref.shape[0]
    size = WIDTH // n
    total_f, total_b = jnp.exp(end_f), jnp.exp(end_b)
    half = lax.broadcasted_iota(jnp.int32, (8, LANES), 0) < 4
    for j in range(HEADS):
        both = jnp.where(half, total_f[:, j : j + 1], total_b[:, j : j + 1])
        for i in range(j * n // HEADS, (j + 1) * n // HEADS):
            out_ref[i, 2 * size :, :] = both


def totals_at(ref, i, start):
    return ref[i, start : start + 1, :], ref[i, start + 4 : start + 5, :]


def sliced(ref, i, size):
    return ref[i, 0:size, :], ref[i, size : 2 * size, :]


def group_totals(dec_ref, rec_ref, out_ref, *, forward_up):
    n = rec_ref.shape[0]
    size = WIDTH // n
    decays = [totals_at(dec_ref, i, 2 * size) for i in range(n)]
    parts = [sliced(rec_ref, i, size) for i in range(n)]
    ups = list(range(n))
    for branch, up in enumerate((forward_up, not forward_up)):
        order = ups if up else ups[::-1]
        acc = parts[order[0]][branch]
        for i in order[1:]:
            acc = decays[i][branch] * acc + parts[i][branch]
        for k in range(out_ref.shape[0]):
            out_ref[k, branch * size : (branch + 1) * size, :] = acc
    if out_ref.shape[1] > 2 * size:
        all_f, all_b = decays[0]
        for i in range(1, n):
            all_f, all_b = all_f * decays[i][0], all_b * decays[i][1]
        half = lax.broadcasted_iota(jnp.int32, (8, LANES), 0) < 4
        for k in range(out_ref.shape[0]):
            out_ref[k, 2 * size :, :] = jnp.where(half, all_f, all_b)


def group_entries(place_ref, zdec_ref, zrec_ref, dec_ref, rec_ref, out_ref, *, forward_up):
    n_g, n = zrec_ref.shape[0], rec_ref.shape[0]
    size = WIDTH // n
    place = place_ref[0]
    for branch, up in enumerate((forward_up, not forward_up)):
        groups = list(range(n_g)) if up else list(range(n_g))[::-1]
        entry = jnp.zeros((size, LANES), F32)
        for k in groups:
            state = sliced(zrec_ref, k, size)[branch]
            passed = place > k if up else place < k
            entry = jnp.where(passed, totals_at(zdec_ref, k, 2 * size)[branch] * entry + state, entry)
        members = list(range(n)) if up else list(range(n))[::-1]
        for i in members:
            out_ref[i, branch * size : (branch + 1) * size, :] = entry
            entry = totals_at(dec_ref, i, 2 * size)[branch] * entry + sliced(rec_ref, i, size)[branch]


def add_rows(rec_ref, out_ref):
    total = rec_ref[0, :, :]
    for i in range(1, rec_ref.shape[0]):
        total = total + rec_ref[i, :, :]
    size = out_ref.shape[1]
    for k in range(out_ref.shape[0]):
        out_ref[k, :, :] = total[k * size : (k + 1) * size, :]


def copy_rows(rec_ref, out_ref):
    n = rec_ref.shape[0]
    size = rec_ref.shape[1]
    for k in range(n):
        part = rec_ref[k, :, :]
        for i in range(out_ref.shape[0]):
            out_ref[i, k * size : (k + 1) * size, :] = part


def weight_rows(rec_ref, gw_ref):
    for j in range(HEADS):
        for block in range(gw_ref.shape[1] // LANES):
            gw_ref[j * 64 : (j + 1) * 64, block * LANES : (block + 1) * LANES] = (
                rec_ref[j, block * 64 : (block + 1) * 64, :] * WEIGHT_SCALE
            )


def across_rows(cols):
    lane = lax.broadcasted_iota(jnp.int32, (LANES, LANES), 1)
    grid = jnp.zeros((LANES, LANES), F32)
    for i, col in enumerate(cols):
        for part in range(FRAMES // LANES):
            at = i * (FRAMES // LANES) + part
            grid = jnp.where(lane == at, col[part * LANES : (part + 1) * LANES, :], grid)
    return jnp.transpose(grid)[0:8, :]


def outputs(
    skip_ref, x_ref, z_ref, b_ref, c_ref, df_ref, db_ref, gain_ref, w_ref, do_ref, ent_ref,
    y_ref, m_ref, sums_ref,
):
    df, db = df_ref[...], db_ref[...]
    cf, be, end_f, end_b = columns(df, db)
    cf_row, be_row = rows(df, db)
    row, col = places()
    c = c_ref[...]
    scores = dot(c, b_ref[...], 1, 1)
    entry_f, entry_b = take_slices(ent_ref)
    far = spread(jnp.exp(cf)) * dot_right(c, entry_f, 1, 1)
    far = far + spread(jnp.exp(end_b - be)) * dot_right(c, entry_b, 1, 1)
    near = []
    lane = lax.broadcasted_iota(jnp.int32, (1, LANES), 1)
    for g in range(HEADS // 2):
        pair = x_ref[:, g * LANES : (g + 1) * LANES]
        acc = jnp.where(lane < HEAD_DIM, skip_ref[2 * g], skip_ref[2 * g + 1]) * pair.astype(F32)
        for hh in range(2):
            weights = scores * pair_decay(2 * g + hh, cf, be, cf_row, be_row, row, col)
            acc = acc + dot_left(weights, own_lanes(pair, hh), 1, 0)
        near.append(acc)
    y = far + jnp.concatenate(near, axis=1)
    z = z_ref[...].astype(F32)
    u = y * z * jax.nn.sigmoid(z)
    m = dot(do_ref[...], w_ref[...], 1, 1) * gain_ref[...]
    y_ref[...] = y
    m_ref[...] = m
    sums = across_rows([jnp.sum(u * u, axis=1, keepdims=True), jnp.sum(u * m, axis=1, keepdims=True)])
    for i in range(sums_ref.shape[0]):
        sums_ref[i, :, :] = sums


def gradients(
    sums_ref, y_ref, m_ref, z_ref, c_ref, df_ref, db_ref, gain_ref, do_ref,
    dy_ref, gz_ref, out_ref, w_ref, *, inner,
):
    total = sums_ref[0, :, :]
    for i in range(1, sums_ref.shape[0]):
        total = total + sums_ref[i, :, :]
    grid = jnp.transpose(jnp.concatenate([total, jnp.zeros((LANES - 8, LANES), F32)], axis=0))
    square = jnp.concatenate([grid[:, 0:1], grid[:, 1:2]], axis=0) / inner
    cross = jnp.concatenate([grid[:, 2:3], grid[:, 3:4]], axis=0) / inner
    q = lax.rsqrt(square + EPS_NORM)
    y, m, z = y_ref[...], m_ref[...], z_ref[...].astype(F32)
    sig = jax.nn.sigmoid(z)
    silu = z * sig
    u = y * z * sig
    normed = (u * q * gain_ref[...]).astype(BF16)
    du = q * m - u * (q * q * q * cross)
    dy = du * silu
    gz_ref[...] = (du * y * sig * (1.0 + z * (1.0 - sig))).astype(BF16)
    dy_ref[...] = dy
    cf, be, end_f, end_b = columns(df_ref[...], db_ref[...])
    c = c_ref[...]
    back_f = dot_left(dy * spread(jnp.exp(cf)), c, 0, 0)
    back_b = dot_left(dy * spread(jnp.exp(end_b - be)), c, 0, 0)
    put_slices(out_ref, back_f, back_b)
    weight = dot(normed, do_ref[...], 0, 0)
    for j in range(HEADS):
        for block in range(weight.shape[1] // LANES):
            w_ref[j, block * 64 : (block + 1) * 64, :] = weight[
                j * 64 : (j + 1) * 64, block * LANES : (block + 1) * LANES
            ]


def finish(
    skip_ref, x_ref, b_ref, c_ref, df_ref, db_ref, dy_ref, ent_ref, exit_ref,
    gx_ref, out_ref,
):
    df, db = df_ref[...], db_ref[...]
    cf, be, end_f, end_b = columns(df, db)
    cf_row, be_row = rows(df, db)
    row, col = places()
    b, c, dy = b_ref[...], c_ref[...], dy_ref[...]
    x = x_ref[...].astype(F32)
    scores = dot(c, b, 1, 1)
    pair_sum = jnp.zeros((FRAMES, FRAMES), F32)
    near = []
    lane = lax.broadcasted_iota(jnp.int32, (1, LANES), 1)
    for g in range(HEADS // 2):
        at = slice(g * LANES, (g + 1) * LANES)
        acc = jnp.where(lane < HEAD_DIM, skip_ref[2 * g], skip_ref[2 * g + 1]) * dy[:, at]
        for hh in range(2):
            decay = pair_decay(2 * g + hh, cf, be, cf_row, be_row, row, col)
            dy_own = own_lanes(dy[:, at], hh)
            pair_sum = pair_sum + decay * dot_left(dy_own, x_ref[:, at], 1, 1)
            acc = acc + dot_both(scores * decay, dy_own, 0, 0)
        near.append(acc)
    rise_f, rise_b = spread(jnp.exp(cf)), spread(jnp.exp(end_b - be))
    tail_f, lead_b = spread(jnp.exp(end_f - cf)), spread(jnp.exp(be))
    entry_f, entry_b = take_slices(ent_ref)
    exit_f, exit_b = take_slices(exit_ref)
    gx = jnp.concatenate(near, axis=1)
    gx = gx + tail_f * dot_right(b, exit_f, 1, 1) + lead_b * dot_right(b, exit_b, 1, 1)
    gx_ref[...] = gx.astype(BF16)
    grad_c = dot_left(pair_sum, b, 1, 0)
    grad_c = grad_c + dot_both(dy * rise_f, entry_f, 1, 0) + dot_both(dy * rise_b, entry_b, 1, 0)
    grad_b = dot_left(pair_sum, c, 0, 0)
    grad_b = grad_b + dot_both(x * tail_f, exit_f, 1, 0) + dot_both(x * lead_b, exit_b, 1, 0)
    n = out_ref.shape[0]
    size = FRAMES // n
    for i in range(n):
        out_ref[i, 0:size, :] = grad_b[i * size : (i + 1) * size, :]
        out_ref[i, size : 2 * size, :] = grad_c[i * size : (i + 1) * size, :]


def add_up(rec_ref, out_ref):
    n = rec_ref.shape[0]
    total = rec_ref[0, :, :]
    for i in range(1, n):
        total = total + rec_ref[i, :, :]
    for i in range(n):
        out_ref[i, :, :] = total


def deal_out(rec_ref, gb_ref, gc_ref):
    n = rec_ref.shape[0]
    size = FRAMES // n
    for i in range(n):
        gb_ref[i * size : (i + 1) * size, :] = rec_ref[i, 0:size, :]
        gc_ref[i * size : (i + 1) * size, :] = rec_ref[i, size : 2 * size, :]


VMEM = pl.BlockSpec(memory_space=pltpu.VMEM)
SMEM = pl.BlockSpec(memory_space=pltpu.SMEM)


def call(kernel, name, out, *args, scalars=0):
    shapes = [jax.ShapeDtypeStruct(shape, dtype) for shape, dtype in out]
    single = len(shapes) == 1
    return pl.pallas_call(
        kernel,
        name=name,
        out_shape=shapes[0] if single else tuple(shapes),
        in_specs=[SMEM] * scalars + [VMEM] * (len(args) - scalars),
        out_specs=VMEM if single else tuple(VMEM for _ in shapes),
        compiler_params=pltpu.CompilerParams(vmem_limit_bytes=48 * 1024 * 1024),
    )(*args)


def exchange(a, axis):
    return lax.all_to_all(a, axis, 0, 0, tiled=True)


def body(x_in, gate_in, b_in, c_in, decay_fwd, decay_bwd, skip_gain, norm_gain, w_out, d_out):
    n_hi, n_lo, n_x, n_h = (lax.axis_size(axis) for axis in ("z_hi", "z_lo", "x", "head"))
    group, along = ("z_lo", "x"), ("z_hi", "z_lo")
    n, n_z = n_lo * n_x, n_hi * n_lo
    gain = norm_gain.reshape(1, WIDTH)
    state = 2 * WIDTH // n
    place = lax.axis_index("z_hi").astype(jnp.int32).reshape(1)

    sent = call(local_states, "local_states", [((n, state + 8, LANES), F32)], x_in, b_in, decay_fwd, decay_bwd)
    rec1 = exchange(sent, group)
    up = functools.partial(group_totals, forward_up=True)
    sent = call(up, "totals_up", [((n_hi, state + 8, LANES), F32)], rec1, rec1)
    recz1 = exchange(sent, "z_hi")
    up = functools.partial(group_entries, forward_up=True)
    sent = call(up, "entries_up", [((n, state, LANES), F32)], place, recz1, recz1, rec1, rec1, scalars=1)
    entries = exchange(sent, group)

    y, m, sums = call(
        outputs, "outputs",
        [((FRAMES, WIDTH), F32), ((FRAMES, WIDTH), F32), ((n_h, 8, LANES), F32)],
        skip_gain, x_in, gate_in, b_in, c_in, decay_fwd, decay_bwd, gain, w_out, d_out, entries,
        scalars=1,
    )
    sums = exchange(sums, "head")
    dy, grad_z, sent, weight = call(
        functools.partial(gradients, inner=WIDTH * n_h), "gradients",
        [((FRAMES, WIDTH), F32), ((FRAMES, WIDTH), BF16), ((n, state, LANES), F32), ((n_x, 512, LANES), F32)],
        sums, y, m, gate_in, c_in, decay_fwd, decay_bwd, gain, d_out,
    )

    rec2 = exchange(sent, group)
    down = functools.partial(group_totals, forward_up=False)
    sent = call(down, "totals_down", [((n_hi, state, LANES), F32)], rec1, rec2)
    recz2 = exchange(sent, "z_hi")
    down = functools.partial(group_entries, forward_up=False)
    sent = call(down, "entries_down", [((n, state, LANES), F32)], place, recz1, recz2, rec1, rec2, scalars=1)
    exits = exchange(sent, group)

    weight = exchange(weight, "x")
    weight = call(add_rows, "weight_x", [((n_z, 512 // n_z, LANES), F32)], weight)
    weight = exchange(weight, along)
    weight = call(add_up, "weight_z", [((n_z, 512 // n_z, LANES), F32)], weight)
    weight = exchange(weight, along)
    weight = call(copy_rows, "weight_copy", [((n_x, 512, LANES), F32)], weight)
    weight = exchange(weight, "x")
    grad_w = call(weight_rows, "weight_rows", [((WIDTH, d_out.shape[1]), F32)], weight)

    chunk = 2 * FRAMES // n_h
    grad_x, sent = call(
        finish, "finish",
        [((FRAMES, WIDTH), BF16), ((n_h, chunk, LANES), F32)],
        skip_gain, x_in, b_in, c_in, decay_fwd, decay_bwd, dy, entries, exits,
        scalars=1,
    )
    rec = exchange(sent, "head")
    sent = call(add_up, "add_up", [((n_h, chunk, LANES), F32)], rec)
    rec = exchange(sent, "head")
    grad_b, grad_c = call(deal_out, "deal_out", [((FRAMES, STATE), F32)] * 2, rec)
    return grad_x, grad_z, grad_b, grad_c, grad_w


def solution(mesh):
    n_seq, n_head = mesh.devices.shape
    n_z = n_seq // HEADS
    n_lo = min(4, n_z // 2)
    split = Mesh(mesh.devices.reshape(n_z // n_lo, n_lo, HEADS, n_head), ("z_hi", "z_lo", "x", "head"))
    seq = ("z_hi", "z_lo", "x")
    in_specs = (
        P(seq, "head"),
        P(seq, "head"),
        P(seq, None),
        P(seq, None),
        P("head", seq),
        P("head", seq),
        P("head"),
        P("head"),
        P("head", None),
        P(seq, None),
    )
    out_specs = (
        P(seq, "head"),
        P(seq, "head"),
        P(seq, None),
        P(seq, None),
        P("head", None),
    )
    return jax.shard_map(body, mesh=split, in_specs=in_specs, out_specs=out_specs, check_vma=False)
```

time: 200 us -> 225 us (1.12)
  blocking collectives: 136 us -> 72.2 us
  waiting for transfers between devices: 26 us -> 76.4 us
  starting transfers between devices: 18.6 us -> 53.5 us
  Pallas kernels: 11.8 us -> 16.6 us
    all_to_all x9 -> x5, blocking collectives: 136 us -> 72.2 us  [exchange(): return lax.all_to_all(a, axis, 0, 0, tiled=True)]
    all_to_all x2 -> x8, waiting for transfers between devices: 26 us -> 76.4 us  [exchange(): return lax.all_to_all(a, axis, 0, 0, tiled=True)]
    all_to_all x2 -> x8, starting transfers between devices: 18.6 us -> 53.5 us  [exchange(): return lax.all_to_all(a, axis, 0, 0, tiled=True)]
    pallas_call x12 -> x14, Pallas kernels: 11.8 us -> 16.6 us  [call(): pl.pallas_call(kernel, name=name, out_shape=shapes[0] if single else tupl...]
  transfers between devices with their start and end apart: 2 -> 8, of which waited for: 2 -> 8; matrix products, arithmetic and copies ran while one was open for 0% -> 0% of each run, Pallas kernels for 0% -> 4%
where the time goes in v2:
time: 225 us; the launch traced here: 223 us
  waiting for transfers between devices  76.4 us (34%)
  blocking collectives  72.2 us (32%)
  starting transfers between devices  53.5 us (24%)
  Pallas kernels  16.6 us (7%)
  local copies, waits for them, and re-layouts  3.76 us (2%)
    all_to_all x8, waiting for transfers between devices, exchange(): return lax.all_to_all(a, axis, 0, 0, tiled=True)  76.4 us
    all_to_all x5, blocking collectives, exchange(): return lax.all_to_all(a, axis, 0, 0, tiled=True)  72.2 us
    all_to_all x8, starting transfers between devices, exchange(): return lax.all_to_all(a, axis, 0, 0, tiled=True)  53.5 us
    pallas_call x14, Pallas kernels, call(): pl.pallas_call(kernel, name=name, out_shape=shapes[0] if single else tupl...  16.6 us
  transfers between devices with their start and end apart: 8, of which 8 were waited for; matrix products, arithmetic and copies ran while one was open for 0% of the time, Pallas kernels for 4%

profile of v2, /device:TPU:1, one launch (start us, length us, event | category | flops | bytes accessed | tf_op | source)
XLA Modules:
  0.0 223.1 jit_solution(8322880767046682039)
XLA Ops:
  0.6 0.9 copy-done.1
  1.5 0.8 copy-done.4
  3.8 1.2 local_states.1
  5.0 19.4 %all_to_all.65.dec_ref.rec_ref = f32[16,40,128]{2,1,0:T(8,128)S(1)} all-to-all(f32[16,40,128]{2,1,0:T(8,128)S(1)} %local_states.1), channel_id=1, replica_groups=mesh['z_hi'=4,'z_lo'=4,'x'=4,'head'=8] {'z_lo','x'}, dimensions={0} | all-to-all | bytes 655360 | tf_op jit(solution)/shard_map/all_to_all | solution.py:359
  25.1 12.1 %all-to-all-start.1 = ((f32[4,40,128]{2,1,0:T(8,128)}), f32[4,40,128]{2,1,0:T(8,128)S(1)}, u32[]{:S(2)}, u32[]{:S(2)}) async-start(f32[4,40,128]{2,1,0:T(8,128)} %totals_up.1), calls=%async_computation.1 | async-start | bytes 163840 | tf_op jit(solution)/shard_map/all_to_all | solution.py:359
  37.2 12.0 %all-to-all-done.1.zdec_ref.zrec_ref = f32[4,40,128]{2,1,0:T(8,128)S(1)} async-done(((f32[4,40,128]{2,1,0:T(8,128)}), f32[4,40,128]{2,1,0:T(8,128)S(1)}, u32[]{:S(2)}, u32[]{:S(2)}) %all-to-all-start.1) | async-done | bytes 81952 | tf_op jit(solution)/shard_map/all_to_all | solution.py:359
  49.4 12.9 %all_to_all.66.ent_ref = f32[16,32,128]{2,1,0:T(8,128)S(1)} all-to-all(f32[16,32,128]{2,1,0:T(8,128)S(1)} %entries_up.1), channel_id=1, replica_groups=mesh['z_hi'=4,'z_lo'=4,'x'=4,'head'=8] {'z_lo','x'}, dimensions={0} | all-to-all | bytes 524288 | tf_op jit(solution)/shard_map/all_to_all | solution.py:359
  62.9 2.4 %outputs.1 = (f32[256,256]{1,0:T(8,128)S(1)}, f32[256,256]{1,0:T(8,128)S(1)}, f32[8,8,128]{2,1,0:T(8,128)S(1)}) custom-call(f32[4]{0:T(128)S(1)} %copy-done.13, bf16[256,256]{1,0:T(8,128)(2,1)S(1)} %copy-done.2, bf16[256,256]{1,0:T(8,128)(2,1)S(1)} %copy-done.7, bf16[256,128]{1,0:T(8,128)(2,1)S(1)} %copy-done.5, bf16[256,128]{1,0:T(8,128)(2,1)S(1)} %copy-done.3, ...), custom_call_target="tpu_custom_call" | custom-call | tf_op jit(solution)/shard_map/outputs/pallas_call | solution.py:348
  65.4 13.7 %all_to_all.67.sums_ref = f32[8,8,128]{2,1,0:T(8,128)S(1)} all-to-all(f32[8,8,128]{2,1,0:T(8,128)S(1)} %get-tuple-element.16), channel_id=1, replica_groups=mesh['z_hi'=4,'z_lo'=4,'x'=4,'head'=8] {'head'}, dimensions={0} | all-to-all | bytes 65536 | tf_op jit(solution)/shard_map/all_to_all | solution.py:359
  79.1 2.4 %gradients.1 = (f32[256,256]{1,0:T(8,128)S(1)}, bf16[256,256]{1,0:T(8,128)(2,1)}, f32[16,32,128]{2,1,0:T(8,128)S(1)}, f32[4,512,128]{2,1,0:T(8,128)}) custom-call(f32[8,8,128]{2,1,0:T(8,128)S(1)} %all_to_all.67.sums_ref, f32[256,256]{1,0:T(8,128)S(1)} %get-tuple-element.17.y_ref, f32[256,256]{1,0:T(8,128)S(1)} %get-tuple-element.18.m_ref, ...), custom_call_target="tpu_custom_call" | custom-call | tf_op jit(solution)/shard_map/gradients/pallas_call | solution.py:348
  81.5 12.0 %all_to_all.68.rec_ref = f32[16,32,128]{2,1,0:T(8,128)S(1)} all-to-all(f32[16,32,128]{2,1,0:T(8,128)S(1)} %get-tuple-element.20), channel_id=1, replica_groups=mesh['z_hi'=4,'z_lo'=4,'x'=4,'head'=8] {'z_lo','x'}, dimensions={0} | all-to-all | bytes 524288 | tf_op jit(solution)/shard_map/all_to_all | solution.py:359
  93.5 14.2 %all_to_all.69.zrec_ref = f32[4,32,128]{2,1,0:T(8,128)S(1)} all-to-all(f32[4,32,128]{2,1,0:T(8,128)S(1)} %totals_down.1), channel_id=1, replica_groups=mesh['z_hi'=4,'z_lo'=4,'x'=4,'head'=8] {'z_hi'}, dimensions={0} | all-to-all | bytes 131072 | tf_op jit(solution)/shard_map/all_to_all | solution.py:359
  107.7 3.5 %all-to-all-start.9 = ((f32[4,512,128]{2,1,0:T(8,128)}), f32[4,512,128]{2,1,0:T(8,128)S(1)}, u32[]{:S(2)}, u32[]{:S(2)}) async-start(f32[4,512,128]{2,1,0:T(8,128)} %get-tuple-element.26), calls=%async_computation.9 | async-start | bytes 2097152 | tf_op jit(solution)/shard_map/all_to_all | solution.py:359
  111.2 0.8 entries_down.1
  111.9 10.6 %all-to-all-done.9.rec_ref = f32[4,512,128]{2,1,0:T(8,128)S(1)} async-done(((f32[4,512,128]{2,1,0:T(8,128)}), f32[4,512,128]{2,1,0:T(8,128)S(1)}, u32[]{:S(2)}, u32[]{:S(2)}) %all-to-all-start.9) | async-done | bytes 1048608 | tf_op jit(solution)/shard_map/all_to_all | solution.py:359
  122.5 5.6 %all-to-all-start.6 = ((f32[16,32,128]{2,1,0:T(8,128)}), f32[16,32,128]{2,1,0:T(8,128)S(1)}, u32[]{:S(2)}, u32[]{:S(2)}) async-start(f32[16,32,128]{2,1,0:T(8,128)} %entries_down.1), calls=%async_computation.6 | async-start | bytes 524288 | tf_op jit(solution)/shard_map/all_to_all | solution.py:359
  128.1 0.8 weight_x.1
  128.9 8.1 %all-to-all-done.6.exit_ref = f32[16,32,128]{2,1,0:T(8,128)S(1)} async-done(((f32[16,32,128]{2,1,0:T(8,128)}), f32[16,32,128]{2,1,0:T(8,128)S(1)}, u32[]{:S(2)}, u32[]{:S(2)}) %all-to-all-start.6) | async-done | bytes 262176 | tf_op jit(solution)/shard_map/all_to_all | solution.py:359
  137.0 3.6 %all-to-all-start.10 = ((f32[16,32,128]{2,1,0:T(8,128)}), f32[16,32,128]{2,1,0:T(8,128)S(1)}, u32[]{:S(2)}, u32[]{:S(2)}) async-start(f32[16,32,128]{2,1,0:T(8,128)} %weight_x.1), calls=%async_computation.10 | async-start | bytes 524288 | tf_op jit(solution)/shard_map/all_to_all | solution.py:359
  140.6 4.0 %finish.1 = (bf16[256,256]{1,0:T(8,128)(2,1)}, f32[8,64,128]{2,1,0:T(8,128)}) custom-call(f32[4]{0:T(128)S(1)} %copy-done.13, bf16[256,256]{1,0:T(8,128)(2,1)S(1)} %copy-done.2, bf16[256,128]{1,0:T(8,128)(2,1)S(1)} %copy-done.5, bf16[256,128]{1,0:T(8,128)(2,1)S(1)} %copy-done.3, f32[4,256]{1,0:T(4,128)S(1)} %copy-done.9, f32[4,256]{1,0:T(4,128)S(1)} %copy-done.11, ...), custom_call_target="tpu_custom_call" | custom-call | tf_op jit(solution)/shard_map/finish/pallas_call | solution.py:348
  144.5 8.8 %all-to-all-done.10.rec_ref = f32[16,32,128]{2,1,0:T(8,128)S(1)} async-done(((f32[16,32,128]{2,1,0:T(8,128)}), f32[16,32,128]{2,1,0:T(8,128)S(1)}, u32[]{:S(2)}, u32[]{:S(2)}) %all-to-all-start.10) | async-done | bytes 262176 | tf_op jit(solution)/shard_map/all_to_all | solution.py:359
  153.3 10.1 %all-to-all-start.7 = ((f32[8,64,128]{2,1,0:T(8,128)}), f32[8,64,128]{2,1,0:T(8,128)S(1)}, u32[]{:S(2)}, u32[]{:S(2)}) async-start(f32[8,64,128]{2,1,0:T(8,128)} %get-tuple-element.23), calls=%async_computation.7 | async-start | bytes 524288 | tf_op jit(solution)/shard_map/all_to_all | solution.py:359
  163.4 0.7 weight_z.1
  164.2 5.8 %all-to-all-done.7.rec_ref = f32[8,64,128]{2,1,0:T(8,128)S(1)} async-done(((f32[8,64,128]{2,1,0:T(8,128)}), f32[8,64,128]{2,1,0:T(8,128)S(1)}, u32[]{:S(2)}, u32[]{:S(2)}) %all-to-all-start.7) | async-done | bytes 262176 | tf_op jit(solution)/shard_map/all_to_all | solution.py:359
  169.9 5.3 %all-to-all-start.11 = ((f32[16,32,128]{2,1,0:T(8,128)}), f32[16,32,128]{2,1,0:T(8,128)S(1)}, u32[]{:S(2)}, u32[]{:S(2)}) async-start(f32[16,32,128]{2,1,0:T(8,128)} %weight_z.1), calls=%async_computation.11 | async-start | bytes 524288 | tf_op jit(solution)/shard_map/all_to_all | solution.py:359
  175.9 12.2 %all-to-all-done.11.rec_ref = f32[16,32,128]{2,1,0:T(8,128)S(1)} async-done(((f32[16,32,128]{2,1,0:T(8,128)}), f32[16,32,128]{2,1,0:T(8,128)S(1)}, u32[]{:S(2)}, u32[]{:S(2)}) %all-to-all-start.11) | async-done | bytes 262176 | tf_op jit(solution)/shard_map/all_to_all | solution.py:359
  188.2 9.8 %all-to-all-start.8 = ((f32[8,64,128]{2,1,0:T(8,128)}), f32[8,64,128]{2,1,0:T(8,128)S(1)}, u32[]{:S(2)}, u32[]{:S(2)}) async-start(f32[8,64,128]{2,1,0:T(8,128)} %add_up.1), calls=%async_computation.8 | async-start | bytes 524288 | tf_op jit(solution)/shard_map/all_to_all | solution.py:359
  198.0 1.0 weight_copy.1
  199.0 5.5 %all-to-all-done.8.rec_ref = f32[8,64,128]{2,1,0:T(8,128)S(1)} async-done(((f32[8,64,128]{2,1,0:T(8,128)}), f32[8,64,128]{2,1,0:T(8,128)S(1)}, u32[]{:S(2)}, u32[]{:S(2)}) %all-to-all-start.8) | async-done | bytes 262176 | tf_op jit(solution)/shard_map/all_to_all | solution.py:359
  204.5 3.5 %all-to-all-start.12 = ((f32[4,512,128]{2,1,0:T(8,128)}), f32[4,512,128]{2,1,0:T(8,128)S(1)}, u32[]{:S(2)}, u32[]{:S(2)}) async-start(f32[4,512,128]{2,1,0:T(8,128)} %weight_copy.1), calls=%async_computation.12 | async-start | bytes 2097152 | tf_op jit(solution)/shard_map/all_to_all | solution.py:359
  208.8 13.3 %all-to-all-done.12.rec_ref = f32[4,512,128]{2,1,0:T(8,128)S(1)} async-done(((f32[4,512,128]{2,1,0:T(8,128)}), f32[4,512,128]{2,1,0:T(8,128)S(1)}, u32[]{:S(2)}, u32[]{:S(2)}) %all-to-all-start.12) | async-done | bytes 1048608 | tf_op jit(solution)/shard_map/all_to_all | solution.py:359
  222.1 1.0 weight_rows.1
  (31 shorter events, 4.2 us)
Async XLA Ops:
  0.6 0.9 copy-start.1
  1.5 0.8 copy-start.4
  2.4 0.7 copy-start.8
  3.1 0.7 copy-start.10
  25.1 24.1 %all-to-all-start.1 = ((f32[4,40,128]{2,1,0:T(8,128)}), f32[4,40,128]{2,1,0:T(8,128)S(1)}, u32[]{:S(2)}, u32[]{:S(2)}) async-start(f32[4,40,128]{2,1,0:T(8,128)} %totals_up.1), calls=%async_computation.1 | async-start | bytes 163840 | tf_op jit(solution)/shard_map/all_to_all | solution.py:359
  49.3 13.0 %copy-start.2 = (bf16[256,256]{1,0:T(8,128)(2,1)S(1)}, bf16[256,256]{1,0:T(8,128)(2,1)}, u32[]{:S(2)}) copy-start(bf16[256,256]{1,0:T(8,128)(2,1)} %x_ref.5) | copy-start | bytes 393220
  49.3 13.0 %copy-start.3 = (bf16[256,128]{1,0:T(8,128)(2,1)S(1)}, bf16[256,128]{1,0:T(8,128)(2,1)}, u32[]{:S(2)}) copy-start(bf16[256,128]{1,0:T(8,128)(2,1)} %c_ref.5) | copy-start | bytes 196612
  49.3 13.0 %copy-start.5 = (bf16[256,128]{1,0:T(8,128)(2,1)S(1)}, bf16[256,128]{1,0:T(8,128)(2,1)}, u32[]{:S(2)}) copy-start(bf16[256,128]{1,0:T(8,128)(2,1)} %b_ref.5) | copy-start | bytes 196612
  49.3 13.0 %copy-start.6 = (bf16[256,1024]{1,0:T(8,128)(2,1)S(1)}, bf16[256,1024]{1,0:T(8,128)(2,1)}, u32[]{:S(2)}) copy-start(bf16[256,1024]{1,0:T(8,128)(2,1)} %w_ref.1) | copy-start | bytes 1572868
  49.3 13.0 %copy-start.7 = (bf16[256,256]{1,0:T(8,128)(2,1)S(1)}, bf16[256,256]{1,0:T(8,128)(2,1)}, u32[]{:S(2)}) copy-start(bf16[256,256]{1,0:T(8,128)(2,1)} %z_ref.3) | copy-start | bytes 393220
  49.3 13.0 %copy-start.9 = (f32[4,256]{1,0:T(4,128)S(1)}, f32[4,256]{1,0:T(4,128)}, u32[]{:S(2)}) copy-start(f32[4,256]{1,0:T(4,128)} %df_ref.7) | copy-start | bytes 12292
  49.3 13.0 %copy-start.11 = (f32[4,256]{1,0:T(4,128)S(1)}, f32[4,256]{1,0:T(4,128)}, u32[]{:S(2)}) copy-start(f32[4,256]{1,0:T(4,128)} %db_ref.7) | copy-start | bytes 12292
  49.4 12.9 %copy-start = (bf16[256,1024]{1,0:T(8,128)(2,1)S(1)}, bf16[256,1024]{1,0:T(8,128)(2,1)}, u32[]{:S(2)}) copy-start(bf16[256,1024]{1,0:T(8,128)(2,1)} %do_ref.3) | copy-start | bytes 1572868
  62.2 0.7 copy-start.12
  62.2 0.7 copy-start.13
  107.7 14.9 %all-to-all-start.9 = ((f32[4,512,128]{2,1,0:T(8,128)}), f32[4,512,128]{2,1,0:T(8,128)S(1)}, u32[]{:S(2)}, u32[]{:S(2)}) async-start(f32[4,512,128]{2,1,0:T(8,128)} %get-tuple-element.26), calls=%async_computation.9 | async-start | bytes 2097152 | tf_op jit(solution)/shard_map/all_to_all | solution.py:359
  122.5 14.4 %all-to-all-start.6 = ((f32[16,32,128]{2,1,0:T(8,128)}), f32[16,32,128]{2,1,0:T(8,128)S(1)}, u32[]{:S(2)}, u32[]{:S(2)}) async-start(f32[16,32,128]{2,1,0:T(8,128)} %entries_down.1), calls=%async_computation.6 | async-start | bytes 524288 | tf_op jit(solution)/shard_map/all_to_all | solution.py:359
  137.0 16.4 %all-to-all-start.10 = ((f32[16,32,128]{2,1,0:T(8,128)}), f32[16,32,128]{2,1,0:T(8,128)S(1)}, u32[]{:S(2)}, u32[]{:S(2)}) async-start(f32[16,32,128]{2,1,0:T(8,128)} %weight_x.1), calls=%async_computation.10 | async-start | bytes 524288 | tf_op jit(solution)/shard_map/all_to_all | solution.py:359
  153.3 16.6 %all-to-all-start.7 = ((f32[8,64,128]{2,1,0:T(8,128)}), f32[8,64,128]{2,1,0:T(8,128)S(1)}, u32[]{:S(2)}, u32[]{:S(2)}) async-start(f32[8,64,128]{2,1,0:T(8,128)} %get-tuple-element.23), calls=%async_computation.7 | async-start | bytes 524288 | tf_op jit(solution)/shard_map/all_to_all | solution.py:359
  169.9 18.3 %all-to-all-start.11 = ((f32[16,32,128]{2,1,0:T(8,128)}), f32[16,32,128]{2,1,0:T(8,128)S(1)}, u32[]{:S(2)}, u32[]{:S(2)}) async-start(f32[16,32,128]{2,1,0:T(8,128)} %weight_z.1), calls=%async_computation.11 | async-start | bytes 524288 | tf_op jit(solution)/shard_map/all_to_all | solution.py:359
  188.2 16.3 %all-to-all-start.8 = ((f32[8,64,128]{2,1,0:T(8,128)}), f32[8,64,128]{2,1,0:T(8,128)S(1)}, u32[]{:S(2)}, u32[]{:S(2)}) async-start(f32[8,64,128]{2,1,0:T(8,128)} %add_up.1), calls=%async_computation.8 | async-start | bytes 524288 | tf_op jit(solution)/shard_map/all_to_all | solution.py:359
  204.5 17.6 %all-to-all-start.12 = ((f32[4,512,128]{2,1,0:T(8,128)}), f32[4,512,128]{2,1,0:T(8,128)S(1)}, u32[]{:S(2)}, u32[]{:S(2)}) async-start(f32[4,512,128]{2,1,0:T(8,128)} %weight_copy.1), calls=%async_computation.12 | async-start | bytes 2097152 | tf_op jit(solution)/shard_map/all_to_all | solution.py:359

commit v3 on v2

--- a/solution.py
+++ b/solution.py
@@ -114,7 +114,13 @@
     return forward, backward
 
 
-def local_states(x_ref, b_ref, df_ref, db_ref, out_ref):
+def local_states(x_hbm, b_hbm, df_hbm, db_hbm, out_ref, x_ref, b_ref, df_ref, db_ref, sems):
+    sources, targets = (x_hbm, b_hbm, df_hbm, db_hbm), (x_ref, b_ref, df_ref, db_ref)
+    copies = [pltpu.make_async_copy(s, t, sems.at[i]) for i, (s, t) in enumerate(zip(sources, targets))]
+    for copy in copies:
+        copy.start()
+    for copy in copies:
+        copy.wait()
     cf, be, end_f, end_b = columns(df_ref[...], db_ref[...])
     x = x_ref[...].astype(F32)
     b = b_ref[...]
@@ -139,68 +145,114 @@
     return ref[i, 0:size, :], ref[i, size : 2 * size, :]
 
 
-def group_totals(dec_ref, rec_ref, out_ref, *, forward_up):
+def group_sums(dec_ref, rec_ref, forward_up):
     n = rec_ref.shape[0]
     size = WIDTH // n
     decays = [totals_at(dec_ref, i, 2 * size) for i in range(n)]
     parts = [sliced(rec_ref, i, size) for i in range(n)]
-    ups = list(range(n))
+    sums = []
     for branch, up in enumerate((forward_up, not forward_up)):
-        order = ups if up else ups[::-1]
+        order = list(range(n)) if up else list(range(n))[::-1]
         acc = parts[order[0]][branch]
         for i in order[1:]:
             acc = decays[i][branch] * acc + parts[i][branch]
-        for k in range(out_ref.shape[0]):
-            out_ref[k, branch * size : (branch + 1) * size, :] = acc
-    if out_ref.shape[1] > 2 * size:
-        all_f, all_b = decays[0]
-        for i in range(1, n):
-            all_f, all_b = all_f * decays[i][0], all_b * decays[i][1]
-        half = lax.broadcasted_iota(jnp.int32, (8, LANES), 0) < 4
-        for k in range(out_ref.shape[0]):
-            out_ref[k, 2 * size :, :] = jnp.where(half, all_f, all_b)
-
-
-def group_entries(place_ref, zdec_ref, zrec_ref, dec_ref, rec_ref, out_ref, *, forward_up):
+        sums.append(acc)
+    return sums, decays
+
+
+def totals_up(place_ref, rec_ref, out_ref):
+    size = WIDTH // rec_ref.shape[0]
+    (sum_f, sum_b), decays = group_sums(rec_ref, rec_ref, True)
+    all_f, all_b = decays[0]
+    for dec_f, dec_b in decays[1:]:
+        all_f, all_b = all_f * dec_f, all_b * dec_b
+    half = lax.broadcasted_iota(jnp.int32, (8, LANES), 0) < 4
+    for k in range(out_ref.shape[0]):
+        out_ref[k, 0:size, :] = jnp.where(place_ref[0] < k, sum_f, sum_b)
+        out_ref[k, size:, :] = jnp.where(half, all_f, all_b)
+
+
+def entries_up(place_ref, zrec_ref, rec_ref, out_ref):
     n_g, n = zrec_ref.shape[0], rec_ref.shape[0]
     size = WIDTH // n
     place = place_ref[0]
-    for branch, up in enumerate((forward_up, not forward_up)):
-        groups = list(range(n_g)) if up else list(range(n_g))[::-1]
+    for branch, up in enumerate((True, False)):
         entry = jnp.zeros((size, LANES), F32)
-        for k in groups:
-            state = sliced(zrec_ref, k, size)[branch]
+        for k in list(range(n_g)) if up else list(range(n_g))[::-1]:
             passed = place > k if up else place < k
-            entry = jnp.where(passed, totals_at(zdec_ref, k, 2 * size)[branch] * entry + state, entry)
-        members = list(range(n)) if up else list(range(n))[::-1]
-        for i in members:
-            out_ref[i, branch * size : (branch + 1) * size, :] = entry
-            entry = totals_at(dec_ref, i, 2 * size)[branch] * entry + sliced(rec_ref, i, size)[branch]
-
-
-def add_rows(rec_ref, out_ref):
-    total = rec_ref[0, :, :]
-    for i in range(1, rec_ref.shape[0]):
-        total = total + rec_ref[i, :, :]
-    size = out_ref.shape[1]
-    for k in range(out_ref.shape[0]):
-        out_ref[k, :, :] = total[k * size : (k + 1) * size, :]
-
-
-def copy_rows(rec_ref, out_ref):
+            after = totals_at(zrec_ref, k, size)[branch] * entry + zrec_ref[k, 0:size, :]
+            entry = jnp.where(passed, after, entry)
+        put_entries(out_ref, branch, up, entry, rec_ref, rec_ref)
+
+
+def put_entries(out_ref, branch, up, entry, dec_ref, rec_ref):
     n = rec_ref.shape[0]
-    size = rec_ref.shape[1]
-    for k in range(n):
-        part = rec_ref[k, :, :]
-        for i in range(out_ref.shape[0]):
-            out_ref[i, k * size : (k + 1) * size, :] = part
+    size = WIDTH // n
+    for i in list(range(n)) if up else list(range(n))[::-1]:
+        out_ref[i, branch * size : (branch + 1) * size, :] = entry
+        entry = totals_at(dec_ref, i, 2 * size)[branch] * entry + sliced(rec_ref, i, size)[branch]
+
+
+def totals_down(dec_ref, rec_ref, out_ref):
+    n, n_g = rec_ref.shape[0], out_ref.shape[0]
+    size = WIDTH // n
+    sums, _ = group_sums(dec_ref, rec_ref, False)
+    both = jnp.concatenate(sums, axis=0)
+    weight = rec_ref[0, 2 * size :, :]
+    for i in range(1, n):
+        weight = weight + rec_ref[i, 2 * size :, :]
+    span, part = 2 * size // n_g, weight.shape[0] // n_g
+    for k in range(n_g):
+        out_ref[k, 0:span, :] = both[k * span : (k + 1) * span, :]
+        out_ref[k, span:, :] = weight[k * part : (k + 1) * part, :]
+
+
+def scan_down(place_ref, dec_ref, rec_ref, out_ref):
+    n_g = rec_ref.shape[0]
+    span = 2 * (dec_ref.shape[1] - 8) // n_g
+    forward = 2 * place_ref[0] < n_g
+    states = [rec_ref[k, 0:span, :] for k in range(n_g)]
+    decays = [totals_at(dec_ref, k, dec_ref.shape[1] - 8) for k in range(n_g)]
+    down, acc = [None] * n_g, jnp.zeros_like(states[0])
+    for k in range(n_g)[::-1]:
+        down[k] = acc
+        acc = decays[k][0] * acc + states[k]
+    up, acc = [None] * n_g, jnp.zeros_like(states[0])
+    for k in range(n_g):
+        up[k] = acc
+        acc = decays[k][1] * acc + states[k]
+    weight = rec_ref[0, span:, :]
+    for k in range(1, n_g):
+        weight = weight + rec_ref[k, span:, :]
+    for k in range(n_g):
+        out_ref[k, 0:span, :] = jnp.where(forward, down[k], up[k])
+        out_ref[k, span:, :] = weight
+
+
+def entries_down(back_ref, dec_ref, rec_ref, out_ref):
+    n_g, n = back_ref.shape[0], rec_ref.shape[0]
+    size = WIDTH // n
+    span = 2 * size // n_g
+    half = n_g // 2
+    entry_f = jnp.concatenate([back_ref[k, 0:span, :] for k in range(half)], axis=0)
+    entry_b = jnp.concatenate([back_ref[k, 0:span, :] for k in range(half, n_g)], axis=0)
+    put_entries(out_ref, 0, False, entry_f, dec_ref, rec_ref)
+    put_entries(out_ref, 1, True, entry_b, dec_ref, rec_ref)
+    part = back_ref.shape[1] - span
+    for k in range(n_g):
+        weight = back_ref[k, span:, :]
+        for i in range(n):
+            out_ref[i, 2 * size + k * part : 2 * size + (k + 1) * part, :] = weight
 
 
 def weight_rows(rec_ref, gw_ref):
-    for j in range(HEADS):
+    n = rec_ref.shape[0]
+    size = WIDTH // n
+    for i in range(n):
         for block in range(gw_ref.shape[1] // LANES):
-            gw_ref[j * 64 : (j + 1) * 64, block * LANES : (block + 1) * LANES] = (
-                rec_ref[j, block * 64 : (block + 1) * 64, :] * WEIGHT_SCALE
+            at = 2 * size + block * size
+            gw_ref[i * size : (i + 1) * size, block * LANES : (block + 1) * LANES] = (
+                rec_ref[i, at : at + size, :] * WEIGHT_SCALE
             )
 
 
@@ -214,34 +266,35 @@
     return jnp.transpose(grid)[0:8, :]
 
 
-def outputs(
-    skip_ref, x_ref, z_ref, b_ref, c_ref, df_ref, db_ref, gain_ref, w_ref, do_ref, ent_ref,
-    y_ref, m_ref, sums_ref,
+def near_outputs(
+    skip_ref, x_ref, b_ref, c_ref, df_ref, db_ref, gain_ref, w_ref, do_ref, y_ref, m_ref
 ):
     df, db = df_ref[...], db_ref[...]
     cf, be, end_f, end_b = columns(df, db)
     cf_row, be_row = rows(df, db)
     row, col = places()
-    c = c_ref[...]
-    scores = dot(c, b_ref[...], 1, 1)
-    entry_f, entry_b = take_slices(ent_ref)
-    far = spread(jnp.exp(cf)) * dot_right(c, entry_f, 1, 1)
-    far = far + spread(jnp.exp(end_b - be)) * dot_right(c, entry_b, 1, 1)
-    near = []
+    scores = dot(c_ref[...], b_ref[...], 1, 1)
     lane = lax.broadcasted_iota(jnp.int32, (1, LANES), 1)
     for g in range(HEADS // 2):
-        pair = x_ref[:, g * LANES : (g + 1) * LANES]
+        at = slice(g * LANES, (g + 1) * LANES)
+        pair = x_ref[:, at]
         acc = jnp.where(lane < HEAD_DIM, skip_ref[2 * g], skip_ref[2 * g + 1]) * pair.astype(F32)
         for hh in range(2):
             weights = scores * pair_decay(2 * g + hh, cf, be, cf_row, be_row, row, col)
             acc = acc + dot_left(weights, own_lanes(pair, hh), 1, 0)
-        near.append(acc)
-    y = far + jnp.concatenate(near, axis=1)
-    z = z_ref[...].astype(F32)
+        y_ref[:, at] = acc
+    m_ref[...] = dot(do_ref[...], w_ref[...], 1, 1) * gain_ref[...]
+
+
+def outputs(near_ref, m_ref, z_ref, c_ref, df_ref, db_ref, ent_ref, y_ref, sums_ref):
+    cf, be, end_f, end_b = columns(df_ref[...], db_ref[...])
+    c = c_ref[...]
+    entry_f, entry_b = take_slices(ent_ref)
+    y = near_ref[...] + spread(jnp.exp(cf)) * dot_right(c, entry_f, 1, 1)
+    y = y + spread(jnp.exp(end_b - be)) * dot_right(c, entry_b, 1, 1)
+    y_ref[...] = y
+    z, m = z_ref[...].astype(F32), m_ref[...]
     u = y * z * jax.nn.sigmoid(z)
-    m = dot(do_ref[...], w_ref[...], 1, 1) * gain_ref[...]
-    y_ref[...] = y
-    m_ref[...] = m
     sums = across_rows([jnp.sum(u * u, axis=1, keepdims=True), jnp.sum(u * m, axis=1, keepdims=True)])
     for i in range(sums_ref.shape[0]):
         sums_ref[i, :, :] = sums
@@ -249,7 +302,7 @@
 
 def gradients(
     sums_ref, y_ref, m_ref, z_ref, c_ref, df_ref, db_ref, gain_ref, do_ref,
-    dy_ref, gz_ref, out_ref, w_ref, *, inner,
+    dy_ref, gz_ref, out_ref, *, inner,
 ):
     total = sums_ref[0, :, :]
     for i in range(1, sums_ref.shape[0]):
@@ -273,26 +326,26 @@
     back_b = dot_left(dy * spread(jnp.exp(end_b - be)), c, 0, 0)
     put_slices(out_ref, back_f, back_b)
     weight = dot(normed, do_ref[...], 0, 0)
-    for j in range(HEADS):
+    n = out_ref.shape[0]
+    size = WIDTH // n
+    for i in range(n):
         for block in range(weight.shape[1] // LANES):
-            w_ref[j, block * 64 : (block + 1) * 64, :] = weight[
-                j * 64 : (j + 1) * 64, block * LANES : (block + 1) * LANES
+            at = 2 * size + block * size
+            out_ref[i, at : at + size, :] = weight[
+                i * size : (i + 1) * size, block * LANES : (block + 1) * LANES
             ]
 
 
-def finish(
-    skip_ref, x_ref, b_ref, c_ref, df_ref, db_ref, dy_ref, ent_ref, exit_ref,
-    gx_ref, out_ref,
+def near_gradients(
+    skip_ref, x_ref, b_ref, c_ref, df_ref, db_ref, dy_ref, ent_ref, gx_ref, gb_ref, gc_ref
 ):
     df, db = df_ref[...], db_ref[...]
     cf, be, end_f, end_b = columns(df, db)
     cf_row, be_row = rows(df, db)
     row, col = places()
     b, c, dy = b_ref[...], c_ref[...], dy_ref[...]
-    x = x_ref[...].astype(F32)
     scores = dot(c, b, 1, 1)
     pair_sum = jnp.zeros((FRAMES, FRAMES), F32)
-    near = []
     lane = lax.broadcasted_iota(jnp.int32, (1, LANES), 1)
     for g in range(HEADS // 2):
         at = slice(g * LANES, (g + 1) * LANES)
@@ -302,18 +355,23 @@
             dy_own = own_lanes(dy[:, at], hh)
             pair_sum = pair_sum + decay * dot_left(dy_own, x_ref[:, at], 1, 1)
             acc = acc + dot_both(scores * decay, dy_own, 0, 0)
-        near.append(acc)
+        gx_ref[:, at] = acc
+    entry_f, entry_b = take_slices(ent_ref)
     rise_f, rise_b = spread(jnp.exp(cf)), spread(jnp.exp(end_b - be))
+    grad_c = dot_left(pair_sum, b, 1, 0)
+    gc_ref[...] = grad_c + dot_both(dy * rise_f, entry_f, 1, 0) + dot_both(dy * rise_b, entry_b, 1, 0)
+    gb_ref[...] = dot_left(pair_sum, c, 0, 0)
+
+
+def finish(x_ref, b_ref, df_ref, db_ref, exit_ref, gx_near, gb_near, gc_near, gx_ref, out_ref):
+    cf, be, end_f, end_b = columns(df_ref[...], db_ref[...])
+    b, x = b_ref[...], x_ref[...].astype(F32)
     tail_f, lead_b = spread(jnp.exp(end_f - cf)), spread(jnp.exp(be))
-    entry_f, entry_b = take_slices(ent_ref)
     exit_f, exit_b = take_slices(exit_ref)
-    gx = jnp.concatenate(near, axis=1)
-    gx = gx + tail_f * dot_right(b, exit_f, 1, 1) + lead_b * dot_right(b, exit_b, 1, 1)
+    gx = gx_near[...] + tail_f * dot_right(b, exit_f, 1, 1) + lead_b * dot_right(b, exit_b, 1, 1)
     gx_ref[...] = gx.astype(BF16)
-    grad_c = dot_left(pair_sum, b, 1, 0)
-    grad_c = grad_c + dot_both(dy * rise_f, entry_f, 1, 0) + dot_both(dy * rise_b, entry_b, 1, 0)
-    grad_b = dot_left(pair_sum, c, 0, 0)
-    grad_b = grad_b + dot_both(x * tail_f, exit_f, 1, 0) + dot_both(x * lead_b, exit_b, 1, 0)
+    grad_b = gb_near[...] + dot_both(x * tail_f, exit_f, 1, 0) + dot_both(x * lead_b, exit_b, 1, 0)
+    grad_c = gc_near[...]
     n = out_ref.shape[0]
     size = FRAMES // n
     for i in range(n):
@@ -340,17 +398,19 @@
 
 VMEM = pl.BlockSpec(memory_space=pltpu.VMEM)
 SMEM = pl.BlockSpec(memory_space=pltpu.SMEM)
-
-
-def call(kernel, name, out, *args, scalars=0):
+HBM = pl.BlockSpec(memory_space=pltpu.MemorySpace.HBM)
+
+
+def call(kernel, name, out, *args, scalars=0, own=()):
     shapes = [jax.ShapeDtypeStruct(shape, dtype) for shape, dtype in out]
     single = len(shapes) == 1
     return pl.pallas_call(
         kernel,
         name=name,
         out_shape=shapes[0] if single else tuple(shapes),
-        in_specs=[SMEM] * scalars + [VMEM] * (len(args) - scalars),
+        in_specs=[SMEM] * scalars + [HBM if own else VMEM] * (len(args) - scalars),
         out_specs=VMEM if single else tuple(VMEM for _ in shapes),
+        scratch_shapes=list(own),
         compiler_params=pltpu.CompilerParams(vmem_limit_bytes=48 * 1024 * 1024),
     )(*args)
 
@@ -361,57 +421,58 @@
 
 def body(x_in, gate_in, b_in, c_in, decay_fwd, decay_bwd, skip_gain, norm_gain, w_out, d_out):
     n_hi, n_lo, n_x, n_h = (lax.axis_size(axis) for axis in ("z_hi", "z_lo", "x", "head"))
-    group, along = ("z_lo", "x"), ("z_hi", "z_lo")
-    n, n_z = n_lo * n_x, n_hi * n_lo
+    group = ("z_lo", "x")
+    n = n_lo * n_x
+    model = d_out.shape[1]
     gain = norm_gain.reshape(1, WIDTH)
-    state = 2 * WIDTH // n
+    size = WIDTH // n
+    weights = size * model // LANES
     place = lax.axis_index("z_hi").astype(jnp.int32).reshape(1)
-
-    sent = call(local_states, "local_states", [((n, state + 8, LANES), F32)], x_in, b_in, decay_fwd, decay_bwd)
+    decays = (decay_fwd, decay_bwd)
+    square = (FRAMES, WIDTH)
+
+    firsts = (x_in, b_in, *decays)
+    own = [pltpu.VMEM(a.shape, a.dtype) for a in firsts] + [pltpu.SemaphoreType.DMA((4,))]
+    sent = call(local_states, "local_states", [((n, 2 * size + 8, LANES), F32)], *firsts, own=own)
     rec1 = exchange(sent, group)
-    up = functools.partial(group_totals, forward_up=True)
-    sent = call(up, "totals_up", [((n_hi, state + 8, LANES), F32)], rec1, rec1)
+    near, m = call(
+        near_outputs, "near_outputs", [(square, F32)] * 2,
+        skip_gain, x_in, b_in, c_in, *decays, gain, w_out, d_out, scalars=1,
+    )
+    sent = call(totals_up, "totals_up", [((n_hi, size + 8, LANES), F32)], place, rec1, scalars=1)
     recz1 = exchange(sent, "z_hi")
-    up = functools.partial(group_entries, forward_up=True)
-    sent = call(up, "entries_up", [((n, state, LANES), F32)], place, recz1, recz1, rec1, rec1, scalars=1)
+    sent = call(entries_up, "entries_up", [((n, 2 * size, LANES), F32)], place, recz1, rec1, scalars=1)
     entries = exchange(sent, group)
 
-    y, m, sums = call(
-        outputs, "outputs",
-        [((FRAMES, WIDTH), F32), ((FRAMES, WIDTH), F32), ((n_h, 8, LANES), F32)],
-        skip_gain, x_in, gate_in, b_in, c_in, decay_fwd, decay_bwd, gain, w_out, d_out, entries,
-        scalars=1,
+    y, sums = call(
+        outputs, "outputs", [(square, F32), ((n_h, 8, LANES), F32)],
+        near, m, gate_in, c_in, *decays, entries,
     )
     sums = exchange(sums, "head")
-    dy, grad_z, sent, weight = call(
+    dy, grad_z, sent = call(
         functools.partial(gradients, inner=WIDTH * n_h), "gradients",
-        [((FRAMES, WIDTH), F32), ((FRAMES, WIDTH), BF16), ((n, state, LANES), F32), ((n_x, 512, LANES), F32)],
-        sums, y, m, gate_in, c_in, decay_fwd, decay_bwd, gain, d_out,
+        [(square, F32), (square, BF16), ((n, 2 * size + weights, LANES), F32)],
+        sums, y, m, gate_in, c_in, *decays, gain, d_out,
     )
 
     rec2 = exchange(sent, group)
-    down = functools.partial(group_totals, forward_up=False)
-    sent = call(down, "totals_down", [((n_hi, state, LANES), F32)], rec1, rec2)
+    gx_near, gb_near, gc_near = call(
+        near_gradients, "near_gradients", [(square, F32)] + [((FRAMES, STATE), F32)] * 2,
+        skip_gain, x_in, b_in, c_in, *decays, dy, entries, scalars=1,
+    )
+    rows_z = (2 * size + weights) // n_hi
+    sent = call(totals_down, "totals_down", [((n_hi, rows_z, LANES), F32)], rec1, rec2)
     recz2 = exchange(sent, "z_hi")
-    down = functools.partial(group_entries, forward_up=False)
-    sent = call(down, "entries_down", [((n, state, LANES), F32)], place, recz1, recz2, rec1, rec2, scalars=1)
+    sent = call(scan_down, "scan_down", [((n_hi, rows_z, LANES), F32)], place, recz1, recz2, scalars=1)
+    back = exchange(sent, "z_hi")
+    sent = call(entries_down, "entries_down", [((n, 2 * size + weights, LANES), F32)], back, rec1, rec2)
     exits = exchange(sent, group)
-
-    weight = exchange(weight, "x")
-    weight = call(add_rows, "weight_x", [((n_z, 512 // n_z, LANES), F32)], weight)
-    weight = exchange(weight, along)
-    weight = call(add_up, "weight_z", [((n_z, 512 // n_z, LANES), F32)], weight)
-    weight = exchange(weight, along)
-    weight = call(copy_rows, "weight_copy", [((n_x, 512, LANES), F32)], weight)
-    weight = exchange(weight, "x")
-    grad_w = call(weight_rows, "weight_rows", [((WIDTH, d_out.shape[1]), F32)], weight)
+    grad_w = call(weight_rows, "weight_rows", [((WIDTH, model), F32)], exits)
 
     chunk = 2 * FRAMES // n_h
     grad_x, sent = call(
-        finish, "finish",
-        [((FRAMES, WIDTH), BF16), ((n_h, chunk, LANES), F32)],
-        skip_gain, x_in, b_in, c_in, decay_fwd, decay_bwd, dy, entries, exits,
-        scalars=1,
+        finish, "finish", [(square, BF16), ((n_h, chunk, LANES), F32)],
+        x_in, b_in, *decays, exits, gx_near, gb_near, gc_near,
     )
     rec = exchange(sent, "head")
     sent = call(add_up, "add_up", [((n_h, chunk, LANES), F32)], rec)
@@ -423,7 +484,7 @@
 def solution(mesh):
     n_seq, n_head = mesh.devices.shape
     n_z = n_seq // HEADS
-    n_lo = min(4, n_z // 2)
+    n_lo = min(2, n_z // 2)
     split = Mesh(mesh.devices.reshape(n_z // n_lo, n_lo, HEADS, n_head), ("z_hi", "z_lo", "x", "head"))
     seq = ("z_hi", "z_lo", "x")
     in_specs = (

time: 225 us -> 174 us (0.77)
  waiting for transfers between devices: 76.4 us -> 24.6 us
  blocking collectives: 72.2 us -> 111 us
  starting transfers between devices: 53.5 us -> 17.7 us
    all_to_all x8 -> x4, waiting for transfers between devices: 76.4 us -> 24.6 us  [exchange(): return lax.all_to_all(a, axis, 0, 0, tiled=True)]
    all_to_all x5 -> x6, blocking collectives: 72.2 us -> 111 us  [exchange(): return lax.all_to_all(a, axis, 0, 0, tiled=True)]
    all_to_all x8 -> x4, starting transfers between devices: 53.5 us -> 17.7 us  [exchange(): return lax.all_to_all(a, axis, 0, 0, tiled=True)]
  transfers between devices with their start and end apart: 8 -> 4, of which waited for: 8 -> 4; matrix products, arithmetic and copies ran while one was open for 0% -> 0% of each run, Pallas kernels for 4% -> 4%
where the time goes in v3:
time: 174 us; the launch traced here: 173 us
  blocking collectives  111 us (64%)
  waiting for transfers between devices  24.6 us (14%)
  starting transfers between devices  17.7 us (10%)
  Pallas kernels  15.9 us (9%)
  local copies, waits for them, and re-layouts  3.17 us (2%)
    all_to_all x6, blocking collectives, exchange(): return lax.all_to_all(a, axis, 0, 0, tiled=True)  111 us
    all_to_all x4, waiting for transfers between devices, exchange(): return lax.all_to_all(a, axis, 0, 0, tiled=True)  24.6 us
    all_to_all x4, starting transfers between devices, exchange(): return lax.all_to_all(a, axis, 0, 0, tiled=True)  17.7 us
    pallas_call x14, Pallas kernels, call(): pl.pallas_call(kernel, name=name, out_shape=shapes[0] if single else tupl...  15.9 us
  transfers between devices with their start and end apart: 4, of which 4 were waited for; matrix products, arithmetic and copies ran while one was open for 0% of the time, Pallas kernels for 4%

profile of v3, /device:TPU:1, one launch (start us, length us, event | category | flops | bytes accessed | tf_op | source)
XLA Modules:
  0.0 173.0 jit_solution(10102319143520484178)
XLA Ops:
  0.6 0.9 copy-done.1
  1.5 0.8 copy-done.3
  2.4 0.7 copy-done.8
  3.1 0.7 copy-done.10
  3.8 2.2 %local_states.1 = f32[8,72,128]{2,1,0:T(8,128)} custom-call(bf16[256,256]{1,0:T(8,128)(2,1)S(1)} %copy-done.1, bf16[256,128]{1,0:T(8,128)(2,1)S(1)} %copy-done.3, f32[4,256]{1,0:T(4,128)S(1)} %copy-done.8, f32[4,256]{1,0:T(4,128)S(1)} %copy-done.10), custom_call_target="tpu_custom_call" | custom-call | tf_op jit(solution)/shard_map/local_states/pallas_call | solution.py:407
  6.0 0.0 copy-start
  6.0 0.0 copy-start.2
  6.1 6.3 %all-to-all-start = ((f32[8,72,128]{2,1,0:T(8,128)}), f32[8,72,128]{2,1,0:T(8,128)S(1)}, u32[]{:S(2)}, u32[]{:S(2)}) async-start(f32[8,72,128]{2,1,0:T(8,128)} %local_states.1), calls=%async_computation | async-start | bytes 589824 | tf_op jit(solution)/shard_map/all_to_all | solution.py:419
  12.4 6.2 %all-to-all-done.rec_ref.dec_ref = f32[8,72,128]{2,1,0:T(8,128)S(1)} async-done(((f32[8,72,128]{2,1,0:T(8,128)}), f32[8,72,128]{2,1,0:T(8,128)S(1)}, u32[]{:S(2)}, u32[]{:S(2)}) %all-to-all-start) | async-done | bytes 294944 | tf_op jit(solution)/shard_map/all_to_all | solution.py:419
  18.7 28.0 %all_to_all.50.zrec_ref.dec_ref = f32[8,40,128]{2,1,0:T(8,128)S(1)} all-to-all(f32[8,40,128]{2,1,0:T(8,128)S(1)} %totals_up.1), channel_id=1, replica_groups=mesh['z_hi'=8,'z_lo'=2,'x'=4,'head'=8] {'z_hi'}, dimensions={0} | all-to-all | bytes 327680 | tf_op jit(solution)/shard_map/all_to_all | solution.py:419
  46.7 0.8 entries_up.1
  47.4 3.4 %all-to-all-start.2 = ((f32[8,64,128]{2,1,0:T(8,128)}), f32[8,64,128]{2,1,0:T(8,128)S(1)}, u32[]{:S(2)}, u32[]{:S(2)}) async-start(f32[8,64,128]{2,1,0:T(8,128)} %entries_up.1), calls=%async_computation.2 | async-start | bytes 524288 | tf_op jit(solution)/shard_map/all_to_all | solution.py:419
  51.0 2.1 %near_outputs.1 = (f32[256,256]{1,0:T(8,128)S(1)}, f32[256,256]{1,0:T(8,128)S(1)}) custom-call(f32[4]{0:T(128)S(1)} %copy-done.13, bf16[256,256]{1,0:T(8,128)(2,1)S(1)} %copy-done.2, bf16[256,128]{1,0:T(8,128)(2,1)S(1)} %copy-done.4, bf16[256,128]{1,0:T(8,128)(2,1)S(1)} %copy-done.5, f32[4,256]{1,0:T(4,128)S(1)} %copy-done.9, f32[4,256]{1,0:T(4,128)S(1)} %copy-done.11, ...), custom_call_target="tpu_custom_call" | custom-call | tf_op jit(solution)/shard_map/near_outputs/pallas_call | solution.py:407
  53.1 3.8 %all-to-all-done.2.ent_ref = f32[8,64,128]{2,1,0:T(8,128)S(1)} async-done(((f32[8,64,128]{2,1,0:T(8,128)}), f32[8,64,128]{2,1,0:T(8,128)S(1)}, u32[]{:S(2)}, u32[]{:S(2)}) %all-to-all-start.2) | async-done | bytes 262176 | tf_op jit(solution)/shard_map/all_to_all | solution.py:419
  56.9 1.0 outputs.1
  57.9 13.7 %all_to_all.51.sums_ref = f32[8,8,128]{2,1,0:T(8,128)S(1)} all-to-all(f32[8,8,128]{2,1,0:T(8,128)S(1)} %get-tuple-element.21), channel_id=1, replica_groups=mesh['z_hi'=8,'z_lo'=2,'x'=4,'head'=8] {'head'}, dimensions={0} | all-to-all | bytes 65536 | tf_op jit(solution)/shard_map/all_to_all | solution.py:419
  71.6 1.4 gradients.1
  73.0 19.6 %all_to_all.52.rec_ref = f32[8,320,128]{2,1,0:T(8,128)S(1)} all-to-all(f32[8,320,128]{2,1,0:T(8,128)S(1)} %get-tuple-element.23), channel_id=1, replica_groups=mesh['z_hi'=8,'z_lo'=2,'x'=4,'head'=8] {'z_lo','x'}, dimensions={0} | all-to-all | bytes 2621440 | tf_op jit(solution)/shard_map/all_to_all | solution.py:419
  92.6 0.1 totals_down.1
  92.7 17.6 %all_to_all.53.rec_ref = f32[8,40,128]{2,1,0:T(8,128)S(1)} all-to-all(f32[8,40,128]{2,1,0:T(8,128)S(1)} %totals_down.1), channel_id=1, replica_groups=mesh['z_hi'=8,'z_lo'=2,'x'=4,'head'=8] {'z_hi'}, dimensions={0} | all-to-all | bytes 327680 | tf_op jit(solution)/shard_map/all_to_all | solution.py:419
  110.3 16.6 %all_to_all.54.back_ref = f32[8,40,128]{2,1,0:T(8,128)S(1)} all-to-all(f32[8,40,128]{2,1,0:T(8,128)S(1)} %scan_down.1), channel_id=1, replica_groups=mesh['z_hi'=8,'z_lo'=2,'x'=4,'head'=8] {'z_hi'}, dimensions={0} | all-to-all | bytes 327680 | tf_op jit(solution)/shard_map/all_to_all | solution.py:419
  126.9 1.2 entries_down.1
  128.1 3.6 %all-to-all-start.7 = ((f32[8,320,128]{2,1,0:T(8,128)}), f32[8,320,128]{2,1,0:T(8,128)S(1)}, u32[]{:S(2)}, u32[]{:S(2)}) async-start(f32[8,320,128]{2,1,0:T(8,128)} %entries_down.1), calls=%async_computation.7 | async-start | bytes 2621440 | tf_op jit(solution)/shard_map/all_to_all | solution.py:419
  131.7 3.0 %near_gradients.1 = (f32[256,256]{1,0:T(8,128)S(1)}, f32[256,128]{1,0:T(8,128)S(1)}, f32[256,128]{1,0:T(8,128)S(1)}) custom-call(f32[4]{0:T(128)S(1)} %copy-done.13, bf16[256,256]{1,0:T(8,128)(2,1)S(1)} %copy-done.2, bf16[256,128]{1,0:T(8,128)(2,1)S(1)} %copy-done.4, bf16[256,128]{1,0:T(8,128)(2,1)S(1)} %copy-done.5, f32[4,256]{1,0:T(4,128)S(1)} %copy-done.9, ...), custom_call_target="tpu_custom_call" | custom-call | tf_op jit(solution)/shard_map/near_gradients/pallas_call | solution.py:407
  134.7 9.1 %all-to-all-done.7.exit_ref.rec_ref = f32[8,320,128]{2,1,0:T(8,128)S(1)} async-done(((f32[8,320,128]{2,1,0:T(8,128)}), f32[8,320,128]{2,1,0:T(8,128)S(1)}, u32[]{:S(2)}, u32[]{:S(2)}) %all-to-all-start.7) | async-done | bytes 1310752 | tf_op jit(solution)/shard_map/all_to_all | solution.py:419
  143.8 1.6 finish.1
  145.4 15.3 %all_to_all.55.rec_ref = f32[8,64,128]{2,1,0:T(8,128)S(1)} all-to-all(f32[8,64,128]{2,1,0:T(8,128)S(1)} %get-tuple-element.30), channel_id=1, replica_groups=mesh['z_hi'=8,'z_lo'=2,'x'=4,'head'=8] {'head'}, dimensions={0} | all-to-all | bytes 524288 | tf_op jit(solution)/shard_map/all_to_all | solution.py:419
  160.7 0.7 add_up.1
  161.4 4.4 %all-to-all-start.9 = ((f32[8,64,128]{2,1,0:T(8,128)}), f32[8,64,128]{2,1,0:T(8,128)S(1)}, u32[]{:S(2)}, u32[]{:S(2)}) async-start(f32[8,64,128]{2,1,0:T(8,128)} %add_up.1), calls=%async_computation.9 | async-start | bytes 524288 | tf_op jit(solution)/shard_map/all_to_all | solution.py:419
  165.8 1.0 weight_rows.1
  166.8 5.5 %all-to-all-done.9.rec_ref = f32[8,64,128]{2,1,0:T(8,128)S(1)} async-done(((f32[8,64,128]{2,1,0:T(8,128)}), f32[8,64,128]{2,1,0:T(8,128)S(1)}, u32[]{:S(2)}, u32[]{:S(2)}) %all-to-all-start.9) | async-done | bytes 262176 | tf_op jit(solution)/shard_map/all_to_all | solution.py:419
  172.3 0.7 deal_out.1
  (24 shorter events, 0.1 us)
Async XLA Ops:
  0.6 0.9 copy-start.1
  1.5 0.8 copy-start.3
  2.4 0.7 copy-start.8
  3.1 0.7 copy-start.10
  6.0 44.9 %copy-start = (bf16[256,1024]{1,0:T(8,128)(2,1)S(1)}, bf16[256,1024]{1,0:T(8,128)(2,1)}, u32[]{:S(2)}) copy-start(bf16[256,1024]{1,0:T(8,128)(2,1)} %do_ref.3) | copy-start | bytes 1572868
  6.0 44.9 %copy-start.2 = (bf16[256,256]{1,0:T(8,128)(2,1)S(1)}, bf16[256,256]{1,0:T(8,128)(2,1)}, u32[]{:S(2)}) copy-start(bf16[256,256]{1,0:T(8,128)(2,1)} %x_ref.5) | copy-start | bytes 393220
  6.0 44.9 %copy-start.4 = (bf16[256,128]{1,0:T(8,128)(2,1)S(1)}, bf16[256,128]{1,0:T(8,128)(2,1)}, u32[]{:S(2)}) copy-start(bf16[256,128]{1,0:T(8,128)(2,1)} %b_ref.5) | copy-start | bytes 196612
  6.0 44.9 %copy-start.5 = (bf16[256,128]{1,0:T(8,128)(2,1)S(1)}, bf16[256,128]{1,0:T(8,128)(2,1)}, u32[]{:S(2)}) copy-start(bf16[256,128]{1,0:T(8,128)(2,1)} %c_ref.7) | copy-start | bytes 196612
  6.0 44.9 %copy-start.7 = (bf16[256,1024]{1,0:T(8,128)(2,1)S(1)}, bf16[256,1024]{1,0:T(8,128)(2,1)}, u32[]{:S(2)}) copy-start(bf16[256,1024]{1,0:T(8,128)(2,1)} %w_ref.1) | copy-start | bytes 1572868
  6.0 44.9 %copy-start.9 = (f32[4,256]{1,0:T(4,128)S(1)}, f32[4,256]{1,0:T(4,128)}, u32[]{:S(2)}) copy-start(f32[4,256]{1,0:T(4,128)} %df_ref.9) | copy-start | bytes 12292
  6.1 44.9 %copy-start.11 = (f32[4,256]{1,0:T(4,128)S(1)}, f32[4,256]{1,0:T(4,128)}, u32[]{:S(2)}) copy-start(f32[4,256]{1,0:T(4,128)} %db_ref.9) | copy-start | bytes 12292
  6.1 44.9 %copy-start.12 = (f32[256]{0:T(256)S(1)}, f32[256]{0:T(256)}, u32[]{:S(2)}) copy-start(f32[256]{0:T(256)} %param.17) | copy-start | bytes 3076
  6.1 44.9 %copy-start.13 = (f32[4]{0:T(128)S(1)}, f32[4]{0:T(128)}, u32[]{:S(2)}) copy-start(f32[4]{0:T(128)} %skip_ref.3) | copy-start | bytes 52
  6.1 12.6 %all-to-all-start = ((f32[8,72,128]{2,1,0:T(8,128)}), f32[8,72,128]{2,1,0:T(8,128)S(1)}, u32[]{:S(2)}, u32[]{:S(2)}) async-start(f32[8,72,128]{2,1,0:T(8,128)} %local_states.1), calls=%async_computation | async-start | bytes 589824 | tf_op jit(solution)/shard_map/all_to_all | solution.py:419
  46.7 10.2 %copy-start.6 = (bf16[256,256]{1,0:T(8,128)(2,1)S(1)}, bf16[256,256]{1,0:T(8,128)(2,1)}, u32[]{:S(2)}) copy-start(bf16[256,256]{1,0:T(8,128)(2,1)} %z_ref.3) | copy-start | bytes 393220
  47.4 9.4 %all-to-all-start.2 = ((f32[8,64,128]{2,1,0:T(8,128)}), f32[8,64,128]{2,1,0:T(8,128)S(1)}, u32[]{:S(2)}, u32[]{:S(2)}) async-start(f32[8,64,128]{2,1,0:T(8,128)} %entries_up.1), calls=%async_computation.2 | async-start | bytes 524288 | tf_op jit(solution)/shard_map/all_to_all | solution.py:419
  128.1 15.7 %all-to-all-start.7 = ((f32[8,320,128]{2,1,0:T(8,128)}), f32[8,320,128]{2,1,0:T(8,128)S(1)}, u32[]{:S(2)}, u32[]{:S(2)}) async-start(f32[8,320,128]{2,1,0:T(8,128)} %entries_down.1), calls=%async_computation.7 | async-start | bytes 2621440 | tf_op jit(solution)/shard_map/all_to_all | solution.py:419
  161.4 10.9 %all-to-all-start.9 = ((f32[8,64,128]{2,1,0:T(8,128)}), f32[8,64,128]{2,1,0:T(8,128)S(1)}, u32[]{:S(2)}, u32[]{:S(2)}) async-start(f32[8,64,128]{2,1,0:T(8,128)} %add_up.1), calls=%async_computation.9 | async-start | bytes 524288 | tf_op jit(solution)/shard_map/all_to_all | solution.py:419

commit v4 on v3

--- a/solution.py
+++ b/solution.py
@@ -302,7 +302,7 @@
 
 def gradients(
     sums_ref, y_ref, m_ref, z_ref, c_ref, df_ref, db_ref, gain_ref, do_ref,
-    dy_ref, gz_ref, out_ref, *, inner,
+    dy_ref, du_ref, out_ref, *, inner,
 ):
     total = sums_ref[0, :, :]
     for i in range(1, sums_ref.shape[0]):
@@ -318,8 +318,8 @@
     normed = (u * q * gain_ref[...]).astype(BF16)
     du = q * m - u * (q * q * q * cross)
     dy = du * silu
-    gz_ref[...] = (du * y * sig * (1.0 + z * (1.0 - sig))).astype(BF16)
     dy_ref[...] = dy
+    du_ref[...] = du
     cf, be, end_f, end_b = columns(df_ref[...], db_ref[...])
     c = c_ref[...]
     back_f = dot_left(dy * spread(jnp.exp(cf)), c, 0, 0)
@@ -363,20 +363,32 @@
     gb_ref[...] = dot_left(pair_sum, c, 0, 0)
 
 
-def finish(x_ref, b_ref, df_ref, db_ref, exit_ref, gx_near, gb_near, gc_near, gx_ref, out_ref):
+def gate_gradient(du_ref, y_ref, z_ref, gz_ref):
+    z = z_ref[...].astype(F32)
+    sig = jax.nn.sigmoid(z)
+    gz_ref[...] = (du_ref[...] * y_ref[...] * sig * (1.0 + z * (1.0 - sig))).astype(BF16)
+
+
+def finish(x_ref, df_ref, db_ref, exit_ref, gb_near, gc_near, out_ref):
     cf, be, end_f, end_b = columns(df_ref[...], db_ref[...])
-    b, x = b_ref[...], x_ref[...].astype(F32)
-    tail_f, lead_b = spread(jnp.exp(end_f - cf)), spread(jnp.exp(be))
+    x = x_ref[...].astype(F32)
     exit_f, exit_b = take_slices(exit_ref)
-    gx = gx_near[...] + tail_f * dot_right(b, exit_f, 1, 1) + lead_b * dot_right(b, exit_b, 1, 1)
-    gx_ref[...] = gx.astype(BF16)
-    grad_b = gb_near[...] + dot_both(x * tail_f, exit_f, 1, 0) + dot_both(x * lead_b, exit_b, 1, 0)
+    grad_b = gb_near[...] + dot_both(x * spread(jnp.exp(end_f - cf)), exit_f, 1, 0)
+    grad_b = grad_b + dot_both(x * spread(jnp.exp(be)), exit_b, 1, 0)
     grad_c = gc_near[...]
     n = out_ref.shape[0]
     size = FRAMES // n
     for i in range(n):
         out_ref[i, 0:size, :] = grad_b[i * size : (i + 1) * size, :]
         out_ref[i, size : 2 * size, :] = grad_c[i * size : (i + 1) * size, :]
+
+
+def finish_x(b_ref, df_ref, db_ref, exit_ref, gx_near, gx_ref):
+    cf, be, end_f, end_b = columns(df_ref[...], db_ref[...])
+    b = b_ref[...]
+    exit_f, exit_b = take_slices(exit_ref)
+    gx = gx_near[...] + spread(jnp.exp(end_f - cf)) * dot_right(b, exit_f, 1, 1)
+    gx_ref[...] = (gx + spread(jnp.exp(be)) * dot_right(b, exit_b, 1, 1)).astype(BF16)
 
 
 def add_up(rec_ref, out_ref):
@@ -431,7 +443,7 @@
     decays = (decay_fwd, decay_bwd)
     square = (FRAMES, WIDTH)
 
-    firsts = (x_in, b_in, *decays)
+    firsts = tuple(pltpu.with_memory_space_constraint(a, pltpu.MemorySpace.HBM) for a in (x_in, b_in, *decays))
     own = [pltpu.VMEM(a.shape, a.dtype) for a in firsts] + [pltpu.SemaphoreType.DMA((4,))]
     sent = call(local_states, "local_states", [((n, 2 * size + 8, LANES), F32)], *firsts, own=own)
     rec1 = exchange(sent, group)
@@ -449,9 +461,9 @@
         near, m, gate_in, c_in, *decays, entries,
     )
     sums = exchange(sums, "head")
-    dy, grad_z, sent = call(
+    dy, du, sent = call(
         functools.partial(gradients, inner=WIDTH * n_h), "gradients",
-        [(square, F32), (square, BF16), ((n, 2 * size + weights, LANES), F32)],
+        [(square, F32), (square, F32), ((n, 2 * size + weights, LANES), F32)],
         sums, y, m, gate_in, c_in, *decays, gain, d_out,
     )
 
@@ -460,6 +472,7 @@
         near_gradients, "near_gradients", [(square, F32)] + [((FRAMES, STATE), F32)] * 2,
         skip_gain, x_in, b_in, c_in, *decays, dy, entries, scalars=1,
     )
+    grad_z = call(gate_gradient, "gate_gradient", [(square, BF16)], du, y, gate_in)
     rows_z = (2 * size + weights) // n_hi
     sent = call(totals_down, "totals_down", [((n_hi, rows_z, LANES), F32)], rec1, rec2)
     recz2 = exchange(sent, "z_hi")
@@ -470,10 +483,10 @@
     grad_w = call(weight_rows, "weight_rows", [((WIDTH, model), F32)], exits)
 
     chunk = 2 * FRAMES // n_h
-    grad_x, sent = call(
-        finish, "finish", [(square, BF16), ((n_h, chunk, LANES), F32)],
-        x_in, b_in, *decays, exits, gx_near, gb_near, gc_near,
-    )
+    sent = call(
+        finish, "finish", [((n_h, chunk, LANES), F32)], x_in, *decays, exits, gb_near, gc_near
+    )
+    grad_x = call(finish_x, "finish_x", [(square, BF16)], b_in, *decays, exits, gx_near)
     rec = exchange(sent, "head")
     sent = call(add_up, "add_up", [((n_h, chunk, LANES), F32)], rec)
     rec = exchange(sent, "head")

time: 174 us -> 171 us (0.983)
  local copies, waits for them, and re-layouts: 3.17 us -> 0.06 us
  Pallas kernels: 15.9 us -> 18.4 us
  waiting for transfers between devices: 24.6 us -> 22.3 us
    unnamed x28 -> x20, local copies, waits for them, and re-layouts: 3.17 us -> 0.06 us
    pallas_call x14 -> x16, Pallas kernels: 15.9 us -> 18.4 us  [call(): pl.pallas_call(kernel, name=name, out_shape=shapes[0] if single else tupl...]
    all_to_all x4, waiting for transfers between devices: 24.6 us -> 22.3 us  [exchange(): return lax.all_to_all(a, axis, 0, 0, tiled=True)]
  transfers between devices with their start and end apart: 4 -> 4, of which waited for: 4 -> 4; matrix products, arithmetic and copies ran while one was open for 0% -> 0% of each run, Pallas kernels for 4% -> 5%
where the time goes in v4:
time: 171 us; the launch traced here: 170 us
  blocking collectives  111 us (65%)
  waiting for transfers between devices  22.3 us (13%)
  Pallas kernels  18.4 us (11%)
  starting transfers between devices  17.7 us (10%)
    all_to_all x6, blocking collectives, exchange(): return lax.all_to_all(a, axis, 0, 0, tiled=True)  111 us
    all_to_all x4, waiting for transfers between devices, exchange(): return lax.all_to_all(a, axis, 0, 0, tiled=True)  22.3 us
    pallas_call x16, Pallas kernels, call(): pl.pallas_call(kernel, name=name, out_shape=shapes[0] if single else tupl...  18.4 us
    all_to_all x4, starting transfers between devices, exchange(): return lax.all_to_all(a, axis, 0, 0, tiled=True)  17.7 us
  transfers between devices with their start and end apart: 4, of which 4 were waited for; matrix products, arithmetic and copies ran while one was open for 0% of the time, Pallas kernels for 5%

profile of v4, /device:TPU:1, one launch (start us, length us, event | category | flops | bytes accessed | tf_op | source)
XLA Modules:
  0.0 170.1 jit_solution(7044138332208468153)
XLA Ops:
  0.6 2.9 %local_states.1 = f32[8,72,128]{2,1,0:T(8,128)} custom-call(bf16[256,256]{1,0:T(8,128)(2,1)} %x_ref.5, bf16[256,128]{1,0:T(8,128)(2,1)} %b_ref.5, f32[4,256]{1,0:T(4,128)} %df_ref.11, f32[4,256]{1,0:T(4,128)} %db_ref.11), custom_call_target="tpu_custom_call" | custom-call | tf_op jit(solution)/shard_map/local_states/pallas_call | solution.py:419
  3.6 0.0 copy-start.3
  3.6 0.0 copy-start.4
  3.6 0.0 copy-start.6
  3.6 0.0 copy-start.7
  3.6 6.3 %all-to-all-start = ((f32[8,72,128]{2,1,0:T(8,128)}), f32[8,72,128]{2,1,0:T(8,128)S(1)}, u32[]{:S(2)}, u32[]{:S(2)}) async-start(f32[8,72,128]{2,1,0:T(8,128)} %local_states.1), calls=%async_computation | async-start | bytes 589824 | tf_op jit(solution)/shard_map/all_to_all | solution.py:431
  10.0 6.2 %all-to-all-done.rec_ref.dec_ref = f32[8,72,128]{2,1,0:T(8,128)S(1)} async-done(((f32[8,72,128]{2,1,0:T(8,128)}), f32[8,72,128]{2,1,0:T(8,128)S(1)}, u32[]{:S(2)}, u32[]{:S(2)}) %all-to-all-start) | async-done | bytes 294944 | tf_op jit(solution)/shard_map/all_to_all | solution.py:431
  16.2 28.0 %all_to_all.50.zrec_ref.dec_ref = f32[8,40,128]{2,1,0:T(8,128)S(1)} all-to-all(f32[8,40,128]{2,1,0:T(8,128)S(1)} %totals_up.1), channel_id=1, replica_groups=mesh['z_hi'=8,'z_lo'=2,'x'=4,'head'=8] {'z_hi'}, dimensions={0} | all-to-all | bytes 327680 | tf_op jit(solution)/shard_map/all_to_all | solution.py:431
  44.2 0.8 entries_up.1
  45.0 3.4 %all-to-all-start.2 = ((f32[8,64,128]{2,1,0:T(8,128)}), f32[8,64,128]{2,1,0:T(8,128)S(1)}, u32[]{:S(2)}, u32[]{:S(2)}) async-start(f32[8,64,128]{2,1,0:T(8,128)} %entries_up.1), calls=%async_computation.2 | async-start | bytes 524288 | tf_op jit(solution)/shard_map/all_to_all | solution.py:431
  48.5 2.1 %near_outputs.1 = (f32[256,256]{1,0:T(8,128)S(1)}, f32[256,256]{1,0:T(8,128)S(1)}) custom-call(f32[4]{0:T(128)S(1)} %copy-done.9, bf16[256,256]{1,0:T(8,128)(2,1)S(1)} %copy-done.1, bf16[256,128]{1,0:T(8,128)(2,1)S(1)} %copy-done.3, bf16[256,128]{1,0:T(8,128)(2,1)S(1)} %copy-done.4, f32[4,256]{1,0:T(4,128)S(1)} %copy-done.6, f32[4,256]{1,0:T(4,128)S(1)} %copy-done.7, ...), custom_call_target="tpu_custom_call" | custom-call | tf_op jit(solution)/shard_map/near_outputs/pallas_call | solution.py:419
  50.6 3.8 %all-to-all-done.2.ent_ref = f32[8,64,128]{2,1,0:T(8,128)S(1)} async-done(((f32[8,64,128]{2,1,0:T(8,128)}), f32[8,64,128]{2,1,0:T(8,128)S(1)}, u32[]{:S(2)}, u32[]{:S(2)}) %all-to-all-start.2) | async-done | bytes 262176 | tf_op jit(solution)/shard_map/all_to_all | solution.py:431
  54.4 1.0 outputs.1
  55.4 13.7 %all_to_all.51.sums_ref = f32[8,8,128]{2,1,0:T(8,128)S(1)} all-to-all(f32[8,8,128]{2,1,0:T(8,128)S(1)} %get-tuple-element.19), channel_id=1, replica_groups=mesh['z_hi'=8,'z_lo'=2,'x'=4,'head'=8] {'head'}, dimensions={0} | all-to-all | bytes 65536 | tf_op jit(solution)/shard_map/all_to_all | solution.py:431
  69.2 1.4 gradients.1
  70.5 19.6 %all_to_all.52.rec_ref = f32[8,320,128]{2,1,0:T(8,128)S(1)} all-to-all(f32[8,320,128]{2,1,0:T(8,128)S(1)} %get-tuple-element.21), channel_id=1, replica_groups=mesh['z_hi'=8,'z_lo'=2,'x'=4,'head'=8] {'z_lo','x'}, dimensions={0} | all-to-all | bytes 2621440 | tf_op jit(solution)/shard_map/all_to_all | solution.py:431
  90.2 0.1 totals_down.1
  90.2 17.6 %all_to_all.53.rec_ref = f32[8,40,128]{2,1,0:T(8,128)S(1)} all-to-all(f32[8,40,128]{2,1,0:T(8,128)S(1)} %totals_down.1), channel_id=1, replica_groups=mesh['z_hi'=8,'z_lo'=2,'x'=4,'head'=8] {'z_hi'}, dimensions={0} | all-to-all | bytes 327680 | tf_op jit(solution)/shard_map/all_to_all | solution.py:431
  107.8 16.6 %all_to_all.54.back_ref = f32[8,40,128]{2,1,0:T(8,128)S(1)} all-to-all(f32[8,40,128]{2,1,0:T(8,128)S(1)} %scan_down.1), channel_id=1, replica_groups=mesh['z_hi'=8,'z_lo'=2,'x'=4,'head'=8] {'z_hi'}, dimensions={0} | all-to-all | bytes 327680 | tf_op jit(solution)/shard_map/all_to_all | solution.py:431
  124.5 1.2 entries_down.1
  125.6 3.6 %all-to-all-start.7 = ((f32[8,320,128]{2,1,0:T(8,128)}), f32[8,320,128]{2,1,0:T(8,128)S(1)}, u32[]{:S(2)}, u32[]{:S(2)}) async-start(f32[8,320,128]{2,1,0:T(8,128)} %entries_down.1), calls=%async_computation.7 | async-start | bytes 2621440 | tf_op jit(solution)/shard_map/all_to_all | solution.py:431
  129.2 3.0 %near_gradients.1 = (f32[256,256]{1,0:T(8,128)S(1)}, f32[256,128]{1,0:T(8,128)S(1)}, f32[256,128]{1,0:T(8,128)S(1)}) custom-call(f32[4]{0:T(128)S(1)} %copy-done.9, bf16[256,256]{1,0:T(8,128)(2,1)S(1)} %copy-done.1, bf16[256,128]{1,0:T(8,128)(2,1)S(1)} %copy-done.3, bf16[256,128]{1,0:T(8,128)(2,1)S(1)} %copy-done.4, f32[4,256]{1,0:T(4,128)S(1)} %copy-done.6, ...), custom_call_target="tpu_custom_call" | custom-call | tf_op jit(solution)/shard_map/near_gradients/pallas_call | solution.py:419
  132.2 9.1 %all-to-all-done.7.exit_ref.rec_ref = f32[8,320,128]{2,1,0:T(8,128)S(1)} async-done(((f32[8,320,128]{2,1,0:T(8,128)}), f32[8,320,128]{2,1,0:T(8,128)S(1)}, u32[]{:S(2)}, u32[]{:S(2)}) %all-to-all-start.7) | async-done | bytes 1310752 | tf_op jit(solution)/shard_map/all_to_all | solution.py:431
  141.3 1.2 finish.1
  142.5 15.3 %all_to_all.55.rec_ref = f32[8,64,128]{2,1,0:T(8,128)S(1)} all-to-all(f32[8,64,128]{2,1,0:T(8,128)S(1)} %finish.1), channel_id=1, replica_groups=mesh['z_hi'=8,'z_lo'=2,'x'=4,'head'=8] {'head'}, dimensions={0} | all-to-all | bytes 524288 | tf_op jit(solution)/shard_map/all_to_all | solution.py:431
  157.8 0.7 add_up.1
  158.5 4.4 %all-to-all-start.9 = ((f32[8,64,128]{2,1,0:T(8,128)}), f32[8,64,128]{2,1,0:T(8,128)S(1)}, u32[]{:S(2)}, u32[]{:S(2)}) async-start(f32[8,64,128]{2,1,0:T(8,128)} %add_up.1), calls=%async_computation.9 | async-start | bytes 524288 | tf_op jit(solution)/shard_map/all_to_all | solution.py:431
  162.8 0.7 gate_gradient.1
  163.6 1.0 weight_rows.1
  164.6 1.5 finish_x.1
  166.2 3.2 %all-to-all-done.9.rec_ref = f32[8,64,128]{2,1,0:T(8,128)S(1)} async-done(((f32[8,64,128]{2,1,0:T(8,128)}), f32[8,64,128]{2,1,0:T(8,128)S(1)}, u32[]{:S(2)}, u32[]{:S(2)}) %all-to-all-start.9) | async-done | bytes 262176 | tf_op jit(solution)/shard_map/all_to_all | solution.py:431
  169.4 0.7 deal_out.1
  (18 shorter events, 0.1 us)
Async XLA Ops:
  3.5 44.9 %copy-start = (bf16[256,1024]{1,0:T(8,128)(2,1)S(1)}, bf16[256,1024]{1,0:T(8,128)(2,1)}, u32[]{:S(2)}) copy-start(bf16[256,1024]{1,0:T(8,128)(2,1)} %do_ref.3) | copy-start | bytes 1572868
  3.5 44.9 %copy-start.1 = (bf16[256,256]{1,0:T(8,128)(2,1)S(1)}, bf16[256,256]{1,0:T(8,128)(2,1)}, u32[]{:S(2)}) copy-start(bf16[256,256]{1,0:T(8,128)(2,1)} %x_ref.5) | copy-start | bytes 393220
  3.6 44.9 %copy-start.3 = (bf16[256,128]{1,0:T(8,128)(2,1)S(1)}, bf16[256,128]{1,0:T(8,128)(2,1)}, u32[]{:S(2)}) copy-start(bf16[256,128]{1,0:T(8,128)(2,1)} %b_ref.5) | copy-start | bytes 196612
  3.6 44.9 %copy-start.4 = (bf16[256,128]{1,0:T(8,128)(2,1)S(1)}, bf16[256,128]{1,0:T(8,128)(2,1)}, u32[]{:S(2)}) copy-start(bf16[256,128]{1,0:T(8,128)(2,1)} %c_ref.7) | copy-start | bytes 196612
  3.6 44.9 %copy-start.5 = (bf16[256,1024]{1,0:T(8,128)(2,1)S(1)}, bf16[256,1024]{1,0:T(8,128)(2,1)}, u32[]{:S(2)}) copy-start(bf16[256,1024]{1,0:T(8,128)(2,1)} %w_ref.1) | copy-start | bytes 1572868
  3.6 44.9 %copy-start.6 = (f32[4,256]{1,0:T(4,128)S(1)}, f32[4,256]{1,0:T(4,128)}, u32[]{:S(2)}) copy-start(f32[4,256]{1,0:T(4,128)} %df_ref.11) | copy-start | bytes 12292
  3.6 44.9 %copy-start.7 = (f32[4,256]{1,0:T(4,128)S(1)}, f32[4,256]{1,0:T(4,128)}, u32[]{:S(2)}) copy-start(f32[4,256]{1,0:T(4,128)} %db_ref.11) | copy-start | bytes 12292
  3.6 44.9 %copy-start.8 = (f32[256]{0:T(256)S(1)}, f32[256]{0:T(256)}, u32[]{:S(2)}) copy-start(f32[256]{0:T(256)} %param.17) | copy-start | bytes 3076
  3.6 44.9 %copy-start.9 = (f32[4]{0:T(128)S(1)}, f32[4]{0:T(128)}, u32[]{:S(2)}) copy-start(f32[4]{0:T(128)} %skip_ref.3) | copy-start | bytes 52
  3.6 12.6 %all-to-all-start = ((f32[8,72,128]{2,1,0:T(8,128)}), f32[8,72,128]{2,1,0:T(8,128)S(1)}, u32[]{:S(2)}, u32[]{:S(2)}) async-start(f32[8,72,128]{2,1,0:T(8,128)} %local_states.1), calls=%async_computation | async-start | bytes 589824 | tf_op jit(solution)/shard_map/all_to_all | solution.py:431
  44.2 10.2 %copy-start.2 = (bf16[256,256]{1,0:T(8,128)(2,1)S(1)}, bf16[256,256]{1,0:T(8,128)(2,1)}, u32[]{:S(2)}) copy-start(bf16[256,256]{1,0:T(8,128)(2,1)} %z_ref.5) | copy-start | bytes 393220
  45.0 9.4 %all-to-all-start.2 = ((f32[8,64,128]{2,1,0:T(8,128)}), f32[8,64,128]{2,1,0:T(8,128)S(1)}, u32[]{:S(2)}, u32[]{:S(2)}) async-start(f32[8,64,128]{2,1,0:T(8,128)} %entries_up.1), calls=%async_computation.2 | async-start | bytes 524288 | tf_op jit(solution)/shard_map/all_to_all | solution.py:431
  125.6 15.7 %all-to-all-start.7 = ((f32[8,320,128]{2,1,0:T(8,128)}), f32[8,320,128]{2,1,0:T(8,128)S(1)}, u32[]{:S(2)}, u32[]{:S(2)}) async-start(f32[8,320,128]{2,1,0:T(8,128)} %entries_down.1), calls=%async_computation.7 | async-start | bytes 2621440 | tf_op jit(solution)/shard_map/all_to_all | solution.py:431
  158.5 10.9 %all-to-all-start.9 = ((f32[8,64,128]{2,1,0:T(8,128)}), f32[8,64,128]{2,1,0:T(8,128)S(1)}, u32[]{:S(2)}, u32[]{:S(2)}) async-start(f32[8,64,128]{2,1,0:T(8,128)} %add_up.1), calls=%async_computation.9 | async-start | bytes 524288 | tf_op jit(solution)/shard_map/all_to_all | solution.py:431

commit v5 on v4

--- a/solution.py
+++ b/solution.py
@@ -117,11 +117,13 @@
 def local_states(x_hbm, b_hbm, df_hbm, db_hbm, out_ref, x_ref, b_ref, df_ref, db_ref, sems):
     sources, targets = (x_hbm, b_hbm, df_hbm, db_hbm), (x_ref, b_ref, df_ref, db_ref)
     copies = [pltpu.make_async_copy(s, t, sems.at[i]) for i, (s, t) in enumerate(zip(sources, targets))]
-    for copy in copies:
+    for copy in copies[::-1]:
         copy.start()
-    for copy in copies:
-        copy.wait()
+    copies[2].wait()
+    copies[3].wait()
     cf, be, end_f, end_b = columns(df_ref[...], db_ref[...])
+    copies[0].wait()
+    copies[1].wait()
     x = x_ref[...].astype(F32)
     b = b_ref[...]
     state_f = dot_left(x * spread(jnp.exp(end_f - cf)), b, 0, 0)
@@ -229,7 +231,7 @@
         out_ref[k, span:, :] = weight
 
 
-def entries_down(back_ref, dec_ref, rec_ref, out_ref):
+def entries_down(back_ref, dec_ref, rec_ref, out_ref, w_ref):
     n_g, n = back_ref.shape[0], rec_ref.shape[0]
     size = WIDTH // n
     span = 2 * size // n_g
@@ -240,20 +242,25 @@
     put_entries(out_ref, 1, True, entry_b, dec_ref, rec_ref)
     part = back_ref.shape[1] - span
     for k in range(n_g):
-        weight = back_ref[k, span:, :]
-        for i in range(n):
-            out_ref[i, 2 * size + k * part : 2 * size + (k + 1) * part, :] = weight
-
-
-def weight_rows(rec_ref, gw_ref):
-    n = rec_ref.shape[0]
-    size = WIDTH // n
-    for i in range(n):
-        for block in range(gw_ref.shape[1] // LANES):
-            at = 2 * size + block * size
-            gw_ref[i * size : (i + 1) * size, block * LANES : (block + 1) * LANES] = (
-                rec_ref[i, at : at + size, :] * WEIGHT_SCALE
-            )
+        w_ref[k * part : (k + 1) * part, :] = back_ref[k, span:, :]
+
+
+def pair_up(own_ref, other_ref, out_ref):
+    out_ref[0, :, :] = own_ref[...]
+    out_ref[1, :, :] = other_ref[...]
+
+
+def weight_rows(at_ref, own_ref, *refs):
+    *other_refs, gw_ref = refs
+    blocks = gw_ref.shape[1] // LANES
+    size = own_ref.shape[1] // blocks
+    for i, ref in enumerate((own_ref, *other_refs)):
+        for j in range(2):
+            at = pl.multiple_of(at_ref[2 * i + j], size)
+            for block in range(blocks):
+                gw_ref[pl.ds(at, size), block * LANES : (block + 1) * LANES] = (
+                    ref[j, block * size : (block + 1) * size, :] * WEIGHT_SCALE
+                )
 
 
 def across_rows(cols):
@@ -476,11 +483,26 @@
     rows_z = (2 * size + weights) // n_hi
     sent = call(totals_down, "totals_down", [((n_hi, rows_z, LANES), F32)], rec1, rec2)
     recz2 = exchange(sent, "z_hi")
+    recz2, gx_near, gb_near, gc_near, grad_z = lax.optimization_barrier(
+        (recz2, gx_near, gb_near, gc_near, grad_z)
+    )
     sent = call(scan_down, "scan_down", [((n_hi, rows_z, LANES), F32)], place, recz1, recz2, scalars=1)
     back = exchange(sent, "z_hi")
-    sent = call(entries_down, "entries_down", [((n, 2 * size + weights, LANES), F32)], back, rec1, rec2)
+    sent, weight = call(
+        entries_down, "entries_down", [((n, 2 * size, LANES), F32), ((weights, LANES), F32)], back, rec1, rec2
+    )
     exits = exchange(sent, group)
-    grad_w = call(weight_rows, "weight_rows", [((WIDTH, model), F32)], exits)
+
+    other = lax.ppermute(weight, "z_lo", [(0, 1), (1, 0)])
+    pair = call(pair_up, "pair_up", [((2, weights, LANES), F32)], weight, other)
+    exits, pair = lax.optimization_barrier((exits, pair))
+    z_lo, x = lax.axis_index("z_lo"), lax.axis_index("x")
+    turns = (2, 1, n_x - 1)
+    at = [size * (z * n_x + (x - turn) % n_x) for turn in (0, *turns) for z in (z_lo, 1 - z_lo)]
+    at = jnp.stack(at).astype(jnp.int32)
+
+    def turned(a, turn):
+        return lax.ppermute(a, "x", [(i, (i + turn) % n_x) for i in range(n_x)])
 
     chunk = 2 * FRAMES // n_h
     sent = call(
@@ -488,8 +510,13 @@
     )
     grad_x = call(finish_x, "finish_x", [(square, BF16)], b_in, *decays, exits, gx_near)
     rec = exchange(sent, "head")
+    pairs = [turned(pair, turn) for turn in turns[:2]]
     sent = call(add_up, "add_up", [((n_h, chunk, LANES), F32)], rec)
+    sent, late = lax.optimization_barrier((sent, pair))
     rec = exchange(sent, "head")
+    pairs.append(turned(late, turns[2]))
+    grad_w = call(weight_rows, "weight_rows", [((WIDTH, model), F32)], at, pair, *pairs, scalars=1)
+    rec, grad_w, grad_x = lax.optimization_barrier((rec, grad_w, grad_x))
     grad_b, grad_c = call(deal_out, "deal_out", [((FRAMES, STATE), F32)] * 2, rec)
     return grad_x, grad_z, grad_b, grad_c, grad_w
 
@@ -497,7 +524,7 @@
 def solution(mesh):
     n_seq, n_head = mesh.devices.shape
     n_z = n_seq // HEADS
-    n_lo = min(2, n_z // 2)
+    n_lo = 2
     split = Mesh(mesh.devices.reshape(n_z // n_lo, n_lo, HEADS, n_head), ("z_hi", "z_lo", "x", "head"))
     seq = ("z_hi", "z_lo", "x")
     in_specs = (

time: 171 us -> 172 us (level)
  blocking collectives: 111 us -> 78.9 us
  starting transfers between devices: 17.7 us -> 45.1 us
  waiting for transfers between devices: 22.3 us -> 26.4 us
    all_to_all x6 -> x4, blocking collectives: 111 us -> 78.9 us  [exchange(): return lax.all_to_all(a, axis, 0, 0, tiled=True)]
    ppermute x0 -> x4, starting transfers between devices: none -> 14.3 us  [the longest x3 11 us: turned(): return lax.ppermute(a, 'x', [(i, (i + turn) % n_x) for i in range(n_x)])]
    all_to_all x4 -> x6, starting transfers between devices: 17.7 us -> 30.8 us  [exchange(): return lax.all_to_all(a, axis, 0, 0, tiled=True)]
    ppermute x0 -> x4, waiting for transfers between devices: none -> 2.44 us  [the longest x1 2.43 us: body(): other = lax.ppermute(weight, 'z_lo', [(0, 1), (1, 0)])]
    all_to_all x4 -> x6, waiting for transfers between devices: 22.3 us -> 24 us  [exchange(): return lax.all_to_all(a, axis, 0, 0, tiled=True)]
    pallas_call x16 -> x17, Pallas kernels: 18.4 us -> 19.8 us  [call(): pl.pallas_call(kernel, name=name, out_shape=shapes[0] if single else tupl...]
  transfers between devices with their start and end apart: 4 -> 10, of which waited for: 4 -> 6; matrix products, arithmetic and copies ran while one was open for 0% -> 0% of each run, Pallas kernels for 5% -> 6%
where the time goes in v5:
time: 172 us; the launch traced here: 171 us
  blocking collectives  78.9 us (46%)
  starting transfers between devices  45.1 us (26%)
  waiting for transfers between devices  26.4 us (15%)
  Pallas kernels  19.8 us (12%)
    all_to_all x4, blocking collectives, exchange(): return lax.all_to_all(a, axis, 0, 0, tiled=True)  78.9 us
    all_to_all x6, starting transfers between devices, exchange(): return lax.all_to_all(a, axis, 0, 0, tiled=True)  30.8 us
    all_to_all x6, waiting for transfers between devices, exchange(): return lax.all_to_all(a, axis, 0, 0, tiled=True)  24 us
    pallas_call x17, Pallas kernels, call(): pl.pallas_call(kernel, name=name, out_shape=shapes[0] if single else tupl...  19.8 us
    ppermute x3, starting transfers between devices, turned(): return lax.ppermute(a, 'x', [(i, (i + turn) % n_x) for i in range(n_x)])  11 us
  transfers between devices with their start and end apart: 10, of which 6 were waited for; matrix products, arithmetic and copies ran while one was open for 0% of the time, Pallas kernels for 6%

profile of v5, /device:TPU:1, one launch (start us, length us, event | category | flops | bytes accessed | tf_op | source)
XLA Modules:
  0.0 171.2 jit_solution(9377380352969729589)
XLA Ops:
  0.6 2.8 %local_states.1 = f32[8,72,128]{2,1,0:T(8,128)} custom-call(bf16[256,256]{1,0:T(8,128)(2,1)} %x_ref.5, bf16[256,128]{1,0:T(8,128)(2,1)} %b_ref.5, f32[4,256]{1,0:T(4,128)} %df_ref.11, f32[4,256]{1,0:T(4,128)} %db_ref.11), custom_call_target="tpu_custom_call" | custom-call | tf_op jit(solution)/shard_map/local_states/pallas_call | solution.py:426
  3.5 6.3 %all-to-all-start = ((f32[8,72,128]{2,1,0:T(8,128)}), f32[8,72,128]{2,1,0:T(8,128)S(1)}, u32[]{:S(2)}, u32[]{:S(2)}) async-start(f32[8,72,128]{2,1,0:T(8,128)} %local_states.1), calls=%async_computation | async-start | bytes 589824 | tf_op jit(solution)/shard_map/all_to_all | solution.py:438
  9.8 6.2 %all-to-all-done.rec_ref.dec_ref = f32[8,72,128]{2,1,0:T(8,128)S(1)} async-done(((f32[8,72,128]{2,1,0:T(8,128)}), f32[8,72,128]{2,1,0:T(8,128)S(1)}, u32[]{:S(2)}, u32[]{:S(2)}) %all-to-all-start) | async-done | bytes 294944 | tf_op jit(solution)/shard_map/all_to_all | solution.py:438
  16.1 28.0 %all_to_all.50.zrec_ref.dec_ref = f32[8,40,128]{2,1,0:T(8,128)S(1)} all-to-all(f32[8,40,128]{2,1,0:T(8,128)S(1)} %totals_up.1), channel_id=1, replica_groups=mesh['z_hi'=8,'z_lo'=2,'x'=4,'head'=8] {'z_hi'}, dimensions={0} | all-to-all | bytes 327680 | tf_op jit(solution)/shard_map/all_to_all | solution.py:438
  44.1 0.8 entries_up.1
  44.9 3.4 %all-to-all-start.2 = ((f32[8,64,128]{2,1,0:T(8,128)}), f32[8,64,128]{2,1,0:T(8,128)S(1)}, u32[]{:S(2)}, u32[]{:S(2)}) async-start(f32[8,64,128]{2,1,0:T(8,128)} %entries_up.1), calls=%async_computation.2 | async-start | bytes 524288 | tf_op jit(solution)/shard_map/all_to_all | solution.py:438
  48.4 2.1 %near_outputs.1 = (f32[256,256]{1,0:T(8,128)S(1)}, f32[256,256]{1,0:T(8,128)S(1)}) custom-call(f32[4]{0:T(128)S(1)} %copy-done.9, bf16[256,256]{1,0:T(8,128)(2,1)S(1)} %copy-done.1, bf16[256,128]{1,0:T(8,128)(2,1)S(1)} %copy-done.3, bf16[256,128]{1,0:T(8,128)(2,1)S(1)} %copy-done.4, f32[4,256]{1,0:T(4,128)S(1)} %copy-done.6, f32[4,256]{1,0:T(4,128)S(1)} %copy-done.7, ...), custom_call_target="tpu_custom_call" | custom-call | tf_op jit(solution)/shard_map/near_outputs/pallas_call | solution.py:426
  50.5 3.8 %all-to-all-done.2.ent_ref = f32[8,64,128]{2,1,0:T(8,128)S(1)} async-done(((f32[8,64,128]{2,1,0:T(8,128)}), f32[8,64,128]{2,1,0:T(8,128)S(1)}, u32[]{:S(2)}, u32[]{:S(2)}) %all-to-all-start.2) | async-done | bytes 262176 | tf_op jit(solution)/shard_map/all_to_all | solution.py:438
  54.3 1.0 outputs.1
  55.3 13.7 %all_to_all.51.sums_ref = f32[8,8,128]{2,1,0:T(8,128)S(1)} all-to-all(f32[8,8,128]{2,1,0:T(8,128)S(1)} %get-tuple-element.33), channel_id=1, replica_groups=mesh['z_hi'=8,'z_lo'=2,'x'=4,'head'=8] {'head'}, dimensions={0} | all-to-all | bytes 65536 | tf_op jit(solution)/shard_map/all_to_all | solution.py:438
  69.0 1.4 gradients.1
  70.4 19.6 %all_to_all.52.rec_ref = f32[8,320,128]{2,1,0:T(8,128)S(1)} all-to-all(f32[8,320,128]{2,1,0:T(8,128)S(1)} %get-tuple-element.35), channel_id=1, replica_groups=mesh['z_hi'=8,'z_lo'=2,'x'=4,'head'=8] {'z_lo','x'}, dimensions={0} | all-to-all | bytes 2621440 | tf_op jit(solution)/shard_map/all_to_all | solution.py:438
  90.0 0.7 totals_down.1
  90.8 3.4 %all-to-all-start.5 = ((f32[8,40,128]{2,1,0:T(8,128)}), f32[8,40,128]{2,1,0:T(8,128)S(1)}, u32[]{:S(2)}, u32[]{:S(2)}) async-start(f32[8,40,128]{2,1,0:T(8,128)} %totals_down.1), calls=%async_computation.5 | async-start | bytes 327680 | tf_op jit(solution)/shard_map/all_to_all | solution.py:438
  94.1 0.7 gate_gradient.1
  94.9 3.0 %near_gradients.1 = (f32[256,256]{1,0:T(8,128)S(1)}, f32[256,128]{1,0:T(8,128)S(1)}, f32[256,128]{1,0:T(8,128)S(1)}) custom-call(f32[4]{0:T(128)S(1)} %copy-done.9, bf16[256,256]{1,0:T(8,128)(2,1)S(1)} %copy-done.1, bf16[256,128]{1,0:T(8,128)(2,1)S(1)} %copy-done.3, bf16[256,128]{1,0:T(8,128)(2,1)S(1)} %copy-done.4, f32[4,256]{1,0:T(4,128)S(1)} %copy-done.6, ...), custom_call_target="tpu_custom_call" | custom-call | tf_op jit(solution)/shard_map/near_gradients/pallas_call | solution.py:426
  97.9 10.4 %all-to-all-done.5.rec_ref = f32[8,40,128]{2,1,0:T(8,128)S(1)} async-done(((f32[8,40,128]{2,1,0:T(8,128)}), f32[8,40,128]{2,1,0:T(8,128)S(1)}, u32[]{:S(2)}, u32[]{:S(2)}) %all-to-all-start.5) | async-done | bytes 163872 | tf_op jit(solution)/shard_map/all_to_all | solution.py:438
  108.4 17.6 %all_to_all.53.back_ref = f32[8,40,128]{2,1,0:T(8,128)S(1)} all-to-all(f32[8,40,128]{2,1,0:T(8,128)S(1)} %scan_down.1), channel_id=1, replica_groups=mesh['z_hi'=8,'z_lo'=2,'x'=4,'head'=8] {'z_hi'}, dimensions={0} | all-to-all | bytes 327680 | tf_op jit(solution)/shard_map/all_to_all | solution.py:438
  126.0 0.7 entries_down.1
  126.7 3.4 %all-to-all-start.7 = ((f32[8,64,128]{2,1,0:T(8,128)}), f32[8,64,128]{2,1,0:T(8,128)S(1)}, u32[]{:S(2)}, u32[]{:S(2)}) async-start(f32[8,64,128]{2,1,0:T(8,128)} %get-tuple-element.42), calls=%async_computation.7 | async-start | bytes 524288 | tf_op jit(solution)/shard_map/all_to_all | solution.py:438
  130.1 3.3 %collective-permute-start = (f32[256,128]{1,0:T(8,128)S(1)}, f32[256,128]{1,0:T(8,128)S(1)}, u32[]{:S(2)}, u32[]{:S(2)}) collective-permute-start(f32[256,128]{1,0:T(8,128)S(1)} %get-tuple-element.43.own_ref), channel_id=1, source_target_pairs={{0,32},{32,0},{1,33},{33,1},{2,34},{34,2},{3,35},{35,3},{4,36},{36... | collective-permute-start | bytes 393224 | tf_op jit(solution)/shard_map/ppermute | solution.py:496
  133.4 2.4 %collective-permute-done.other_ref = f32[256,128]{1,0:T(8,128)S(1)} collective-permute-done((f32[256,128]{1,0:T(8,128)S(1)}, f32[256,128]{1,0:T(8,128)S(1)}, u32[]{:S(2)}, u32[]{:S(2)}) %collective-permute-start) | collective-permute-done | bytes 131104 | tf_op jit(solution)/shard_map/ppermute | solution.py:496
  136.1 1.9 %finish.1 = f32[8,64,128]{2,1,0:T(8,128)} custom-call(bf16[256,256]{1,0:T(8,128)(2,1)S(1)} %copy-done.1, f32[4,256]{1,0:T(4,128)S(1)} %copy-done.6, f32[4,256]{1,0:T(4,128)S(1)} %copy-done.7, f32[8,64,128]{2,1,0:T(8,128)S(1)} %all-to-all-done.7.exit_ref, f32[256,128]{1,0:T(8,128)S(1)} %get-tuple-element.45.gb_near, f32[256,128]{1,0:T(8,128)S(1)} %get-tuple-element.46.gc_near), custom_call_target="tpu_custom_call" | custom-call | tf_op jit(solution)/shard_map/finish/pallas_call | solution.py:426
  138.0 8.9 %all-to-all-start.8 = ((f32[8,64,128]{2,1,0:T(8,128)}), f32[8,64,128]{2,1,0:T(8,128)S(1)}, u32[]{:S(2)}, u32[]{:S(2)}) async-start(f32[8,64,128]{2,1,0:T(8,128)} %finish.1), calls=%async_computation.8 | async-start | bytes 524288 | tf_op jit(solution)/shard_map/all_to_all | solution.py:438
  146.9 3.3 %collective-permute-start.2 = (f32[2,256,128]{2,1,0:T(8,128)S(1)}, f32[2,256,128]{2,1,0:T(8,128)S(1)}, u32[]{:S(2)}, u32[]{:S(2)}) collective-permute-start(f32[2,256,128]{2,1,0:T(8,128)S(1)} %pair_up.1.own_ref), channel_id=1, source_target_pairs={{0,8},{8,16},{16,24},{24,0},{1,9},{9,17},{17,25},{25,1},{2,10},{10... | collective-permute-start | bytes 786440 | tf_op jit(solution)/shard_map/ppermute | solution.py:505
  150.2 4.3 %collective-permute-start.1 = (f32[2,256,128]{2,1,0:T(8,128)S(1)}, f32[2,256,128]{2,1,0:T(8,128)S(1)}, u32[]{:S(2)}, u32[]{:S(2)}) collective-permute-start(f32[2,256,128]{2,1,0:T(8,128)S(1)} %pair_up.1.own_ref), channel_id=1, source_target_pairs={{0,16},{8,24},{16,0},{24,8},{1,17},{9,25},{17,1},{25,9},{2,18},{10... | collective-permute-start | bytes 786440 | tf_op jit(solution)/shard_map/ppermute | solution.py:505
  154.5 0.7 add_up.1
  155.3 3.4 %collective-permute-start.3 = (f32[2,256,128]{2,1,0:T(8,128)S(1)}, f32[2,256,128]{2,1,0:T(8,128)S(1)}, u32[]{:S(2)}, u32[]{:S(2)}) collective-permute-start(f32[2,256,128]{2,1,0:T(8,128)S(1)} %pair_up.1.own_ref), channel_id=1, source_target_pairs={{0,24},{8,0},{16,8},{24,16},{1,25},{9,1},{17,9},{25,17},{2,26},{10... | collective-permute-start | bytes 786440 | tf_op jit(solution)/shard_map/ppermute | solution.py:505
  158.7 5.3 %all-to-all-start.9 = ((f32[8,64,128]{2,1,0:T(8,128)}), f32[8,64,128]{2,1,0:T(8,128)S(1)}, u32[]{:S(2)}, u32[]{:S(2)}) async-start(f32[8,64,128]{2,1,0:T(8,128)} %add_up.1), calls=%async_computation.9 | async-start | bytes 524288 | tf_op jit(solution)/shard_map/all_to_all | solution.py:438
  164.1 1.5 finish_x.1
  165.7 1.6 weight_rows.1
  167.2 3.3 %all-to-all-done.9.rec_ref = f32[8,64,128]{2,1,0:T(8,128)S(1)} async-done(((f32[8,64,128]{2,1,0:T(8,128)}), f32[8,64,128]{2,1,0:T(8,128)S(1)}, u32[]{:S(2)}, u32[]{:S(2)}) %all-to-all-start.9) | async-done | bytes 262176 | tf_op jit(solution)/shard_map/all_to_all | solution.py:438
  (30 shorter events, 1.2 us)
Async XLA Ops:
  3.4 44.9 %copy-start = (bf16[256,1024]{1,0:T(8,128)(2,1)S(1)}, bf16[256,1024]{1,0:T(8,128)(2,1)}, u32[]{:S(2)}) copy-start(bf16[256,1024]{1,0:T(8,128)(2,1)} %do_ref.3) | copy-start | bytes 1572868
  3.4 44.9 %copy-start.1 = (bf16[256,256]{1,0:T(8,128)(2,1)S(1)}, bf16[256,256]{1,0:T(8,128)(2,1)}, u32[]{:S(2)}) copy-start(bf16[256,256]{1,0:T(8,128)(2,1)} %x_ref.5) | copy-start | bytes 393220
  3.4 44.9 %copy-start.3 = (bf16[256,128]{1,0:T(8,128)(2,1)S(1)}, bf16[256,128]{1,0:T(8,128)(2,1)}, u32[]{:S(2)}) copy-start(bf16[256,128]{1,0:T(8,128)(2,1)} %b_ref.5) | copy-start | bytes 196612
  3.4 44.9 %copy-start.4 = (bf16[256,128]{1,0:T(8,128)(2,1)S(1)}, bf16[256,128]{1,0:T(8,128)(2,1)}, u32[]{:S(2)}) copy-start(bf16[256,128]{1,0:T(8,128)(2,1)} %c_ref.7) | copy-start | bytes 196612
  3.4 44.9 %copy-start.5 = (bf16[256,1024]{1,0:T(8,128)(2,1)S(1)}, bf16[256,1024]{1,0:T(8,128)(2,1)}, u32[]{:S(2)}) copy-start(bf16[256,1024]{1,0:T(8,128)(2,1)} %w_ref.1) | copy-start | bytes 1572868
  3.4 44.9 %copy-start.6 = (f32[4,256]{1,0:T(4,128)S(1)}, f32[4,256]{1,0:T(4,128)}, u32[]{:S(2)}) copy-start(f32[4,256]{1,0:T(4,128)} %df_ref.11) | copy-start | bytes 12292
  3.5 44.9 %copy-start.7 = (f32[4,256]{1,0:T(4,128)S(1)}, f32[4,256]{1,0:T(4,128)}, u32[]{:S(2)}) copy-start(f32[4,256]{1,0:T(4,128)} %db_ref.11) | copy-start | bytes 12292
  3.5 44.9 %copy-start.8 = (f32[256]{0:T(256)S(1)}, f32[256]{0:T(256)}, u32[]{:S(2)}) copy-start(f32[256]{0:T(256)} %param.17) | copy-start | bytes 3076
  3.5 44.9 %copy-start.9 = (f32[4]{0:T(128)S(1)}, f32[4]{0:T(128)}, u32[]{:S(2)}) copy-start(f32[4]{0:T(128)} %skip_ref.3) | copy-start | bytes 52
  3.5 12.6 %all-to-all-start = ((f32[8,72,128]{2,1,0:T(8,128)}), f32[8,72,128]{2,1,0:T(8,128)S(1)}, u32[]{:S(2)}, u32[]{:S(2)}) async-start(f32[8,72,128]{2,1,0:T(8,128)} %local_states.1), calls=%async_computation | async-start | bytes 589824 | tf_op jit(solution)/shard_map/all_to_all | solution.py:438
  44.1 10.2 %copy-start.2 = (bf16[256,256]{1,0:T(8,128)(2,1)S(1)}, bf16[256,256]{1,0:T(8,128)(2,1)}, u32[]{:S(2)}) copy-start(bf16[256,256]{1,0:T(8,128)(2,1)} %z_ref.5) | copy-start | bytes 393220
  44.9 9.4 %all-to-all-start.2 = ((f32[8,64,128]{2,1,0:T(8,128)}), f32[8,64,128]{2,1,0:T(8,128)S(1)}, u32[]{:S(2)}, u32[]{:S(2)}) async-start(f32[8,64,128]{2,1,0:T(8,128)} %entries_up.1), calls=%async_computation.2 | async-start | bytes 524288 | tf_op jit(solution)/shard_map/all_to_all | solution.py:438
  90.8 17.6 %all-to-all-start.5 = ((f32[8,40,128]{2,1,0:T(8,128)}), f32[8,40,128]{2,1,0:T(8,128)S(1)}, u32[]{:S(2)}, u32[]{:S(2)}) async-start(f32[8,40,128]{2,1,0:T(8,128)} %totals_down.1), calls=%async_computation.5 | async-start | bytes 327680 | tf_op jit(solution)/shard_map/all_to_all | solution.py:438
  126.7 9.4 %all-to-all-start.7 = ((f32[8,64,128]{2,1,0:T(8,128)}), f32[8,64,128]{2,1,0:T(8,128)S(1)}, u32[]{:S(2)}, u32[]{:S(2)}) async-start(f32[8,64,128]{2,1,0:T(8,128)} %get-tuple-element.42), calls=%async_computation.7 | async-start | bytes 524288 | tf_op jit(solution)/shard_map/all_to_all | solution.py:438
  130.1 5.7 %collective-permute-start = (f32[256,128]{1,0:T(8,128)S(1)}, f32[256,128]{1,0:T(8,128)S(1)}, u32[]{:S(2)}, u32[]{:S(2)}) collective-permute-start(f32[256,128]{1,0:T(8,128)S(1)} %get-tuple-element.43.own_ref), channel_id=1, source_target_pairs={{0,32},{32,0},{1,33},{33,1},{2,34},{34,2},{3,35},{35,3},{4,36},{36... | collective-permute-start | bytes 393224 | tf_op jit(solution)/shard_map/ppermute | solution.py:496
  138.0 16.5 %all-to-all-start.8 = ((f32[8,64,128]{2,1,0:T(8,128)}), f32[8,64,128]{2,1,0:T(8,128)S(1)}, u32[]{:S(2)}, u32[]{:S(2)}) async-start(f32[8,64,128]{2,1,0:T(8,128)} %finish.1), calls=%async_computation.8 | async-start | bytes 524288 | tf_op jit(solution)/shard_map/all_to_all | solution.py:438
  146.9 18.7 %collective-permute-start.2 = (f32[2,256,128]{2,1,0:T(8,128)S(1)}, f32[2,256,128]{2,1,0:T(8,128)S(1)}, u32[]{:S(2)}, u32[]{:S(2)}) collective-permute-start(f32[2,256,128]{2,1,0:T(8,128)S(1)} %pair_up.1.own_ref), channel_id=1, source_target_pairs={{0,8},{8,16},{16,24},{24,0},{1,9},{9,17},{17,25},{25,1},{2,10},{10... | collective-permute-start | bytes 786440 | tf_op jit(solution)/shard_map/ppermute | solution.py:505
  150.2 15.4 %collective-permute-start.1 = (f32[2,256,128]{2,1,0:T(8,128)S(1)}, f32[2,256,128]{2,1,0:T(8,128)S(1)}, u32[]{:S(2)}, u32[]{:S(2)}) collective-permute-start(f32[2,256,128]{2,1,0:T(8,128)S(1)} %pair_up.1.own_ref), channel_id=1, source_target_pairs={{0,16},{8,24},{16,0},{24,8},{1,17},{9,25},{17,1},{25,9},{2,18},{10... | collective-permute-start | bytes 786440 | tf_op jit(solution)/shard_map/ppermute | solution.py:505
  155.3 10.4 %collective-permute-start.3 = (f32[2,256,128]{2,1,0:T(8,128)S(1)}, f32[2,256,128]{2,1,0:T(8,128)S(1)}, u32[]{:S(2)}, u32[]{:S(2)}) collective-permute-start(f32[2,256,128]{2,1,0:T(8,128)S(1)} %pair_up.1.own_ref), channel_id=1, source_target_pairs={{0,24},{8,0},{16,8},{24,16},{1,25},{9,1},{17,9},{25,17},{2,26},{10... | collective-permute-start | bytes 786440 | tf_op jit(solution)/shard_map/ppermute | solution.py:505
  158.7 11.8 %all-to-all-start.9 = ((f32[8,64,128]{2,1,0:T(8,128)}), f32[8,64,128]{2,1,0:T(8,128)S(1)}, u32[]{:S(2)}, u32[]{:S(2)}) async-start(f32[8,64,128]{2,1,0:T(8,128)} %add_up.1), calls=%async_computation.9 | async-start | bytes 524288 | tf_op jit(solution)/shard_map/all_to_all | solution.py:438

commit v6 on v4

--- a/solution.py
+++ b/solution.py
@@ -117,11 +117,13 @@
 def local_states(x_hbm, b_hbm, df_hbm, db_hbm, out_ref, x_ref, b_ref, df_ref, db_ref, sems):
     sources, targets = (x_hbm, b_hbm, df_hbm, db_hbm), (x_ref, b_ref, df_ref, db_ref)
     copies = [pltpu.make_async_copy(s, t, sems.at[i]) for i, (s, t) in enumerate(zip(sources, targets))]
-    for copy in copies:
+    for copy in copies[::-1]:
         copy.start()
-    for copy in copies:
-        copy.wait()
+    copies[2].wait()
+    copies[3].wait()
     cf, be, end_f, end_b = columns(df_ref[...], db_ref[...])
+    copies[0].wait()
+    copies[1].wait()
     x = x_ref[...].astype(F32)
     b = b_ref[...]
     state_f = dot_left(x * spread(jnp.exp(end_f - cf)), b, 0, 0)
@@ -476,6 +478,9 @@
     rows_z = (2 * size + weights) // n_hi
     sent = call(totals_down, "totals_down", [((n_hi, rows_z, LANES), F32)], rec1, rec2)
     recz2 = exchange(sent, "z_hi")
+    recz2, gx_near, gb_near, gc_near, grad_z = lax.optimization_barrier(
+        (recz2, gx_near, gb_near, gc_near, grad_z)
+    )
     sent = call(scan_down, "scan_down", [((n_hi, rows_z, LANES), F32)], place, recz1, recz2, scalars=1)
     back = exchange(sent, "z_hi")
     sent = call(entries_down, "entries_down", [((n, 2 * size + weights, LANES), F32)], back, rec1, rec2)

time: 171 us -> 172 us (level)
  waiting for transfers between devices: 22.3 us -> 24.4 us
    all_to_all x4, waiting for transfers between devices: 22.3 us -> 24.4 us  [exchange(): return lax.all_to_all(a, axis, 0, 0, tiled=True)]
where the time goes in v6:
time: 172 us
  blocking collectives  110 us (64%)
  waiting for transfers between devices  24.4 us (14%)
  Pallas kernels  17.9 us (10%)
  starting transfers between devices  17.5 us (10%)
    all_to_all x6, blocking collectives, exchange(): return lax.all_to_all(a, axis, 0, 0, tiled=True)  110 us
    all_to_all x4, waiting for transfers between devices, exchange(): return lax.all_to_all(a, axis, 0, 0, tiled=True)  24.4 us
    pallas_call x16, Pallas kernels, call(): pl.pallas_call(kernel, name=name, out_shape=shapes[0] if single else tupl...  17.9 us
    all_to_all x4, starting transfers between devices, exchange(): return lax.all_to_all(a, axis, 0, 0, tiled=True)  17.5 us
  transfers between devices with their start and end apart: 4, of which 4 were waited for; matrix products, arithmetic and copies ran while one was open for 0% of the time, Pallas kernels for 5%

profile of v6, /device:TPU:1, one launch (start us, length us, event | category | flops | bytes accessed | tf_op | source)
XLA Modules:
  0.0 171.7 jit_solution(5277160509312072633)
XLA Ops:
  0.6 2.8 %local_states.1 = f32[8,72,128]{2,1,0:T(8,128)} custom-call(bf16[256,256]{1,0:T(8,128)(2,1)} %x_ref.5, bf16[256,128]{1,0:T(8,128)(2,1)} %b_ref.5, f32[4,256]{1,0:T(4,128)} %df_ref.11, f32[4,256]{1,0:T(4,128)} %db_ref.11), custom_call_target="tpu_custom_call" | custom-call | tf_op jit(solution)/shard_map/local_states/pallas_call | solution.py:421
  3.4 0.0 copy-start
  3.4 0.0 copy-start.1
  3.4 0.0 copy-start.5
  3.5 6.3 %all-to-all-start = ((f32[8,72,128]{2,1,0:T(8,128)}), f32[8,72,128]{2,1,0:T(8,128)S(1)}, u32[]{:S(2)}, u32[]{:S(2)}) async-start(f32[8,72,128]{2,1,0:T(8,128)} %local_states.1), calls=%async_computation | async-start | bytes 589824 | tf_op jit(solution)/shard_map/all_to_all | solution.py:433
  9.8 6.2 %all-to-all-done.rec_ref.dec_ref = f32[8,72,128]{2,1,0:T(8,128)S(1)} async-done(((f32[8,72,128]{2,1,0:T(8,128)}), f32[8,72,128]{2,1,0:T(8,128)S(1)}, u32[]{:S(2)}, u32[]{:S(2)}) %all-to-all-start) | async-done | bytes 294944 | tf_op jit(solution)/shard_map/all_to_all | solution.py:433
  16.1 28.0 %all_to_all.50.zrec_ref.dec_ref = f32[8,40,128]{2,1,0:T(8,128)S(1)} all-to-all(f32[8,40,128]{2,1,0:T(8,128)S(1)} %totals_up.1), channel_id=1, replica_groups=mesh['z_hi'=8,'z_lo'=2,'x'=4,'head'=8] {'z_hi'}, dimensions={0} | all-to-all | bytes 327680 | tf_op jit(solution)/shard_map/all_to_all | solution.py:433
  44.1 0.8 entries_up.1
  44.9 3.4 %all-to-all-start.2 = ((f32[8,64,128]{2,1,0:T(8,128)}), f32[8,64,128]{2,1,0:T(8,128)S(1)}, u32[]{:S(2)}, u32[]{:S(2)}) async-start(f32[8,64,128]{2,1,0:T(8,128)} %entries_up.1), calls=%async_computation.2 | async-start | bytes 524288 | tf_op jit(solution)/shard_map/all_to_all | solution.py:433
  48.4 2.1 %near_outputs.1 = (f32[256,256]{1,0:T(8,128)S(1)}, f32[256,256]{1,0:T(8,128)S(1)}) custom-call(f32[4]{0:T(128)S(1)} %copy-done.11, bf16[256,256]{1,0:T(8,128)(2,1)S(1)} %copy-done.1, bf16[256,128]{1,0:T(8,128)(2,1)S(1)} %copy-done.3, bf16[256,128]{1,0:T(8,128)(2,1)S(1)} %copy-done.4, f32[4,256]{1,0:T(4,128)S(1)} %copy-done.6, f32[4,256]{1,0:T(4,128)S(1)} %copy-done.7, ...), custom_call_target="tpu_custom_call" | custom-call | tf_op jit(solution)/shard_map/near_outputs/pallas_call | solution.py:421
  50.5 3.8 %all-to-all-done.2.ent_ref = f32[8,64,128]{2,1,0:T(8,128)S(1)} async-done(((f32[8,64,128]{2,1,0:T(8,128)}), f32[8,64,128]{2,1,0:T(8,128)S(1)}, u32[]{:S(2)}, u32[]{:S(2)}) %all-to-all-start.2) | async-done | bytes 262176 | tf_op jit(solution)/shard_map/all_to_all | solution.py:433
  54.3 1.0 outputs.1
  55.3 13.7 %all_to_all.51.sums_ref = f32[8,8,128]{2,1,0:T(8,128)S(1)} all-to-all(f32[8,8,128]{2,1,0:T(8,128)S(1)} %get-tuple-element.24), channel_id=1, replica_groups=mesh['z_hi'=8,'z_lo'=2,'x'=4,'head'=8] {'head'}, dimensions={0} | all-to-all | bytes 65536 | tf_op jit(solution)/shard_map/all_to_all | solution.py:433
  69.0 1.4 gradients.1
  70.4 19.6 %all_to_all.52.rec_ref = f32[8,320,128]{2,1,0:T(8,128)S(1)} all-to-all(f32[8,320,128]{2,1,0:T(8,128)S(1)} %get-tuple-element.26), channel_id=1, replica_groups=mesh['z_hi'=8,'z_lo'=2,'x'=4,'head'=8] {'z_lo','x'}, dimensions={0} | all-to-all | bytes 2621440 | tf_op jit(solution)/shard_map/all_to_all | solution.py:433
  90.0 0.7 totals_down.1
  90.8 3.4 %all-to-all-start.5 = ((f32[8,40,128]{2,1,0:T(8,128)}), f32[8,40,128]{2,1,0:T(8,128)S(1)}, u32[]{:S(2)}, u32[]{:S(2)}) async-start(f32[8,40,128]{2,1,0:T(8,128)} %totals_down.1), calls=%async_computation.5 | async-start | bytes 327680 | tf_op jit(solution)/shard_map/all_to_all | solution.py:433
  94.1 0.7 gate_gradient.1
  94.9 3.0 %near_gradients.1 = (f32[256,256]{1,0:T(8,128)S(1)}, f32[256,128]{1,0:T(8,128)S(1)}, f32[256,128]{1,0:T(8,128)S(1)}) custom-call(f32[4]{0:T(128)S(1)} %copy-done.11, bf16[256,256]{1,0:T(8,128)(2,1)S(1)} %copy-done.1, bf16[256,128]{1,0:T(8,128)(2,1)S(1)} %copy-done.3, bf16[256,128]{1,0:T(8,128)(2,1)S(1)} %copy-done.4, f32[4,256]{1,0:T(4,128)S(1)} %copy-done.6, ...), custom_call_target="tpu_custom_call" | custom-call | tf_op jit(solution)/shard_map/near_gradients/pallas_call | solution.py:421
  97.9 10.4 %all-to-all-done.5.rec_ref = f32[8,40,128]{2,1,0:T(8,128)S(1)} async-done(((f32[8,40,128]{2,1,0:T(8,128)}), f32[8,40,128]{2,1,0:T(8,128)S(1)}, u32[]{:S(2)}, u32[]{:S(2)}) %all-to-all-start.5) | async-done | bytes 163872 | tf_op jit(solution)/shard_map/all_to_all | solution.py:433
  108.4 17.6 %all_to_all.53.back_ref = f32[8,40,128]{2,1,0:T(8,128)S(1)} all-to-all(f32[8,40,128]{2,1,0:T(8,128)S(1)} %scan_down.1), channel_id=1, replica_groups=mesh['z_hi'=8,'z_lo'=2,'x'=4,'head'=8] {'z_hi'}, dimensions={0} | all-to-all | bytes 327680 | tf_op jit(solution)/shard_map/all_to_all | solution.py:433
  126.0 0.1 entries_down.1
  126.1 15.8 %all_to_all.54.exit_ref.rec_ref = f32[8,320,128]{2,1,0:T(8,128)S(1)} all-to-all(f32[8,320,128]{2,1,0:T(8,128)S(1)} %entries_down.1), channel_id=1, replica_groups=mesh['z_hi'=8,'z_lo'=2,'x'=4,'head'=8] {'z_lo','x'}, dimensions={0} | all-to-all | bytes 2621440 | tf_op jit(solution)/shard_map/all_to_all | solution.py:433
  141.9 0.9 copy-done.9
  142.8 1.2 finish.1
  144.0 15.3 %all_to_all.55.rec_ref = f32[8,64,128]{2,1,0:T(8,128)S(1)} all-to-all(f32[8,64,128]{2,1,0:T(8,128)S(1)} %finish.1), channel_id=1, replica_groups=mesh['z_hi'=8,'z_lo'=2,'x'=4,'head'=8] {'head'}, dimensions={0} | all-to-all | bytes 524288 | tf_op jit(solution)/shard_map/all_to_all | solution.py:433
  159.3 0.7 add_up.1
  160.1 4.4 %all-to-all-start.9 = ((f32[8,64,128]{2,1,0:T(8,128)}), f32[8,64,128]{2,1,0:T(8,128)S(1)}, u32[]{:S(2)}, u32[]{:S(2)}) async-start(f32[8,64,128]{2,1,0:T(8,128)} %add_up.1), calls=%async_computation.9 | async-start | bytes 524288 | tf_op jit(solution)/shard_map/all_to_all | solution.py:433
  164.4 1.0 weight_rows.1
  165.5 1.5 finish_x.1
  167.0 3.9 %all-to-all-done.9.rec_ref = f32[8,64,128]{2,1,0:T(8,128)S(1)} async-done(((f32[8,64,128]{2,1,0:T(8,128)}), f32[8,64,128]{2,1,0:T(8,128)S(1)}, u32[]{:S(2)}, u32[]{:S(2)}) %all-to-all-start.9) | async-done | bytes 262176 | tf_op jit(solution)/shard_map/all_to_all | solution.py:433
  170.9 0.7 deal_out.1
  (22 shorter events, 0.1 us)
Async XLA Ops:
  3.4 44.9 %copy-start = (bf16[256,1024]{1,0:T(8,128)(2,1)S(1)}, bf16[256,1024]{1,0:T(8,128)(2,1)}, u32[]{:S(2)}) copy-start(bf16[256,1024]{1,0:T(8,128)(2,1)} %do_ref.3) | copy-start | bytes 1572868
  3.4 44.9 %copy-start.1 = (bf16[256,256]{1,0:T(8,128)(2,1)S(1)}, bf16[256,256]{1,0:T(8,128)(2,1)}, u32[]{:S(2)}) copy-start(bf16[256,256]{1,0:T(8,128)(2,1)} %x_ref.5) | copy-start | bytes 393220
  3.4 44.9 %copy-start.3 = (bf16[256,128]{1,0:T(8,128)(2,1)S(1)}, bf16[256,128]{1,0:T(8,128)(2,1)}, u32[]{:S(2)}) copy-start(bf16[256,128]{1,0:T(8,128)(2,1)} %b_ref.5) | copy-start | bytes 196612
  3.4 44.9 %copy-start.4 = (bf16[256,128]{1,0:T(8,128)(2,1)S(1)}, bf16[256,128]{1,0:T(8,128)(2,1)}, u32[]{:S(2)}) copy-start(bf16[256,128]{1,0:T(8,128)(2,1)} %c_ref.7) | copy-start | bytes 196612
  3.4 44.9 %copy-start.5 = (bf16[256,1024]{1,0:T(8,128)(2,1)S(1)}, bf16[256,1024]{1,0:T(8,128)(2,1)}, u32[]{:S(2)}) copy-start(bf16[256,1024]{1,0:T(8,128)(2,1)} %w_ref.1) | copy-start | bytes 1572868
  3.4 44.9 %copy-start.6 = (f32[4,256]{1,0:T(4,128)S(1)}, f32[4,256]{1,0:T(4,128)}, u32[]{:S(2)}) copy-start(f32[4,256]{1,0:T(4,128)} %df_ref.11) | copy-start | bytes 12292
  3.5 44.9 %copy-start.7 = (f32[4,256]{1,0:T(4,128)S(1)}, f32[4,256]{1,0:T(4,128)}, u32[]{:S(2)}) copy-start(f32[4,256]{1,0:T(4,128)} %db_ref.11) | copy-start | bytes 12292
  3.5 44.9 %copy-start.10 = (f32[256]{0:T(256)S(1)}, f32[256]{0:T(256)}, u32[]{:S(2)}) copy-start(f32[256]{0:T(256)} %param.17) | copy-start | bytes 3076
  3.5 44.9 %copy-start.11 = (f32[4]{0:T(128)S(1)}, f32[4]{0:T(128)}, u32[]{:S(2)}) copy-start(f32[4]{0:T(128)} %skip_ref.3) | copy-start | bytes 52
  3.5 12.6 %all-to-all-start = ((f32[8,72,128]{2,1,0:T(8,128)}), f32[8,72,128]{2,1,0:T(8,128)S(1)}, u32[]{:S(2)}, u32[]{:S(2)}) async-start(f32[8,72,128]{2,1,0:T(8,128)} %local_states.1), calls=%async_computation | async-start | bytes 589824 | tf_op jit(solution)/shard_map/all_to_all | solution.py:433
  44.1 10.2 %copy-start.2 = (bf16[256,256]{1,0:T(8,128)(2,1)S(1)}, bf16[256,256]{1,0:T(8,128)(2,1)}, u32[]{:S(2)}) copy-start(bf16[256,256]{1,0:T(8,128)(2,1)} %z_ref.5) | copy-start | bytes 393220
  44.9 9.4 %all-to-all-start.2 = ((f32[8,64,128]{2,1,0:T(8,128)}), f32[8,64,128]{2,1,0:T(8,128)S(1)}, u32[]{:S(2)}, u32[]{:S(2)}) async-start(f32[8,64,128]{2,1,0:T(8,128)} %entries_up.1), calls=%async_computation.2 | async-start | bytes 524288 | tf_op jit(solution)/shard_map/all_to_all | solution.py:433
  90.8 17.6 %all-to-all-start.5 = ((f32[8,40,128]{2,1,0:T(8,128)}), f32[8,40,128]{2,1,0:T(8,128)S(1)}, u32[]{:S(2)}, u32[]{:S(2)}) async-start(f32[8,40,128]{2,1,0:T(8,128)} %totals_down.1), calls=%async_computation.5 | async-start | bytes 327680 | tf_op jit(solution)/shard_map/all_to_all | solution.py:433
  97.9 28.2 %copy-start.8 = (f32[256,128]{1,0:T(8,128)}, f32[256,128]{1,0:T(8,128)S(1)}, u32[]{:S(2)}) copy-start(f32[256,128]{1,0:T(8,128)S(1)} %get-tuple-element.36.gc_near) | copy-start | bytes 393220
  141.9 0.9 copy-start.9
  160.1 10.9 %all-to-all-start.9 = ((f32[8,64,128]{2,1,0:T(8,128)}), f32[8,64,128]{2,1,0:T(8,128)S(1)}, u32[]{:S(2)}, u32[]{:S(2)}) async-start(f32[8,64,128]{2,1,0:T(8,128)} %add_up.1), calls=%async_computation.9 | async-start | bytes 524288 | tf_op jit(solution)/shard_map/all_to_all | solution.py:433

commit v7 on v6

--- a/solution.py
+++ b/solution.py
@@ -195,56 +195,43 @@
         entry = totals_at(dec_ref, i, 2 * size)[branch] * entry + sliced(rec_ref, i, size)[branch]
 
 
-def totals_down(dec_ref, rec_ref, out_ref):
+def totals_down(place_ref, dec_ref, rec_ref, out_ref):
     n, n_g = rec_ref.shape[0], out_ref.shape[0]
     size = WIDTH // n
-    sums, _ = group_sums(dec_ref, rec_ref, False)
-    both = jnp.concatenate(sums, axis=0)
+    (sum_f, sum_b), _ = group_sums(dec_ref, rec_ref, False)
     weight = rec_ref[0, 2 * size :, :]
     for i in range(1, n):
         weight = weight + rec_ref[i, 2 * size :, :]
-    span, part = 2 * size // n_g, weight.shape[0] // n_g
+    part = weight.shape[0] // n_g
     for k in range(n_g):
-        out_ref[k, 0:span, :] = both[k * span : (k + 1) * span, :]
-        out_ref[k, span:, :] = weight[k * part : (k + 1) * part, :]
-
-
-def scan_down(place_ref, dec_ref, rec_ref, out_ref):
-    n_g = rec_ref.shape[0]
-    span = 2 * (dec_ref.shape[1] - 8) // n_g
-    forward = 2 * place_ref[0] < n_g
-    states = [rec_ref[k, 0:span, :] for k in range(n_g)]
-    decays = [totals_at(dec_ref, k, dec_ref.shape[1] - 8) for k in range(n_g)]
-    down, acc = [None] * n_g, jnp.zeros_like(states[0])
-    for k in range(n_g)[::-1]:
-        down[k] = acc
-        acc = decays[k][0] * acc + states[k]
-    up, acc = [None] * n_g, jnp.zeros_like(states[0])
+        out_ref[k, 0:size, :] = jnp.where(place_ref[0] > k, sum_f, sum_b)
+        out_ref[k, size:, :] = weight[k * part : (k + 1) * part, :]
+
+
+def entries_down(place_ref, zdec_ref, zrec_ref, dec_ref, rec_ref, out_ref, w_ref):
+    n_g, n = zrec_ref.shape[0], rec_ref.shape[0]
+    size = WIDTH // n
+    place = place_ref[0]
+    for branch, up in enumerate((False, True)):
+        entry = jnp.zeros((size, LANES), F32)
+        for k in list(range(n_g)) if up else list(range(n_g))[::-1]:
+            passed = place > k if up else place < k
+            after = totals_at(zdec_ref, k, size)[branch] * entry + zrec_ref[k, 0:size, :]
+            entry = jnp.where(passed, after, entry)
+        put_entries(out_ref, branch, up, entry, dec_ref, rec_ref)
+    weight = zrec_ref[0, size:, :]
+    for k in range(1, n_g):
+        weight = weight + zrec_ref[k, size:, :]
     for k in range(n_g):
-        up[k] = acc
-        acc = decays[k][1] * acc + states[k]
-    weight = rec_ref[0, span:, :]
-    for k in range(1, n_g):
-        weight = weight + rec_ref[k, span:, :]
+        w_ref[k, :, :] = weight
+
+
+def weight_copy(rec_ref, out_ref):
+    n_g, part = rec_ref.shape[0], rec_ref.shape[1]
     for k in range(n_g):
-        out_ref[k, 0:span, :] = jnp.where(forward, down[k], up[k])
-        out_ref[k, span:, :] = weight
-
-
-def entries_down(back_ref, dec_ref, rec_ref, out_ref):
-    n_g, n = back_ref.shape[0], rec_ref.shape[0]
-    size = WIDTH // n
-    span = 2 * size // n_g
-    half = n_g // 2
-    entry_f = jnp.concatenate([back_ref[k, 0:span, :] for k in range(half)], axis=0)
-    entry_b = jnp.concatenate([back_ref[k, 0:span, :] for k in range(half, n_g)], axis=0)
-    put_entries(out_ref, 0, False, entry_f, dec_ref, rec_ref)
-    put_entries(out_ref, 1, True, entry_b, dec_ref, rec_ref)
-    part = back_ref.shape[1] - span
-    for k in range(n_g):
-        weight = back_ref[k, span:, :]
-        for i in range(n):
-            out_ref[i, 2 * size + k * part : 2 * size + (k + 1) * part, :] = weight
+        rows = rec_ref[k, :, :]
+        for i in range(out_ref.shape[0]):
+            out_ref[i, k * part : (k + 1) * part, :] = rows
 
 
 def weight_rows(rec_ref, gw_ref):
@@ -252,9 +239,8 @@
     size = WIDTH // n
     for i in range(n):
         for block in range(gw_ref.shape[1] // LANES):
-            at = 2 * size + block * size
             gw_ref[i * size : (i + 1) * size, block * LANES : (block + 1) * LANES] = (
-                rec_ref[i, at : at + size, :] * WEIGHT_SCALE
+                rec_ref[i, block * size : (block + 1) * size, :] * WEIGHT_SCALE
             )
 
 
@@ -371,18 +357,18 @@
     gz_ref[...] = (du_ref[...] * y_ref[...] * sig * (1.0 + z * (1.0 - sig))).astype(BF16)
 
 
-def finish(x_ref, df_ref, db_ref, exit_ref, gb_near, gc_near, out_ref):
+def finish(core_ref, x_ref, df_ref, db_ref, exit_ref, gb_near, gc_near, keep_ref, give_ref):
     cf, be, end_f, end_b = columns(df_ref[...], db_ref[...])
     x = x_ref[...].astype(F32)
     exit_f, exit_b = take_slices(exit_ref)
     grad_b = gb_near[...] + dot_both(x * spread(jnp.exp(end_f - cf)), exit_f, 1, 0)
     grad_b = grad_b + dot_both(x * spread(jnp.exp(be)), exit_b, 1, 0)
-    grad_c = gc_near[...]
-    n = out_ref.shape[0]
-    size = FRAMES // n
-    for i in range(n):
-        out_ref[i, 0:size, :] = grad_b[i * size : (i + 1) * size, :]
-        out_ref[i, size : 2 * size, :] = grad_c[i * size : (i + 1) * size, :]
+    half = FRAMES // 2
+    first = core_ref[0] == 0
+    for i, grad in enumerate((grad_b, gc_near[...])):
+        at = slice(i * half, (i + 1) * half)
+        keep_ref[at, :] = jnp.where(first, grad[:half, :], grad[half:, :])
+        give_ref[at, :] = jnp.where(first, grad[half:, :], grad[:half, :])
 
 
 def finish_x(b_ref, df_ref, db_ref, exit_ref, gx_near, gx_ref):
@@ -393,21 +379,17 @@
     gx_ref[...] = (gx + spread(jnp.exp(be)) * dot_right(b, exit_b, 1, 1)).astype(BF16)
 
 
-def add_up(rec_ref, out_ref):
-    n = rec_ref.shape[0]
-    total = rec_ref[0, :, :]
-    for i in range(1, n):
-        total = total + rec_ref[i, :, :]
-    for i in range(n):
-        out_ref[i, :, :] = total
-
-
-def deal_out(rec_ref, gb_ref, gc_ref):
-    n = rec_ref.shape[0]
-    size = FRAMES // n
-    for i in range(n):
-        gb_ref[i * size : (i + 1) * size, :] = rec_ref[i, 0:size, :]
-        gc_ref[i * size : (i + 1) * size, :] = rec_ref[i, size : 2 * size, :]
+def add_two(a_ref, b_ref, out_ref):
+    out_ref[...] = a_ref[...] + b_ref[...]
+
+
+def deal_out(core_ref, own_ref, other_ref, gb_ref, gc_ref):
+    half = FRAMES // 2
+    first = core_ref[0] == 0
+    for i, ref in enumerate((gb_ref, gc_ref)):
+        at = slice(i * half, (i + 1) * half)
+        ref[0:half, :] = jnp.where(first, own_ref[at, :], other_ref[at, :])
+        ref[half:, :] = jnp.where(first, other_ref[at, :], own_ref[at, :])
 
 
 VMEM = pl.BlockSpec(memory_space=pltpu.VMEM)
@@ -433,6 +415,10 @@
     return lax.all_to_all(a, axis, 0, 0, tiled=True)
 
 
+def swapped(a, mask, n_h):
+    return lax.ppermute(a, "head", [(i, i ^ mask) for i in range(n_h)])
+
+
 def body(x_in, gate_in, b_in, c_in, decay_fwd, decay_bwd, skip_gain, norm_gain, w_out, d_out):
     n_hi, n_lo, n_x, n_h = (lax.axis_size(axis) for axis in ("z_hi", "z_lo", "x", "head"))
     group = ("z_lo", "x")
@@ -475,27 +461,36 @@
         skip_gain, x_in, b_in, c_in, *decays, dy, entries, scalars=1,
     )
     grad_z = call(gate_gradient, "gate_gradient", [(square, BF16)], du, y, gate_in)
-    rows_z = (2 * size + weights) // n_hi
-    sent = call(totals_down, "totals_down", [((n_hi, rows_z, LANES), F32)], rec1, rec2)
+    part = weights // n_hi
+    sent = call(totals_down, "totals_down", [((n_hi, size + part, LANES), F32)], place, rec1, rec2, scalars=1)
     recz2 = exchange(sent, "z_hi")
     recz2, gx_near, gb_near, gc_near, grad_z = lax.optimization_barrier(
         (recz2, gx_near, gb_near, gc_near, grad_z)
     )
-    sent = call(scan_down, "scan_down", [((n_hi, rows_z, LANES), F32)], place, recz1, recz2, scalars=1)
-    back = exchange(sent, "z_hi")
-    sent = call(entries_down, "entries_down", [((n, 2 * size + weights, LANES), F32)], back, rec1, rec2)
+    sent, weight = call(
+        entries_down, "entries_down", [((n, 2 * size, LANES), F32), ((n_hi, part, LANES), F32)],
+        place, recz1, recz2, rec1, rec2, scalars=1,
+    )
     exits = exchange(sent, group)
-    grad_w = call(weight_rows, "weight_rows", [((WIDTH, model), F32)], exits)
-
-    chunk = 2 * FRAMES // n_h
-    sent = call(
-        finish, "finish", [((n_h, chunk, LANES), F32)], x_in, *decays, exits, gb_near, gc_near
-    )
+
+    exits, weight = lax.optimization_barrier((exits, weight))
+    weight = exchange(weight, "z_hi")
+
+    core = (lax.axis_index("head") % 2).astype(jnp.int32).reshape(1)
+    half = [((FRAMES, STATE), F32)]
+    own, give = call(finish, "finish", half * 2, core, x_in, *decays, exits, gb_near, gc_near, scalars=1)
+    own = call(add_two, "add_core", half, own, swapped(give, 1, n_h))
+    own = call(add_two, "add_y", half, own, swapped(own, 2, n_h))
+    weight, own = lax.optimization_barrier((weight, own))
+
+    weight = call(weight_copy, "weight_copy", [((n, weights, LANES), F32)], weight)
+    weight = exchange(weight, group)
+    grad_w = call(weight_rows, "weight_rows", [((WIDTH, model), F32)], weight)
+
+    own = call(add_two, "add_y", half, own, swapped(own, 6, n_h))
+    other = swapped(own, 1, n_h)
     grad_x = call(finish_x, "finish_x", [(square, BF16)], b_in, *decays, exits, gx_near)
-    rec = exchange(sent, "head")
-    sent = call(add_up, "add_up", [((n_h, chunk, LANES), F32)], rec)
-    rec = exchange(sent, "head")
-    grad_b, grad_c = call(deal_out, "deal_out", [((FRAMES, STATE), F32)] * 2, rec)
+    grad_b, grad_c = call(deal_out, "deal_out", half * 2, core, own, other, scalars=1)
     return grad_x, grad_z, grad_b, grad_c, grad_w
 
 

time: 172 us -> 163 us (0.948)
  blocking collectives: 110 us -> 69.8 us
  starting transfers between devices: 17.5 us -> 39.3 us
  waiting for transfers between devices: 24.4 us -> 33.3 us
    all_to_all x6 -> x4, blocking collectives: 110 us -> 69.8 us  [exchange(): return lax.all_to_all(a, axis, 0, 0, tiled=True)]
    ppermute x0 -> x4, starting transfers between devices: none -> 15.1 us  [swapped(): return lax.ppermute(a, 'head', [(i, i ^ mask) for i in range(n_h)])]
    ppermute x0 -> x4, waiting for transfers between devices: none -> 9.5 us  [swapped(): return lax.ppermute(a, 'head', [(i, i ^ mask) for i in range(n_h)])]
    all_to_all x4 -> x5, starting transfers between devices: 17.5 us -> 24.2 us  [exchange(): return lax.all_to_all(a, axis, 0, 0, tiled=True)]
    pallas_call x16 -> x18, Pallas kernels: 17.9 us -> 18.8 us  [call(): pl.pallas_call(kernel, name=name, out_shape=shapes[0] if single else tupl...]
    all_to_all x4 -> x5, waiting for transfers between devices: 24.4 us -> 23.8 us  [exchange(): return lax.all_to_all(a, axis, 0, 0, tiled=True)]
  transfers between devices with their start and end apart: 4 -> 9, of which waited for: 4 -> 7; matrix products, arithmetic and copies ran while one was open for 0% -> 0% of each run, Pallas kernels for 5% -> 6%
where the time goes in v7:
time: 163 us; the launch traced here: 162 us
  blocking collectives  69.8 us (43%)
  starting transfers between devices  39.3 us (24%)
  waiting for transfers between devices  33.3 us (20%)
  Pallas kernels  18.8 us (12%)
    all_to_all x4, blocking collectives, exchange(): return lax.all_to_all(a, axis, 0, 0, tiled=True)  69.8 us
    all_to_all x5, starting transfers between devices, exchange(): return lax.all_to_all(a, axis, 0, 0, tiled=True)  24.2 us
    all_to_all x5, waiting for transfers between devices, exchange(): return lax.all_to_all(a, axis, 0, 0, tiled=True)  23.8 us
    pallas_call x18, Pallas kernels, call(): pl.pallas_call(kernel, name=name, out_shape=shapes[0] if single else tupl...  18.8 us
    ppermute x4, starting transfers between devices, swapped(): return lax.ppermute(a, 'head', [(i, i ^ mask) for i in range(n_h)])  15.1 us
    ppermute x4, waiting for transfers between devices, swapped(): return lax.ppermute(a, 'head', [(i, i ^ mask) for i in range(n_h)])  9.5 us
  transfers between devices with their start and end apart: 9, of which 7 were waited for; matrix products, arithmetic and copies ran while one was open for 0% of the time, Pallas kernels for 6%

profile of v7, /device:TPU:1, one launch (start us, length us, event | category | flops | bytes accessed | tf_op | source)
XLA Modules:
  0.0 162.2 jit_solution(14097058497825218968)
XLA Ops:
  0.6 2.8 %local_states.1 = f32[8,72,128]{2,1,0:T(8,128)} custom-call(bf16[256,256]{1,0:T(8,128)(2,1)} %x_ref.5, bf16[256,128]{1,0:T(8,128)(2,1)} %b_ref.5, f32[4,256]{1,0:T(4,128)} %df_ref.11, f32[4,256]{1,0:T(4,128)} %db_ref.11), custom_call_target="tpu_custom_call" | custom-call | tf_op jit(solution)/shard_map/local_states/pallas_call | solution.py:403
  3.5 6.3 %all-to-all-start = ((f32[8,72,128]{2,1,0:T(8,128)}), f32[8,72,128]{2,1,0:T(8,128)S(1)}, u32[]{:S(2)}, u32[]{:S(2)}) async-start(f32[8,72,128]{2,1,0:T(8,128)} %local_states.1), calls=%async_computation | async-start | bytes 589824 | tf_op jit(solution)/shard_map/all_to_all | solution.py:415
  9.8 6.2 %all-to-all-done.rec_ref.dec_ref = f32[8,72,128]{2,1,0:T(8,128)S(1)} async-done(((f32[8,72,128]{2,1,0:T(8,128)}), f32[8,72,128]{2,1,0:T(8,128)S(1)}, u32[]{:S(2)}, u32[]{:S(2)}) %all-to-all-start) | async-done | bytes 294944 | tf_op jit(solution)/shard_map/all_to_all | solution.py:415
  16.1 28.0 %all_to_all.45.zrec_ref.zdec_ref = f32[8,40,128]{2,1,0:T(8,128)S(1)} all-to-all(f32[8,40,128]{2,1,0:T(8,128)S(1)} %totals_up.1), channel_id=1, replica_groups=mesh['z_hi'=8,'z_lo'=2,'x'=4,'head'=8] {'z_hi'}, dimensions={0} | all-to-all | bytes 327680 | tf_op jit(solution)/shard_map/all_to_all | solution.py:415
  44.1 0.8 entries_up.1
  44.9 3.4 %all-to-all-start.2 = ((f32[8,64,128]{2,1,0:T(8,128)}), f32[8,64,128]{2,1,0:T(8,128)S(1)}, u32[]{:S(2)}, u32[]{:S(2)}) async-start(f32[8,64,128]{2,1,0:T(8,128)} %entries_up.1), calls=%async_computation.2 | async-start | bytes 524288 | tf_op jit(solution)/shard_map/all_to_all | solution.py:415
  48.4 2.1 %near_outputs.1 = (f32[256,256]{1,0:T(8,128)S(1)}, f32[256,256]{1,0:T(8,128)S(1)}) custom-call(f32[4]{0:T(128)S(1)} %copy-done.9, bf16[256,256]{1,0:T(8,128)(2,1)S(1)} %copy-done.1, bf16[256,128]{1,0:T(8,128)(2,1)S(1)} %copy-done.3, bf16[256,128]{1,0:T(8,128)(2,1)S(1)} %copy-done.4, f32[4,256]{1,0:T(4,128)S(1)} %copy-done.6, f32[4,256]{1,0:T(4,128)S(1)} %copy-done.7, ...), custom_call_target="tpu_custom_call" | custom-call | tf_op jit(solution)/shard_map/near_outputs/pallas_call | solution.py:403
  50.5 3.8 %all-to-all-done.2.ent_ref = f32[8,64,128]{2,1,0:T(8,128)S(1)} async-done(((f32[8,64,128]{2,1,0:T(8,128)}), f32[8,64,128]{2,1,0:T(8,128)S(1)}, u32[]{:S(2)}, u32[]{:S(2)}) %all-to-all-start.2) | async-done | bytes 262176 | tf_op jit(solution)/shard_map/all_to_all | solution.py:415
  54.3 1.0 outputs.1
  55.3 13.7 %all_to_all.46.sums_ref = f32[8,8,128]{2,1,0:T(8,128)S(1)} all-to-all(f32[8,8,128]{2,1,0:T(8,128)S(1)} %get-tuple-element.32), channel_id=1, replica_groups=mesh['z_hi'=8,'z_lo'=2,'x'=4,'head'=8] {'head'}, dimensions={0} | all-to-all | bytes 65536 | tf_op jit(solution)/shard_map/all_to_all | solution.py:415
  69.0 1.4 gradients.1
  70.4 19.6 %all_to_all.47.rec_ref = f32[8,320,128]{2,1,0:T(8,128)S(1)} all-to-all(f32[8,320,128]{2,1,0:T(8,128)S(1)} %get-tuple-element.34), channel_id=1, replica_groups=mesh['z_hi'=8,'z_lo'=2,'x'=4,'head'=8] {'z_lo','x'}, dimensions={0} | all-to-all | bytes 2621440 | tf_op jit(solution)/shard_map/all_to_all | solution.py:415
  90.0 0.8 totals_down.1
  90.8 3.4 %all-to-all-start.5 = ((f32[8,64,128]{2,1,0:T(8,128)}), f32[8,64,128]{2,1,0:T(8,128)S(1)}, u32[]{:S(2)}, u32[]{:S(2)}) async-start(f32[8,64,128]{2,1,0:T(8,128)} %totals_down.1), calls=%async_computation.5 | async-start | bytes 524288 | tf_op jit(solution)/shard_map/all_to_all | solution.py:415
  94.2 0.7 gate_gradient.1
  95.0 3.0 %near_gradients.1 = (f32[256,256]{1,0:T(8,128)S(1)}, f32[256,128]{1,0:T(8,128)S(1)}, f32[256,128]{1,0:T(8,128)S(1)}) custom-call(f32[4]{0:T(128)S(1)} %copy-done.9, bf16[256,256]{1,0:T(8,128)(2,1)S(1)} %copy-done.1, bf16[256,128]{1,0:T(8,128)(2,1)S(1)} %copy-done.3, bf16[256,128]{1,0:T(8,128)(2,1)S(1)} %copy-done.4, f32[4,256]{1,0:T(4,128)S(1)} %copy-done.6, ...), custom_call_target="tpu_custom_call" | custom-call | tf_op jit(solution)/shard_map/near_gradients/pallas_call | solution.py:403
  98.0 13.8 %all-to-all-done.5.zrec_ref = f32[8,64,128]{2,1,0:T(8,128)S(1)} async-done(((f32[8,64,128]{2,1,0:T(8,128)}), f32[8,64,128]{2,1,0:T(8,128)S(1)}, u32[]{:S(2)}, u32[]{:S(2)}) %all-to-all-start.5) | async-done | bytes 262176 | tf_op jit(solution)/shard_map/all_to_all | solution.py:415
  112.4 8.5 %all_to_all.48.exit_ref = f32[8,64,128]{2,1,0:T(8,128)S(1)} all-to-all(f32[8,64,128]{2,1,0:T(8,128)S(1)} %get-tuple-element.41), channel_id=1, replica_groups=mesh['z_hi'=8,'z_lo'=2,'x'=4,'head'=8] {'z_lo','x'}, dimensions={0} | all-to-all | bytes 524288 | tf_op jit(solution)/shard_map/all_to_all | solution.py:415
  120.9 7.2 %all-to-all-start.7 = ((f32[8,32,128]{2,1,0:T(8,128)}), f32[8,32,128]{2,1,0:T(8,128)S(1)}, u32[]{:S(2)}, u32[]{:S(2)}) async-start(f32[8,32,128]{2,1,0:T(8,128)} %get-tuple-element.46), calls=%async_computation.7 | async-start | bytes 262144 | tf_op jit(solution)/shard_map/all_to_all | solution.py:415
  128.1 1.2 finish.1
  129.2 4.2 %collective-permute-start = (f32[256,128]{1,0:T(8,128)S(1)}, f32[256,128]{1,0:T(8,128)S(1)}, u32[]{:S(2)}, u32[]{:S(2)}) collective-permute-start(f32[256,128]{1,0:T(8,128)S(1)} %get-tuple-element.50), channel_id=1, source_target_pairs={{0,1},{1,0},{2,3},{3,2},{4,5},{5,4},{6,7},{7,6},{8,9},{9,8},{10,11... | collective-permute-start | bytes 393224 | tf_op jit(solution)/shard_map/ppermute | solution.py:419
  133.4 1.0 collective-permute-done.b_ref
  134.4 2.2 %collective-permute-start.1 = (f32[256,128]{1,0:T(8,128)S(1)}, f32[256,128]{1,0:T(8,128)S(1)}, u32[]{:S(2)}, u32[]{:S(2)}) collective-permute-start(f32[256,128]{1,0:T(8,128)S(1)} %add_core.1.a_ref), channel_id=1, source_target_pairs={{0,2},{1,3},{2,0},{3,1},{4,6},{5,7},{6,4},{7,5},{8,10},{9,11},{10,... | collective-permute-start | bytes 393224 | tf_op jit(solution)/shard_map/ppermute | solution.py:419
  136.6 4.4 %collective-permute-done.1.b_ref = f32[256,128]{1,0:T(8,128)S(1)} collective-permute-done((f32[256,128]{1,0:T(8,128)S(1)}, f32[256,128]{1,0:T(8,128)S(1)}, u32[]{:S(2)}, u32[]{:S(2)}) %collective-permute-start.1) | collective-permute-done | bytes 131104 | tf_op jit(solution)/shard_map/ppermute | solution.py:419
  141.1 1.0 weight_copy.1
  142.1 3.8 %all-to-all-start.8 = ((f32[8,256,128]{2,1,0:T(8,128)}), f32[8,256,128]{2,1,0:T(8,128)S(1)}, u32[]{:S(2)}, u32[]{:S(2)}) async-start(f32[8,256,128]{2,1,0:T(8,128)} %weight_copy.1), calls=%async_computation.8 | async-start | bytes 2097152 | tf_op jit(solution)/shard_map/all_to_all | solution.py:415
  146.0 2.8 %collective-permute-start.2 = (f32[256,128]{1,0:T(8,128)S(1)}, f32[256,128]{1,0:T(8,128)S(1)}, u32[]{:S(2)}, u32[]{:S(2)}) collective-permute-start(f32[256,128]{1,0:T(8,128)S(1)} %add_y.2.a_ref), channel_id=1, source_target_pairs={{0,6},{1,7},{2,4},{3,5},{4,2},{5,3},{6,0},{7,1},{8,14},{9,15},{10,... | collective-permute-start | bytes 393224 | tf_op jit(solution)/shard_map/ppermute | solution.py:419
  148.8 4.1 %collective-permute-done.2.b_ref = f32[256,128]{1,0:T(8,128)S(1)} collective-permute-done((f32[256,128]{1,0:T(8,128)S(1)}, f32[256,128]{1,0:T(8,128)S(1)}, u32[]{:S(2)}, u32[]{:S(2)}) %collective-permute-start.2) | collective-permute-done | bytes 131104 | tf_op jit(solution)/shard_map/ppermute | solution.py:419
  152.9 6.0 %collective-permute-start.3 = (f32[256,128]{1,0:T(8,128)S(1)}, f32[256,128]{1,0:T(8,128)S(1)}, u32[]{:S(2)}, u32[]{:S(2)}) collective-permute-start(f32[256,128]{1,0:T(8,128)S(1)} %add_y.3.own_ref), channel_id=1, source_target_pairs={{0,1},{1,0},{2,3},{3,2},{4,5},{5,4},{6,7},{7,6},{8,9},{9,8},{10,11... | collective-permute-start | bytes 393224 | tf_op jit(solution)/shard_map/ppermute | solution.py:419
  158.9 1.5 finish_x.1
  160.4 0.7 deal_out.1
  161.2 1.0 weight_rows.1
  (28 shorter events, 0.9 us)
Async XLA Ops:
  3.4 44.9 %copy-start = (bf16[256,1024]{1,0:T(8,128)(2,1)S(1)}, bf16[256,1024]{1,0:T(8,128)(2,1)}, u32[]{:S(2)}) copy-start(bf16[256,1024]{1,0:T(8,128)(2,1)} %do_ref.3) | copy-start | bytes 1572868
  3.4 44.9 %copy-start.1 = (bf16[256,256]{1,0:T(8,128)(2,1)S(1)}, bf16[256,256]{1,0:T(8,128)(2,1)}, u32[]{:S(2)}) copy-start(bf16[256,256]{1,0:T(8,128)(2,1)} %x_ref.5) | copy-start | bytes 393220
  3.4 44.9 %copy-start.3 = (bf16[256,128]{1,0:T(8,128)(2,1)S(1)}, bf16[256,128]{1,0:T(8,128)(2,1)}, u32[]{:S(2)}) copy-start(bf16[256,128]{1,0:T(8,128)(2,1)} %b_ref.5) | copy-start | bytes 196612
  3.4 44.9 %copy-start.4 = (bf16[256,128]{1,0:T(8,128)(2,1)S(1)}, bf16[256,128]{1,0:T(8,128)(2,1)}, u32[]{:S(2)}) copy-start(bf16[256,128]{1,0:T(8,128)(2,1)} %c_ref.7) | copy-start | bytes 196612
  3.4 44.9 %copy-start.5 = (bf16[256,1024]{1,0:T(8,128)(2,1)S(1)}, bf16[256,1024]{1,0:T(8,128)(2,1)}, u32[]{:S(2)}) copy-start(bf16[256,1024]{1,0:T(8,128)(2,1)} %w_ref.1) | copy-start | bytes 1572868
  3.4 44.9 %copy-start.6 = (f32[4,256]{1,0:T(4,128)S(1)}, f32[4,256]{1,0:T(4,128)}, u32[]{:S(2)}) copy-start(f32[4,256]{1,0:T(4,128)} %df_ref.11) | copy-start | bytes 12292
  3.5 44.9 %copy-start.7 = (f32[4,256]{1,0:T(4,128)S(1)}, f32[4,256]{1,0:T(4,128)}, u32[]{:S(2)}) copy-start(f32[4,256]{1,0:T(4,128)} %db_ref.11) | copy-start | bytes 12292
  3.5 44.9 %copy-start.8 = (f32[256]{0:T(256)S(1)}, f32[256]{0:T(256)}, u32[]{:S(2)}) copy-start(f32[256]{0:T(256)} %param.17) | copy-start | bytes 3076
  3.5 44.9 %copy-start.9 = (f32[4]{0:T(128)S(1)}, f32[4]{0:T(128)}, u32[]{:S(2)}) copy-start(f32[4]{0:T(128)} %skip_ref.3) | copy-start | bytes 52
  3.5 12.6 %all-to-all-start = ((f32[8,72,128]{2,1,0:T(8,128)}), f32[8,72,128]{2,1,0:T(8,128)S(1)}, u32[]{:S(2)}, u32[]{:S(2)}) async-start(f32[8,72,128]{2,1,0:T(8,128)} %local_states.1), calls=%async_computation | async-start | bytes 589824 | tf_op jit(solution)/shard_map/all_to_all | solution.py:415
  44.1 10.2 %copy-start.2 = (bf16[256,256]{1,0:T(8,128)(2,1)S(1)}, bf16[256,256]{1,0:T(8,128)(2,1)}, u32[]{:S(2)}) copy-start(bf16[256,256]{1,0:T(8,128)(2,1)} %z_ref.5) | copy-start | bytes 393220
  44.9 9.4 %all-to-all-start.2 = ((f32[8,64,128]{2,1,0:T(8,128)}), f32[8,64,128]{2,1,0:T(8,128)S(1)}, u32[]{:S(2)}, u32[]{:S(2)}) async-start(f32[8,64,128]{2,1,0:T(8,128)} %entries_up.1), calls=%async_computation.2 | async-start | bytes 524288 | tf_op jit(solution)/shard_map/all_to_all | solution.py:415
  90.8 20.9 %all-to-all-start.5 = ((f32[8,64,128]{2,1,0:T(8,128)}), f32[8,64,128]{2,1,0:T(8,128)S(1)}, u32[]{:S(2)}, u32[]{:S(2)}) async-start(f32[8,64,128]{2,1,0:T(8,128)} %totals_down.1), calls=%async_computation.5 | async-start | bytes 524288 | tf_op jit(solution)/shard_map/all_to_all | solution.py:415
  120.9 20.2 %all-to-all-start.7 = ((f32[8,32,128]{2,1,0:T(8,128)}), f32[8,32,128]{2,1,0:T(8,128)S(1)}, u32[]{:S(2)}, u32[]{:S(2)}) async-start(f32[8,32,128]{2,1,0:T(8,128)} %get-tuple-element.46), calls=%async_computation.7 | async-start | bytes 262144 | tf_op jit(solution)/shard_map/all_to_all | solution.py:415
  129.2 5.1 %collective-permute-start = (f32[256,128]{1,0:T(8,128)S(1)}, f32[256,128]{1,0:T(8,128)S(1)}, u32[]{:S(2)}, u32[]{:S(2)}) collective-permute-start(f32[256,128]{1,0:T(8,128)S(1)} %get-tuple-element.50), channel_id=1, source_target_pairs={{0,1},{1,0},{2,3},{3,2},{4,5},{5,4},{6,7},{7,6},{8,9},{9,8},{10,11... | collective-permute-start | bytes 393224 | tf_op jit(solution)/shard_map/ppermute | solution.py:419
  134.4 6.6 %collective-permute-start.1 = (f32[256,128]{1,0:T(8,128)S(1)}, f32[256,128]{1,0:T(8,128)S(1)}, u32[]{:S(2)}, u32[]{:S(2)}) collective-permute-start(f32[256,128]{1,0:T(8,128)S(1)} %add_core.1.a_ref), channel_id=1, source_target_pairs={{0,2},{1,3},{2,0},{3,1},{4,6},{5,7},{6,4},{7,5},{8,10},{9,11},{10,... | collective-permute-start | bytes 393224 | tf_op jit(solution)/shard_map/ppermute | solution.py:419
  142.1 19.0 %all-to-all-start.8 = ((f32[8,256,128]{2,1,0:T(8,128)}), f32[8,256,128]{2,1,0:T(8,128)S(1)}, u32[]{:S(2)}, u32[]{:S(2)}) async-start(f32[8,256,128]{2,1,0:T(8,128)} %weight_copy.1), calls=%async_computation.8 | async-start | bytes 2097152 | tf_op jit(solution)/shard_map/all_to_all | solution.py:415
  146.0 6.9 %collective-permute-start.2 = (f32[256,128]{1,0:T(8,128)S(1)}, f32[256,128]{1,0:T(8,128)S(1)}, u32[]{:S(2)}, u32[]{:S(2)}) collective-permute-start(f32[256,128]{1,0:T(8,128)S(1)} %add_y.2.a_ref), channel_id=1, source_target_pairs={{0,6},{1,7},{2,4},{3,5},{4,2},{5,3},{6,0},{7,1},{8,14},{9,15},{10,... | collective-permute-start | bytes 393224 | tf_op jit(solution)/shard_map/ppermute | solution.py:419
  152.9 7.5 %collective-permute-start.3 = (f32[256,128]{1,0:T(8,128)S(1)}, f32[256,128]{1,0:T(8,128)S(1)}, u32[]{:S(2)}, u32[]{:S(2)}) collective-permute-start(f32[256,128]{1,0:T(8,128)S(1)} %add_y.3.own_ref), channel_id=1, source_target_pairs={{0,1},{1,0},{2,3},{3,2},{4,5},{5,4},{6,7},{7,6},{8,9},{9,8},{10,11... | collective-permute-start | bytes 393224 | tf_op jit(solution)/shard_map/ppermute | solution.py:419

commit v8 on v7

--- a/solution.py
+++ b/solution.py
@@ -383,6 +383,10 @@
     out_ref[...] = a_ref[...] + b_ref[...]
 
 
+def add_four(a_ref, b_ref, c_ref, d_ref, out_ref):
+    out_ref[...] = (a_ref[...] + b_ref[...]) + (c_ref[...] + d_ref[...])
+
+
 def deal_out(core_ref, own_ref, other_ref, gb_ref, gc_ref):
     half = FRAMES // 2
     first = core_ref[0] == 0
@@ -480,14 +484,14 @@
     half = [((FRAMES, STATE), F32)]
     own, give = call(finish, "finish", half * 2, core, x_in, *decays, exits, gb_near, gc_near, scalars=1)
     own = call(add_two, "add_core", half, own, swapped(give, 1, n_h))
-    own = call(add_two, "add_y", half, own, swapped(own, 2, n_h))
-    weight, own = lax.optimization_barrier((weight, own))
+    across = [swapped(own, mask, n_h) for mask in (4, 2)]
+    weight, own, *across = lax.optimization_barrier((weight, own, *across))
 
     weight = call(weight_copy, "weight_copy", [((n, weights, LANES), F32)], weight)
     weight = exchange(weight, group)
     grad_w = call(weight_rows, "weight_rows", [((WIDTH, model), F32)], weight)
 
-    own = call(add_two, "add_y", half, own, swapped(own, 6, n_h))
+    own = call(add_four, "add_y", half, own, across[1], across[0], swapped(own, 6, n_h))
     other = swapped(own, 1, n_h)
     grad_x = call(finish_x, "finish_x", [(square, BF16)], b_in, *decays, exits, gx_near)
     grad_b, grad_c = call(deal_out, "deal_out", half * 2, core, own, other, scalars=1)

time: 163 us -> 165 us (1.012)
  starting transfers between devices: 39.3 us -> 42.1 us
    ppermute x4 -> x5, starting transfers between devices: 15.1 us -> 18.2 us  [swapped(): return lax.ppermute(a, 'head', [(i, i ^ mask) for i in range(n_h)])]
    ppermute x4 -> x5, waiting for transfers between devices: 9.5 us -> 8.43 us  [swapped(): return lax.ppermute(a, 'head', [(i, i ^ mask) for i in range(n_h)])]
    pallas_call x18 -> x17, Pallas kernels: 18.8 us -> 18.8 us  [call(): pl.pallas_call(kernel, name=name, out_shape=shapes[0] if single else tupl...]
  transfers between devices with their start and end apart: 9 -> 10, of which waited for: 7 -> 8; matrix products, arithmetic and copies ran while one was open for 0% -> 0% of each run, Pallas kernels for 6% -> 6%
where the time goes in v8:
time: 165 us; the launch traced here: 164 us
  blocking collectives  69.8 us (42%)
  starting transfers between devices  42.1 us (26%)
  waiting for transfers between devices  32.2 us (20%)
  Pallas kernels  18.8 us (11%)
    all_to_all x4, blocking collectives, exchange(): return lax.all_to_all(a, axis, 0, 0, tiled=True)  69.8 us
    all_to_all x5, starting transfers between devices, exchange(): return lax.all_to_all(a, axis, 0, 0, tiled=True)  23.9 us
    all_to_all x5, waiting for transfers between devices, exchange(): return lax.all_to_all(a, axis, 0, 0, tiled=True)  23.8 us
    pallas_call x17, Pallas kernels, call(): pl.pallas_call(kernel, name=name, out_shape=shapes[0] if single else tupl...  18.8 us
    ppermute x5, starting transfers between devices, swapped(): return lax.ppermute(a, 'head', [(i, i ^ mask) for i in range(n_h)])  18.2 us
    ppermute x5, waiting for transfers between devices, swapped(): return lax.ppermute(a, 'head', [(i, i ^ mask) for i in range(n_h)])  8.43 us
  transfers between devices with their start and end apart: 10, of which 8 were waited for; matrix products, arithmetic and copies ran while one was open for 0% of the time, Pallas kernels for 6%

profile of v8, /device:TPU:1, one launch (start us, length us, event | category | flops | bytes accessed | tf_op | source)
XLA Modules:
  0.0 163.9 jit_solution(4726046852215312611)
XLA Ops:
  0.6 2.8 %local_states.1 = f32[8,72,128]{2,1,0:T(8,128)} custom-call(bf16[256,256]{1,0:T(8,128)(2,1)} %x_ref.5, bf16[256,128]{1,0:T(8,128)(2,1)} %b_ref.5, f32[4,256]{1,0:T(4,128)} %df_ref.11, f32[4,256]{1,0:T(4,128)} %db_ref.11), custom_call_target="tpu_custom_call" | custom-call | tf_op jit(solution)/shard_map/local_states/pallas_call | solution.py:407
  3.5 6.3 %all-to-all-start = ((f32[8,72,128]{2,1,0:T(8,128)}), f32[8,72,128]{2,1,0:T(8,128)S(1)}, u32[]{:S(2)}, u32[]{:S(2)}) async-start(f32[8,72,128]{2,1,0:T(8,128)} %local_states.1), calls=%async_computation | async-start | bytes 589824 | tf_op jit(solution)/shard_map/all_to_all | solution.py:419
  9.8 6.2 %all-to-all-done.rec_ref.dec_ref = f32[8,72,128]{2,1,0:T(8,128)S(1)} async-done(((f32[8,72,128]{2,1,0:T(8,128)}), f32[8,72,128]{2,1,0:T(8,128)S(1)}, u32[]{:S(2)}, u32[]{:S(2)}) %all-to-all-start) | async-done | bytes 294944 | tf_op jit(solution)/shard_map/all_to_all | solution.py:419
  16.1 28.0 %all_to_all.45.zrec_ref.zdec_ref = f32[8,40,128]{2,1,0:T(8,128)S(1)} all-to-all(f32[8,40,128]{2,1,0:T(8,128)S(1)} %totals_up.1), channel_id=1, replica_groups=mesh['z_hi'=8,'z_lo'=2,'x'=4,'head'=8] {'z_hi'}, dimensions={0} | all-to-all | bytes 327680 | tf_op jit(solution)/shard_map/all_to_all | solution.py:419
  44.1 0.8 entries_up.1
  44.9 3.4 %all-to-all-start.2 = ((f32[8,64,128]{2,1,0:T(8,128)}), f32[8,64,128]{2,1,0:T(8,128)S(1)}, u32[]{:S(2)}, u32[]{:S(2)}) async-start(f32[8,64,128]{2,1,0:T(8,128)} %entries_up.1), calls=%async_computation.2 | async-start | bytes 524288 | tf_op jit(solution)/shard_map/all_to_all | solution.py:419
  48.4 2.1 %near_outputs.1 = (f32[256,256]{1,0:T(8,128)S(1)}, f32[256,256]{1,0:T(8,128)S(1)}) custom-call(f32[4]{0:T(128)S(1)} %copy-done.9, bf16[256,256]{1,0:T(8,128)(2,1)S(1)} %copy-done.1, bf16[256,128]{1,0:T(8,128)(2,1)S(1)} %copy-done.3, bf16[256,128]{1,0:T(8,128)(2,1)S(1)} %copy-done.4, f32[4,256]{1,0:T(4,128)S(1)} %copy-done.6, f32[4,256]{1,0:T(4,128)S(1)} %copy-done.7, ...), custom_call_target="tpu_custom_call" | custom-call | tf_op jit(solution)/shard_map/near_outputs/pallas_call | solution.py:407
  50.5 3.8 %all-to-all-done.2.ent_ref = f32[8,64,128]{2,1,0:T(8,128)S(1)} async-done(((f32[8,64,128]{2,1,0:T(8,128)}), f32[8,64,128]{2,1,0:T(8,128)S(1)}, u32[]{:S(2)}, u32[]{:S(2)}) %all-to-all-start.2) | async-done | bytes 262176 | tf_op jit(solution)/shard_map/all_to_all | solution.py:419
  54.3 1.0 outputs.1
  55.3 13.7 %all_to_all.46.sums_ref = f32[8,8,128]{2,1,0:T(8,128)S(1)} all-to-all(f32[8,8,128]{2,1,0:T(8,128)S(1)} %get-tuple-element.34), channel_id=1, replica_groups=mesh['z_hi'=8,'z_lo'=2,'x'=4,'head'=8] {'head'}, dimensions={0} | all-to-all | bytes 65536 | tf_op jit(solution)/shard_map/all_to_all | solution.py:419
  69.0 1.4 gradients.1
  70.4 19.6 %all_to_all.47.rec_ref = f32[8,320,128]{2,1,0:T(8,128)S(1)} all-to-all(f32[8,320,128]{2,1,0:T(8,128)S(1)} %get-tuple-element.36), channel_id=1, replica_groups=mesh['z_hi'=8,'z_lo'=2,'x'=4,'head'=8] {'z_lo','x'}, dimensions={0} | all-to-all | bytes 2621440 | tf_op jit(solution)/shard_map/all_to_all | solution.py:419
  90.0 0.8 totals_down.1
  90.8 3.4 %all-to-all-start.5 = ((f32[8,64,128]{2,1,0:T(8,128)}), f32[8,64,128]{2,1,0:T(8,128)S(1)}, u32[]{:S(2)}, u32[]{:S(2)}) async-start(f32[8,64,128]{2,1,0:T(8,128)} %totals_down.1), calls=%async_computation.5 | async-start | bytes 524288 | tf_op jit(solution)/shard_map/all_to_all | solution.py:419
  94.2 0.7 gate_gradient.1
  95.0 3.0 %near_gradients.1 = (f32[256,256]{1,0:T(8,128)S(1)}, f32[256,128]{1,0:T(8,128)S(1)}, f32[256,128]{1,0:T(8,128)S(1)}) custom-call(f32[4]{0:T(128)S(1)} %copy-done.9, bf16[256,256]{1,0:T(8,128)(2,1)S(1)} %copy-done.1, bf16[256,128]{1,0:T(8,128)(2,1)S(1)} %copy-done.3, bf16[256,128]{1,0:T(8,128)(2,1)S(1)} %copy-done.4, f32[4,256]{1,0:T(4,128)S(1)} %copy-done.6, ...), custom_call_target="tpu_custom_call" | custom-call | tf_op jit(solution)/shard_map/near_gradients/pallas_call | solution.py:407
  98.0 13.8 %all-to-all-done.5.zrec_ref = f32[8,64,128]{2,1,0:T(8,128)S(1)} async-done(((f32[8,64,128]{2,1,0:T(8,128)}), f32[8,64,128]{2,1,0:T(8,128)S(1)}, u32[]{:S(2)}, u32[]{:S(2)}) %all-to-all-start.5) | async-done | bytes 262176 | tf_op jit(solution)/shard_map/all_to_all | solution.py:419
  112.4 8.5 %all_to_all.48.exit_ref = f32[8,64,128]{2,1,0:T(8,128)S(1)} all-to-all(f32[8,64,128]{2,1,0:T(8,128)S(1)} %get-tuple-element.43), channel_id=1, replica_groups=mesh['z_hi'=8,'z_lo'=2,'x'=4,'head'=8] {'z_lo','x'}, dimensions={0} | all-to-all | bytes 524288 | tf_op jit(solution)/shard_map/all_to_all | solution.py:419
  120.9 7.2 %all-to-all-start.7 = ((f32[8,32,128]{2,1,0:T(8,128)}), f32[8,32,128]{2,1,0:T(8,128)S(1)}, u32[]{:S(2)}, u32[]{:S(2)}) async-start(f32[8,32,128]{2,1,0:T(8,128)} %get-tuple-element.48), calls=%async_computation.7 | async-start | bytes 262144 | tf_op jit(solution)/shard_map/all_to_all | solution.py:419
  128.1 1.2 finish.1
  129.2 4.2 %collective-permute-start = (f32[256,128]{1,0:T(8,128)S(1)}, f32[256,128]{1,0:T(8,128)S(1)}, u32[]{:S(2)}, u32[]{:S(2)}) collective-permute-start(f32[256,128]{1,0:T(8,128)S(1)} %get-tuple-element.52), channel_id=1, source_target_pairs={{0,1},{1,0},{2,3},{3,2},{4,5},{5,4},{6,7},{7,6},{8,9},{9,8},{10,11... | collective-permute-start | bytes 393224 | tf_op jit(solution)/shard_map/ppermute | solution.py:423
  133.4 1.0 collective-permute-done.b_ref
  134.4 2.2 %collective-permute-start.2 = (f32[256,128]{1,0:T(8,128)S(1)}, f32[256,128]{1,0:T(8,128)S(1)}, u32[]{:S(2)}, u32[]{:S(2)}) collective-permute-start(f32[256,128]{1,0:T(8,128)S(1)} %add_core.1.a_ref), channel_id=1, source_target_pairs={{0,2},{1,3},{2,0},{3,1},{4,6},{5,7},{6,4},{7,5},{8,10},{9,11},{10,... | collective-permute-start | bytes 393224 | tf_op jit(solution)/shard_map/ppermute | solution.py:423
  136.6 3.7 %collective-permute-start.1 = (f32[256,128]{1,0:T(8,128)S(1)}, f32[256,128]{1,0:T(8,128)S(1)}, u32[]{:S(2)}, u32[]{:S(2)}) collective-permute-start(f32[256,128]{1,0:T(8,128)S(1)} %add_core.1.a_ref), channel_id=1, source_target_pairs={{0,4},{1,5},{2,6},{3,7},{4,0},{5,1},{6,2},{7,3},{8,12},{9,13},{10,... | collective-permute-start | bytes 393224 | tf_op jit(solution)/shard_map/ppermute | solution.py:423
  141.0 3.4 %collective-permute-done.1.c_ref = f32[256,128]{1,0:T(8,128)S(1)} collective-permute-done((f32[256,128]{1,0:T(8,128)S(1)}, f32[256,128]{1,0:T(8,128)S(1)}, u32[]{:S(2)}, u32[]{:S(2)}) %collective-permute-start.1) | collective-permute-done | bytes 131104 | tf_op jit(solution)/shard_map/ppermute | solution.py:423
  144.4 1.0 weight_copy.1
  145.4 3.6 %all-to-all-start.8 = ((f32[8,256,128]{2,1,0:T(8,128)}), f32[8,256,128]{2,1,0:T(8,128)S(1)}, u32[]{:S(2)}, u32[]{:S(2)}) async-start(f32[8,256,128]{2,1,0:T(8,128)} %weight_copy.1), calls=%async_computation.8 | async-start | bytes 2097152 | tf_op jit(solution)/shard_map/all_to_all | solution.py:419
  149.0 3.8 %collective-permute-start.3 = (f32[256,128]{1,0:T(8,128)S(1)}, f32[256,128]{1,0:T(8,128)S(1)}, u32[]{:S(2)}, u32[]{:S(2)}) collective-permute-start(f32[256,128]{1,0:T(8,128)S(1)} %add_core.1.a_ref), channel_id=1, source_target_pairs={{0,6},{1,7},{2,4},{3,5},{4,2},{5,3},{6,0},{7,1},{8,14},{9,15},{10,... | collective-permute-start | bytes 393224 | tf_op jit(solution)/shard_map/ppermute | solution.py:423
  152.8 3.4 %collective-permute-done.3.d_ref = f32[256,128]{1,0:T(8,128)S(1)} collective-permute-done((f32[256,128]{1,0:T(8,128)S(1)}, f32[256,128]{1,0:T(8,128)S(1)}, u32[]{:S(2)}, u32[]{:S(2)}) %collective-permute-start.3) | collective-permute-done | bytes 131104 | tf_op jit(solution)/shard_map/ppermute | solution.py:423
  156.2 4.3 %collective-permute-start.4 = (f32[256,128]{1,0:T(8,128)S(1)}, f32[256,128]{1,0:T(8,128)S(1)}, u32[]{:S(2)}, u32[]{:S(2)}) collective-permute-start(f32[256,128]{1,0:T(8,128)S(1)} %add_y.1.own_ref), channel_id=1, source_target_pairs={{0,1},{1,0},{2,3},{3,2},{4,5},{5,4},{6,7},{7,6},{8,9},{9,8},{10,11... | collective-permute-start | bytes 393224 | tf_op jit(solution)/shard_map/ppermute | solution.py:423
  160.5 1.5 finish_x.1
  162.8 1.0 weight_rows.1
  (29 shorter events, 2.3 us)
Async XLA Ops:
  3.4 44.9 %copy-start = (bf16[256,1024]{1,0:T(8,128)(2,1)S(1)}, bf16[256,1024]{1,0:T(8,128)(2,1)}, u32[]{:S(2)}) copy-start(bf16[256,1024]{1,0:T(8,128)(2,1)} %do_ref.3) | copy-start | bytes 1572868
  3.4 44.9 %copy-start.1 = (bf16[256,256]{1,0:T(8,128)(2,1)S(1)}, bf16[256,256]{1,0:T(8,128)(2,1)}, u32[]{:S(2)}) copy-start(bf16[256,256]{1,0:T(8,128)(2,1)} %x_ref.5) | copy-start | bytes 393220
  3.4 44.9 %copy-start.3 = (bf16[256,128]{1,0:T(8,128)(2,1)S(1)}, bf16[256,128]{1,0:T(8,128)(2,1)}, u32[]{:S(2)}) copy-start(bf16[256,128]{1,0:T(8,128)(2,1)} %b_ref.5) | copy-start | bytes 196612
  3.4 44.9 %copy-start.4 = (bf16[256,128]{1,0:T(8,128)(2,1)S(1)}, bf16[256,128]{1,0:T(8,128)(2,1)}, u32[]{:S(2)}) copy-start(bf16[256,128]{1,0:T(8,128)(2,1)} %c_ref.7) | copy-start | bytes 196612
  3.4 44.9 %copy-start.5 = (bf16[256,1024]{1,0:T(8,128)(2,1)S(1)}, bf16[256,1024]{1,0:T(8,128)(2,1)}, u32[]{:S(2)}) copy-start(bf16[256,1024]{1,0:T(8,128)(2,1)} %w_ref.1) | copy-start | bytes 1572868
  3.4 44.9 %copy-start.6 = (f32[4,256]{1,0:T(4,128)S(1)}, f32[4,256]{1,0:T(4,128)}, u32[]{:S(2)}) copy-start(f32[4,256]{1,0:T(4,128)} %df_ref.11) | copy-start | bytes 12292
  3.5 44.9 %copy-start.7 = (f32[4,256]{1,0:T(4,128)S(1)}, f32[4,256]{1,0:T(4,128)}, u32[]{:S(2)}) copy-start(f32[4,256]{1,0:T(4,128)} %db_ref.11) | copy-start | bytes 12292
  3.5 44.9 %copy-start.8 = (f32[256]{0:T(256)S(1)}, f32[256]{0:T(256)}, u32[]{:S(2)}) copy-start(f32[256]{0:T(256)} %param.17) | copy-start | bytes 3076
  3.5 44.9 %copy-start.9 = (f32[4]{0:T(128)S(1)}, f32[4]{0:T(128)}, u32[]{:S(2)}) copy-start(f32[4]{0:T(128)} %skip_ref.3) | copy-start | bytes 52
  3.5 12.6 %all-to-all-start = ((f32[8,72,128]{2,1,0:T(8,128)}), f32[8,72,128]{2,1,0:T(8,128)S(1)}, u32[]{:S(2)}, u32[]{:S(2)}) async-start(f32[8,72,128]{2,1,0:T(8,128)} %local_states.1), calls=%async_computation | async-start | bytes 589824 | tf_op jit(solution)/shard_map/all_to_all | solution.py:419
  44.1 10.2 %copy-start.2 = (bf16[256,256]{1,0:T(8,128)(2,1)S(1)}, bf16[256,256]{1,0:T(8,128)(2,1)}, u32[]{:S(2)}) copy-start(bf16[256,256]{1,0:T(8,128)(2,1)} %z_ref.5) | copy-start | bytes 393220
  44.9 9.4 %all-to-all-start.2 = ((f32[8,64,128]{2,1,0:T(8,128)}), f32[8,64,128]{2,1,0:T(8,128)S(1)}, u32[]{:S(2)}, u32[]{:S(2)}) async-start(f32[8,64,128]{2,1,0:T(8,128)} %entries_up.1), calls=%async_computation.2 | async-start | bytes 524288 | tf_op jit(solution)/shard_map/all_to_all | solution.py:419
  90.8 20.9 %all-to-all-start.5 = ((f32[8,64,128]{2,1,0:T(8,128)}), f32[8,64,128]{2,1,0:T(8,128)S(1)}, u32[]{:S(2)}, u32[]{:S(2)}) async-start(f32[8,64,128]{2,1,0:T(8,128)} %totals_down.1), calls=%async_computation.5 | async-start | bytes 524288 | tf_op jit(solution)/shard_map/all_to_all | solution.py:419
  120.9 23.5 %all-to-all-start.7 = ((f32[8,32,128]{2,1,0:T(8,128)}), f32[8,32,128]{2,1,0:T(8,128)S(1)}, u32[]{:S(2)}, u32[]{:S(2)}) async-start(f32[8,32,128]{2,1,0:T(8,128)} %get-tuple-element.48), calls=%async_computation.7 | async-start | bytes 262144 | tf_op jit(solution)/shard_map/all_to_all | solution.py:419
  129.2 5.1 %collective-permute-start = (f32[256,128]{1,0:T(8,128)S(1)}, f32[256,128]{1,0:T(8,128)S(1)}, u32[]{:S(2)}, u32[]{:S(2)}) collective-permute-start(f32[256,128]{1,0:T(8,128)S(1)} %get-tuple-element.52), channel_id=1, source_target_pairs={{0,1},{1,0},{2,3},{3,2},{4,5},{5,4},{6,7},{7,6},{8,9},{9,8},{10,11... | collective-permute-start | bytes 393224 | tf_op jit(solution)/shard_map/ppermute | solution.py:423
  134.4 6.6 %collective-permute-start.2 = (f32[256,128]{1,0:T(8,128)S(1)}, f32[256,128]{1,0:T(8,128)S(1)}, u32[]{:S(2)}, u32[]{:S(2)}) collective-permute-start(f32[256,128]{1,0:T(8,128)S(1)} %add_core.1.a_ref), channel_id=1, source_target_pairs={{0,2},{1,3},{2,0},{3,1},{4,6},{5,7},{6,4},{7,5},{8,10},{9,11},{10,... | collective-permute-start | bytes 393224 | tf_op jit(solution)/shard_map/ppermute | solution.py:423
  136.6 7.8 %collective-permute-start.1 = (f32[256,128]{1,0:T(8,128)S(1)}, f32[256,128]{1,0:T(8,128)S(1)}, u32[]{:S(2)}, u32[]{:S(2)}) collective-permute-start(f32[256,128]{1,0:T(8,128)S(1)} %add_core.1.a_ref), channel_id=1, source_target_pairs={{0,4},{1,5},{2,6},{3,7},{4,0},{5,1},{6,2},{7,3},{8,12},{9,13},{10,... | collective-permute-start | bytes 393224 | tf_op jit(solution)/shard_map/ppermute | solution.py:423
  145.4 17.4 %all-to-all-start.8 = ((f32[8,256,128]{2,1,0:T(8,128)}), f32[8,256,128]{2,1,0:T(8,128)S(1)}, u32[]{:S(2)}, u32[]{:S(2)}) async-start(f32[8,256,128]{2,1,0:T(8,128)} %weight_copy.1), calls=%async_computation.8 | async-start | bytes 2097152 | tf_op jit(solution)/shard_map/all_to_all | solution.py:419
  149.0 7.2 %collective-permute-start.3 = (f32[256,128]{1,0:T(8,128)S(1)}, f32[256,128]{1,0:T(8,128)S(1)}, u32[]{:S(2)}, u32[]{:S(2)}) collective-permute-start(f32[256,128]{1,0:T(8,128)S(1)} %add_core.1.a_ref), channel_id=1, source_target_pairs={{0,6},{1,7},{2,4},{3,5},{4,2},{5,3},{6,0},{7,1},{8,14},{9,15},{10,... | collective-permute-start | bytes 393224 | tf_op jit(solution)/shard_map/ppermute | solution.py:423
  156.2 5.8 %collective-permute-start.4 = (f32[256,128]{1,0:T(8,128)S(1)}, f32[256,128]{1,0:T(8,128)S(1)}, u32[]{:S(2)}, u32[]{:S(2)}) collective-permute-start(f32[256,128]{1,0:T(8,128)S(1)} %add_y.1.own_ref), channel_id=1, source_target_pairs={{0,1},{1,0},{2,3},{3,2},{4,5},{5,4},{6,7},{7,6},{8,9},{9,8},{10,11... | collective-permute-start | bytes 393224 | tf_op jit(solution)/shard_map/ppermute | solution.py:423

commit v9 on v7

--- a/solution.py
+++ b/solution.py
@@ -461,12 +461,12 @@
         skip_gain, x_in, b_in, c_in, *decays, dy, entries, scalars=1,
     )
     grad_z = call(gate_gradient, "gate_gradient", [(square, BF16)], du, y, gate_in)
+    rec2, gx_near, gb_near, gc_near, grad_z = lax.optimization_barrier(
+        (rec2, gx_near, gb_near, gc_near, grad_z)
+    )
     part = weights // n_hi
     sent = call(totals_down, "totals_down", [((n_hi, size + part, LANES), F32)], place, rec1, rec2, scalars=1)
     recz2 = exchange(sent, "z_hi")
-    recz2, gx_near, gb_near, gc_near, grad_z = lax.optimization_barrier(
-        (recz2, gx_near, gb_near, gc_near, grad_z)
-    )
     sent, weight = call(
         entries_down, "entries_down", [((n, 2 * size, LANES), F32), ((n_hi, part, LANES), F32)],
         place, recz1, recz2, rec1, rec2, scalars=1,

time: 163 us -> 164 us (level)
  blocking collectives: 69.8 us -> 73 us
  starting transfers between devices: 39.3 us -> 36.7 us
    all_to_all x4, blocking collectives: 69.8 us -> 73 us  [exchange(): return lax.all_to_all(a, axis, 0, 0, tiled=True)]
    all_to_all x5, starting transfers between devices: 24.2 us -> 21.2 us  [exchange(): return lax.all_to_all(a, axis, 0, 0, tiled=True)]
  transfers between devices with their start and end apart: 9 -> 9, of which waited for: 7 -> 6; matrix products, arithmetic and copies ran while one was open for 0% -> 0% of each run, Pallas kernels for 6% -> 6%
where the time goes in v9:
time: 164 us; the launch traced here: 163 us
  blocking collectives  73 us (45%)
  starting transfers between devices  36.7 us (22%)
  waiting for transfers between devices  33.4 us (20%)
  Pallas kernels  19.2 us (12%)
    all_to_all x4, blocking collectives, exchange(): return lax.all_to_all(a, axis, 0, 0, tiled=True)  73 us
    all_to_all x5, waiting for transfers between devices, exchange(): return lax.all_to_all(a, axis, 0, 0, tiled=True)  23.9 us
    all_to_all x5, starting transfers between devices, exchange(): return lax.all_to_all(a, axis, 0, 0, tiled=True)  21.2 us
    pallas_call x18, Pallas kernels, call(): pl.pallas_call(kernel, name=name, out_shape=shapes[0] if single else tupl...  19.2 us
    ppermute x4, starting transfers between devices, swapped(): return lax.ppermute(a, 'head', [(i, i ^ mask) for i in range(n_h)])  15.6 us
    ppermute x4, waiting for transfers between devices, swapped(): return lax.ppermute(a, 'head', [(i, i ^ mask) for i in range(n_h)])  9.5 us
  transfers between devices with their start and end apart: 9, of which 6 were waited for; matrix products, arithmetic and copies ran while one was open for 0% of the time, Pallas kernels for 6%

profile of v9, /device:TPU:1, one launch (start us, length us, event | category | flops | bytes accessed | tf_op | source)
XLA Modules:
  0.0 163.3 jit_solution(2892144710688494601)
XLA Ops:
  0.6 2.8 %local_states.1 = f32[8,72,128]{2,1,0:T(8,128)} custom-call(bf16[256,256]{1,0:T(8,128)(2,1)} %x_ref.5, bf16[256,128]{1,0:T(8,128)(2,1)} %b_ref.5, f32[4,256]{1,0:T(4,128)} %df_ref.11, f32[4,256]{1,0:T(4,128)} %db_ref.11), custom_call_target="tpu_custom_call" | custom-call | tf_op jit(solution)/shard_map/local_states/pallas_call | solution.py:403
  3.5 6.3 %all-to-all-start = ((f32[8,72,128]{2,1,0:T(8,128)}), f32[8,72,128]{2,1,0:T(8,128)S(1)}, u32[]{:S(2)}, u32[]{:S(2)}) async-start(f32[8,72,128]{2,1,0:T(8,128)} %local_states.1), calls=%async_computation | async-start | bytes 589824 | tf_op jit(solution)/shard_map/all_to_all | solution.py:415
  9.8 6.2 %all-to-all-done.rec_ref.dec_ref = f32[8,72,128]{2,1,0:T(8,128)S(1)} async-done(((f32[8,72,128]{2,1,0:T(8,128)}), f32[8,72,128]{2,1,0:T(8,128)S(1)}, u32[]{:S(2)}, u32[]{:S(2)}) %all-to-all-start) | async-done | bytes 294944 | tf_op jit(solution)/shard_map/all_to_all | solution.py:415
  16.1 28.0 %all_to_all.45.zrec_ref.zdec_ref = f32[8,40,128]{2,1,0:T(8,128)S(1)} all-to-all(f32[8,40,128]{2,1,0:T(8,128)S(1)} %totals_up.1), channel_id=1, replica_groups=mesh['z_hi'=8,'z_lo'=2,'x'=4,'head'=8] {'z_hi'}, dimensions={0} | all-to-all | bytes 327680 | tf_op jit(solution)/shard_map/all_to_all | solution.py:415
  44.1 0.8 entries_up.1
  44.9 3.4 %all-to-all-start.2 = ((f32[8,64,128]{2,1,0:T(8,128)}), f32[8,64,128]{2,1,0:T(8,128)S(1)}, u32[]{:S(2)}, u32[]{:S(2)}) async-start(f32[8,64,128]{2,1,0:T(8,128)} %entries_up.1), calls=%async_computation.2 | async-start | bytes 524288 | tf_op jit(solution)/shard_map/all_to_all | solution.py:415
  48.4 2.1 %near_outputs.1 = (f32[256,256]{1,0:T(8,128)S(1)}, f32[256,256]{1,0:T(8,128)S(1)}) custom-call(f32[4]{0:T(128)S(1)} %copy-done.9, bf16[256,256]{1,0:T(8,128)(2,1)S(1)} %copy-done.1, bf16[256,128]{1,0:T(8,128)(2,1)S(1)} %copy-done.3, bf16[256,128]{1,0:T(8,128)(2,1)S(1)} %copy-done.4, f32[4,256]{1,0:T(4,128)S(1)} %copy-done.6, f32[4,256]{1,0:T(4,128)S(1)} %copy-done.7, ...), custom_call_target="tpu_custom_call" | custom-call | tf_op jit(solution)/shard_map/near_outputs/pallas_call | solution.py:403
  50.5 3.8 %all-to-all-done.2.ent_ref = f32[8,64,128]{2,1,0:T(8,128)S(1)} async-done(((f32[8,64,128]{2,1,0:T(8,128)}), f32[8,64,128]{2,1,0:T(8,128)S(1)}, u32[]{:S(2)}, u32[]{:S(2)}) %all-to-all-start.2) | async-done | bytes 262176 | tf_op jit(solution)/shard_map/all_to_all | solution.py:415
  54.3 1.0 outputs.1
  55.3 13.7 %all_to_all.46.sums_ref = f32[8,8,128]{2,1,0:T(8,128)S(1)} all-to-all(f32[8,8,128]{2,1,0:T(8,128)S(1)} %get-tuple-element.32), channel_id=1, replica_groups=mesh['z_hi'=8,'z_lo'=2,'x'=4,'head'=8] {'head'}, dimensions={0} | all-to-all | bytes 65536 | tf_op jit(solution)/shard_map/all_to_all | solution.py:415
  69.0 2.5 %gradients.1 = (f32[256,256]{1,0:T(8,128)S(1)}, f32[256,256]{1,0:T(8,128)S(1)}, f32[8,320,128]{2,1,0:T(8,128)}) custom-call(f32[8,8,128]{2,1,0:T(8,128)S(1)} %all_to_all.46.sums_ref, f32[256,256]{1,0:T(8,128)S(1)} %get-tuple-element.33.y_ref, f32[256,256]{1,0:T(8,128)S(1)} %get-tuple-element.31.m_ref, bf16[256,256]{1,0:T(8,128)(2,1)S(1)} %copy-done.2, ...), custom_call_target="tpu_custom_call" | custom-call | tf_op jit(solution)/shard_map/gradients/pallas_call | solution.py:403
  71.5 3.6 %all-to-all-start.4 = ((f32[8,320,128]{2,1,0:T(8,128)}), f32[8,320,128]{2,1,0:T(8,128)S(1)}, u32[]{:S(2)}, u32[]{:S(2)}) async-start(f32[8,320,128]{2,1,0:T(8,128)} %get-tuple-element.34), calls=%async_computation.4 | async-start | bytes 2621440 | tf_op jit(solution)/shard_map/all_to_all | solution.py:415
  75.1 0.7 gate_gradient.1
  75.8 3.0 %near_gradients.1 = (f32[256,256]{1,0:T(8,128)S(1)}, f32[256,128]{1,0:T(8,128)S(1)}, f32[256,128]{1,0:T(8,128)S(1)}) custom-call(f32[4]{0:T(128)S(1)} %copy-done.9, bf16[256,256]{1,0:T(8,128)(2,1)S(1)} %copy-done.1, bf16[256,128]{1,0:T(8,128)(2,1)S(1)} %copy-done.3, bf16[256,128]{1,0:T(8,128)(2,1)S(1)} %copy-done.4, f32[4,256]{1,0:T(4,128)S(1)} %copy-done.6, ...), custom_call_target="tpu_custom_call" | custom-call | tf_op jit(solution)/shard_map/near_gradients/pallas_call | solution.py:403
  78.8 13.9 %all-to-all-done.4.rec_ref = f32[8,320,128]{2,1,0:T(8,128)S(1)} async-done(((f32[8,320,128]{2,1,0:T(8,128)}), f32[8,320,128]{2,1,0:T(8,128)S(1)}, u32[]{:S(2)}, u32[]{:S(2)}) %all-to-all-start.4) | async-done | bytes 1310752 | tf_op jit(solution)/shard_map/all_to_all | solution.py:415
  92.8 19.1 %all_to_all.47.zrec_ref = f32[8,64,128]{2,1,0:T(8,128)S(1)} all-to-all(f32[8,64,128]{2,1,0:T(8,128)S(1)} %totals_down.1), channel_id=1, replica_groups=mesh['z_hi'=8,'z_lo'=2,'x'=4,'head'=8] {'z_hi'}, dimensions={0} | all-to-all | bytes 524288 | tf_op jit(solution)/shard_map/all_to_all | solution.py:415
  111.8 0.7 entries_down.1
  112.5 12.2 %all_to_all.48.exit_ref = f32[8,64,128]{2,1,0:T(8,128)S(1)} all-to-all(f32[8,64,128]{2,1,0:T(8,128)S(1)} %get-tuple-element.41), channel_id=1, replica_groups=mesh['z_hi'=8,'z_lo'=2,'x'=4,'head'=8] {'z_lo','x'}, dimensions={0} | all-to-all | bytes 524288 | tf_op jit(solution)/shard_map/all_to_all | solution.py:415
  124.7 4.3 %all-to-all-start.7 = ((f32[8,32,128]{2,1,0:T(8,128)}), f32[8,32,128]{2,1,0:T(8,128)S(1)}, u32[]{:S(2)}, u32[]{:S(2)}) async-start(f32[8,32,128]{2,1,0:T(8,128)} %get-tuple-element.46), calls=%async_computation.7 | async-start | bytes 262144 | tf_op jit(solution)/shard_map/all_to_all | solution.py:415
  129.0 1.2 finish.1
  130.2 4.4 %collective-permute-start = (f32[256,128]{1,0:T(8,128)S(1)}, f32[256,128]{1,0:T(8,128)S(1)}, u32[]{:S(2)}, u32[]{:S(2)}) collective-permute-start(f32[256,128]{1,0:T(8,128)S(1)} %get-tuple-element.50), channel_id=1, source_target_pairs={{0,1},{1,0},{2,3},{3,2},{4,5},{5,4},{6,7},{7,6},{8,9},{9,8},{10,11... | collective-permute-start | bytes 393224 | tf_op jit(solution)/shard_map/ppermute | solution.py:419
  134.6 1.0 collective-permute-done.b_ref
  135.5 2.2 %collective-permute-start.1 = (f32[256,128]{1,0:T(8,128)S(1)}, f32[256,128]{1,0:T(8,128)S(1)}, u32[]{:S(2)}, u32[]{:S(2)}) collective-permute-start(f32[256,128]{1,0:T(8,128)S(1)} %add_core.1.a_ref), channel_id=1, source_target_pairs={{0,2},{1,3},{2,0},{3,1},{4,6},{5,7},{6,4},{7,5},{8,10},{9,11},{10,... | collective-permute-start | bytes 393224 | tf_op jit(solution)/shard_map/ppermute | solution.py:419
  137.7 4.4 %collective-permute-done.1.b_ref = f32[256,128]{1,0:T(8,128)S(1)} collective-permute-done((f32[256,128]{1,0:T(8,128)S(1)}, f32[256,128]{1,0:T(8,128)S(1)}, u32[]{:S(2)}, u32[]{:S(2)}) %collective-permute-start.1) | collective-permute-done | bytes 131104 | tf_op jit(solution)/shard_map/ppermute | solution.py:419
  142.2 1.0 weight_copy.1
  143.2 3.6 %all-to-all-start.8 = ((f32[8,256,128]{2,1,0:T(8,128)}), f32[8,256,128]{2,1,0:T(8,128)S(1)}, u32[]{:S(2)}, u32[]{:S(2)}) async-start(f32[8,256,128]{2,1,0:T(8,128)} %weight_copy.1), calls=%async_computation.8 | async-start | bytes 2097152 | tf_op jit(solution)/shard_map/all_to_all | solution.py:415
  146.8 2.8 %collective-permute-start.2 = (f32[256,128]{1,0:T(8,128)S(1)}, f32[256,128]{1,0:T(8,128)S(1)}, u32[]{:S(2)}, u32[]{:S(2)}) collective-permute-start(f32[256,128]{1,0:T(8,128)S(1)} %add_y.2.a_ref), channel_id=1, source_target_pairs={{0,6},{1,7},{2,4},{3,5},{4,2},{5,3},{6,0},{7,1},{8,14},{9,15},{10,... | collective-permute-start | bytes 393224 | tf_op jit(solution)/shard_map/ppermute | solution.py:419
  149.6 4.1 %collective-permute-done.2.b_ref = f32[256,128]{1,0:T(8,128)S(1)} collective-permute-done((f32[256,128]{1,0:T(8,128)S(1)}, f32[256,128]{1,0:T(8,128)S(1)}, u32[]{:S(2)}, u32[]{:S(2)}) %collective-permute-start.2) | collective-permute-done | bytes 131104 | tf_op jit(solution)/shard_map/ppermute | solution.py:419
  153.7 6.2 %collective-permute-start.3 = (f32[256,128]{1,0:T(8,128)S(1)}, f32[256,128]{1,0:T(8,128)S(1)}, u32[]{:S(2)}, u32[]{:S(2)}) collective-permute-start(f32[256,128]{1,0:T(8,128)S(1)} %add_y.3.own_ref), channel_id=1, source_target_pairs={{0,1},{1,0},{2,3},{3,2},{4,5},{5,4},{6,7},{7,6},{8,9},{9,8},{10,11... | collective-permute-start | bytes 393224 | tf_op jit(solution)/shard_map/ppermute | solution.py:419
  159.9 1.5 finish_x.1
  161.5 0.7 deal_out.1
  162.2 1.0 weight_rows.1
  (28 shorter events, 0.2 us)
Async XLA Ops:
  3.4 44.9 %copy-start = (bf16[256,1024]{1,0:T(8,128)(2,1)S(1)}, bf16[256,1024]{1,0:T(8,128)(2,1)}, u32[]{:S(2)}) copy-start(bf16[256,1024]{1,0:T(8,128)(2,1)} %do_ref.3) | copy-start | bytes 1572868
  3.4 44.9 %copy-start.1 = (bf16[256,256]{1,0:T(8,128)(2,1)S(1)}, bf16[256,256]{1,0:T(8,128)(2,1)}, u32[]{:S(2)}) copy-start(bf16[256,256]{1,0:T(8,128)(2,1)} %x_ref.5) | copy-start | bytes 393220
  3.4 44.9 %copy-start.3 = (bf16[256,128]{1,0:T(8,128)(2,1)S(1)}, bf16[256,128]{1,0:T(8,128)(2,1)}, u32[]{:S(2)}) copy-start(bf16[256,128]{1,0:T(8,128)(2,1)} %b_ref.5) | copy-start | bytes 196612
  3.4 44.9 %copy-start.4 = (bf16[256,128]{1,0:T(8,128)(2,1)S(1)}, bf16[256,128]{1,0:T(8,128)(2,1)}, u32[]{:S(2)}) copy-start(bf16[256,128]{1,0:T(8,128)(2,1)} %c_ref.7) | copy-start | bytes 196612
  3.4 44.9 %copy-start.5 = (bf16[256,1024]{1,0:T(8,128)(2,1)S(1)}, bf16[256,1024]{1,0:T(8,128)(2,1)}, u32[]{:S(2)}) copy-start(bf16[256,1024]{1,0:T(8,128)(2,1)} %w_ref.1) | copy-start | bytes 1572868
  3.4 44.9 %copy-start.6 = (f32[4,256]{1,0:T(4,128)S(1)}, f32[4,256]{1,0:T(4,128)}, u32[]{:S(2)}) copy-start(f32[4,256]{1,0:T(4,128)} %df_ref.11) | copy-start | bytes 12292
  3.5 44.9 %copy-start.7 = (f32[4,256]{1,0:T(4,128)S(1)}, f32[4,256]{1,0:T(4,128)}, u32[]{:S(2)}) copy-start(f32[4,256]{1,0:T(4,128)} %db_ref.11) | copy-start | bytes 12292
  3.5 44.9 %copy-start.8 = (f32[256]{0:T(256)S(1)}, f32[256]{0:T(256)}, u32[]{:S(2)}) copy-start(f32[256]{0:T(256)} %param.17) | copy-start | bytes 3076
  3.5 44.9 %copy-start.9 = (f32[4]{0:T(128)S(1)}, f32[4]{0:T(128)}, u32[]{:S(2)}) copy-start(f32[4]{0:T(128)} %skip_ref.3) | copy-start | bytes 52
  3.5 12.6 %all-to-all-start = ((f32[8,72,128]{2,1,0:T(8,128)}), f32[8,72,128]{2,1,0:T(8,128)S(1)}, u32[]{:S(2)}, u32[]{:S(2)}) async-start(f32[8,72,128]{2,1,0:T(8,128)} %local_states.1), calls=%async_computation | async-start | bytes 589824 | tf_op jit(solution)/shard_map/all_to_all | solution.py:415
  44.1 10.2 %copy-start.2 = (bf16[256,256]{1,0:T(8,128)(2,1)S(1)}, bf16[256,256]{1,0:T(8,128)(2,1)}, u32[]{:S(2)}) copy-start(bf16[256,256]{1,0:T(8,128)(2,1)} %z_ref.5) | copy-start | bytes 393220
  44.9 9.4 %all-to-all-start.2 = ((f32[8,64,128]{2,1,0:T(8,128)}), f32[8,64,128]{2,1,0:T(8,128)S(1)}, u32[]{:S(2)}, u32[]{:S(2)}) async-start(f32[8,64,128]{2,1,0:T(8,128)} %entries_up.1), calls=%async_computation.2 | async-start | bytes 524288 | tf_op jit(solution)/shard_map/all_to_all | solution.py:415
  71.5 21.2 %all-to-all-start.4 = ((f32[8,320,128]{2,1,0:T(8,128)}), f32[8,320,128]{2,1,0:T(8,128)S(1)}, u32[]{:S(2)}, u32[]{:S(2)}) async-start(f32[8,320,128]{2,1,0:T(8,128)} %get-tuple-element.34), calls=%async_computation.4 | async-start | bytes 2621440 | tf_op jit(solution)/shard_map/all_to_all | solution.py:415
  124.7 17.5 %all-to-all-start.7 = ((f32[8,32,128]{2,1,0:T(8,128)}), f32[8,32,128]{2,1,0:T(8,128)S(1)}, u32[]{:S(2)}, u32[]{:S(2)}) async-start(f32[8,32,128]{2,1,0:T(8,128)} %get-tuple-element.46), calls=%async_computation.7 | async-start | bytes 262144 | tf_op jit(solution)/shard_map/all_to_all | solution.py:415
  130.2 5.4 %collective-permute-start = (f32[256,128]{1,0:T(8,128)S(1)}, f32[256,128]{1,0:T(8,128)S(1)}, u32[]{:S(2)}, u32[]{:S(2)}) collective-permute-start(f32[256,128]{1,0:T(8,128)S(1)} %get-tuple-element.50), channel_id=1, source_target_pairs={{0,1},{1,0},{2,3},{3,2},{4,5},{5,4},{6,7},{7,6},{8,9},{9,8},{10,11... | collective-permute-start | bytes 393224 | tf_op jit(solution)/shard_map/ppermute | solution.py:419
  135.5 6.6 %collective-permute-start.1 = (f32[256,128]{1,0:T(8,128)S(1)}, f32[256,128]{1,0:T(8,128)S(1)}, u32[]{:S(2)}, u32[]{:S(2)}) collective-permute-start(f32[256,128]{1,0:T(8,128)S(1)} %add_core.1.a_ref), channel_id=1, source_target_pairs={{0,2},{1,3},{2,0},{3,1},{4,6},{5,7},{6,4},{7,5},{8,10},{9,11},{10,... | collective-permute-start | bytes 393224 | tf_op jit(solution)/shard_map/ppermute | solution.py:419
  143.2 19.0 %all-to-all-start.8 = ((f32[8,256,128]{2,1,0:T(8,128)}), f32[8,256,128]{2,1,0:T(8,128)S(1)}, u32[]{:S(2)}, u32[]{:S(2)}) async-start(f32[8,256,128]{2,1,0:T(8,128)} %weight_copy.1), calls=%async_computation.8 | async-start | bytes 2097152 | tf_op jit(solution)/shard_map/all_to_all | solution.py:415
  146.8 6.9 %collective-permute-start.2 = (f32[256,128]{1,0:T(8,128)S(1)}, f32[256,128]{1,0:T(8,128)S(1)}, u32[]{:S(2)}, u32[]{:S(2)}) collective-permute-start(f32[256,128]{1,0:T(8,128)S(1)} %add_y.2.a_ref), channel_id=1, source_target_pairs={{0,6},{1,7},{2,4},{3,5},{4,2},{5,3},{6,0},{7,1},{8,14},{9,15},{10,... | collective-permute-start | bytes 393224 | tf_op jit(solution)/shard_map/ppermute | solution.py:419
  153.7 7.7 %collective-permute-start.3 = (f32[256,128]{1,0:T(8,128)S(1)}, f32[256,128]{1,0:T(8,128)S(1)}, u32[]{:S(2)}, u32[]{:S(2)}) collective-permute-start(f32[256,128]{1,0:T(8,128)S(1)} %add_y.3.own_ref), channel_id=1, source_target_pairs={{0,1},{1,0},{2,3},{3,2},{4,5},{5,4},{6,7},{7,6},{8,9},{9,8},{10,11... | collective-permute-start | bytes 393224 | tf_op jit(solution)/shard_map/ppermute | solution.py:419

commit v10 on v7

--- a/solution.py
+++ b/solution.py
@@ -114,7 +114,7 @@
     return forward, backward
 
 
-def local_states(x_hbm, b_hbm, df_hbm, db_hbm, out_ref, x_ref, b_ref, df_ref, db_ref, sems):
+def local_states(_, x_hbm, b_hbm, df_hbm, db_hbm, out_ref, x_ref, b_ref, df_ref, db_ref, sems):
     sources, targets = (x_hbm, b_hbm, df_hbm, db_hbm), (x_ref, b_ref, df_ref, db_ref)
     copies = [pltpu.make_async_copy(s, t, sems.at[i]) for i, (s, t) in enumerate(zip(sources, targets))]
     for copy in copies[::-1]:
@@ -433,7 +433,9 @@
 
     firsts = tuple(pltpu.with_memory_space_constraint(a, pltpu.MemorySpace.HBM) for a in (x_in, b_in, *decays))
     own = [pltpu.VMEM(a.shape, a.dtype) for a in firsts] + [pltpu.SemaphoreType.DMA((4,))]
-    sent = call(local_states, "local_states", [((n, 2 * size + 8, LANES), F32)], *firsts, own=own)
+    sent = call(
+        local_states, "local_states", [((n, 2 * size + 8, LANES), F32)], place, *firsts, scalars=1, own=own
+    )
     rec1 = exchange(sent, group)
     near, m = call(
         near_outputs, "near_outputs", [(square, F32)] * 2,
@@ -441,6 +443,7 @@
     )
     sent = call(totals_up, "totals_up", [((n_hi, size + 8, LANES), F32)], place, rec1, scalars=1)
     recz1 = exchange(sent, "z_hi")
+    recz1, near, m = lax.optimization_barrier((recz1, near, m))
     sent = call(entries_up, "entries_up", [((n, 2 * size, LANES), F32)], place, recz1, rec1, scalars=1)
     entries = exchange(sent, group)
 

time: 163 us -> 163 us (level)
  blocking collectives: 69.8 us -> 64.6 us
  starting transfers between devices: 39.3 us -> 44 us
    all_to_all x4 -> x5, blocking collectives: 69.8 us -> 64.6 us  [exchange(): return lax.all_to_all(a, axis, 0, 0, tiled=True)]
    all_to_all x5 -> x4, starting transfers between devices: 24.2 us -> 27.3 us  [exchange(): return lax.all_to_all(a, axis, 0, 0, tiled=True)]
    all_to_all x5 -> x4, waiting for transfers between devices: 23.8 us -> 24.8 us  [exchange(): return lax.all_to_all(a, axis, 0, 0, tiled=True)]
  transfers between devices with their start and end apart: 9 -> 8, of which waited for: 7 -> 5; matrix products, arithmetic and copies ran while one was open for 0% -> 0% of each run, Pallas kernels for 6% -> 6%
where the time goes in v10:
time: 163 us; the launch traced here: 162 us
  blocking collectives  64.6 us (40%)
  starting transfers between devices  44 us (27%)
  waiting for transfers between devices  34.3 us (21%)
  Pallas kernels  18.2 us (11%)
    all_to_all x5, blocking collectives, exchange(): return lax.all_to_all(a, axis, 0, 0, tiled=True)  64.6 us
    all_to_all x4, starting transfers between devices, exchange(): return lax.all_to_all(a, axis, 0, 0, tiled=True)  27.3 us
    all_to_all x4, waiting for transfers between devices, exchange(): return lax.all_to_all(a, axis, 0, 0, tiled=True)  24.8 us
    pallas_call x18, Pallas kernels, call(): pl.pallas_call(kernel, name=name, out_shape=shapes[0] if single else tupl...  18.2 us
    ppermute x4, starting transfers between devices, swapped(): return lax.ppermute(a, 'head', [(i, i ^ mask) for i in range(n_h)])  16.7 us
    ppermute x4, waiting for transfers between devices, swapped(): return lax.ppermute(a, 'head', [(i, i ^ mask) for i in range(n_h)])  9.51 us
  transfers between devices with their start and end apart: 8, of which 5 were waited for; matrix products, arithmetic and copies ran while one was open for 0% of the time, Pallas kernels for 6%

profile of v10, /device:TPU:1, one launch (start us, length us, event | category | flops | bytes accessed | tf_op | source)
XLA Modules:
  0.0 162.0 jit_solution(14437782833607201947)
XLA Ops:
  0.7 2.1 %local_states.1 = f32[8,72,128]{2,1,0:T(8,128)S(1)} custom-call(s32[1]{0:T(128)} %bitcast._.place_ref, bf16[256,256]{1,0:T(8,128)(2,1)} %x_ref.5, bf16[256,128]{1,0:T(8,128)(2,1)} %b_ref.5, f32[4,256]{1,0:T(4,128)} %df_ref.11, f32[4,256]{1,0:T(4,128)} %db_ref.11), custom_call_target="tpu_custom_call" | custom-call | tf_op jit(solution)/shard_map/local_states/pallas_call | solution.py:403
  2.9 12.5 %all_to_all.45.rec_ref.dec_ref = f32[8,72,128]{2,1,0:T(8,128)S(1)} all-to-all(f32[8,72,128]{2,1,0:T(8,128)S(1)} %local_states.1), channel_id=1, replica_groups=mesh['z_hi'=8,'z_lo'=2,'x'=4,'head'=8] {'z_lo','x'}, dimensions={0} | all-to-all | bytes 589824 | tf_op jit(solution)/shard_map/all_to_all | solution.py:415
  15.4 0.7 totals_up.1
  16.1 14.0 %all-to-all-start.1 = ((f32[8,40,128]{2,1,0:T(8,128)}), f32[8,40,128]{2,1,0:T(8,128)S(1)}, u32[]{:S(2)}, u32[]{:S(2)}) async-start(f32[8,40,128]{2,1,0:T(8,128)} %totals_up.1), calls=%async_computation.1 | async-start | bytes 327680 | tf_op jit(solution)/shard_map/all_to_all | solution.py:415
  30.2 2.1 %near_outputs.1 = (f32[256,256]{1,0:T(8,128)S(1)}, f32[256,256]{1,0:T(8,128)S(1)}) custom-call(f32[4]{0:T(128)S(1)} %copy-done.9, bf16[256,256]{1,0:T(8,128)(2,1)S(1)} %copy-done.1, bf16[256,128]{1,0:T(8,128)(2,1)S(1)} %copy-done.3, bf16[256,128]{1,0:T(8,128)(2,1)S(1)} %copy-done.4, f32[4,256]{1,0:T(4,128)S(1)} %copy-done.6, f32[4,256]{1,0:T(4,128)S(1)} %copy-done.7, ...), custom_call_target="tpu_custom_call" | custom-call | tf_op jit(solution)/shard_map/near_outputs/pallas_call | solution.py:403
  32.3 11.0 %all-to-all-done.1.zrec_ref.zdec_ref = f32[8,40,128]{2,1,0:T(8,128)S(1)} async-done(((f32[8,40,128]{2,1,0:T(8,128)}), f32[8,40,128]{2,1,0:T(8,128)S(1)}, u32[]{:S(2)}, u32[]{:S(2)}) %all-to-all-start.1) | async-done | bytes 163872 | tf_op jit(solution)/shard_map/all_to_all | solution.py:415
  43.4 9.3 %all_to_all.46.ent_ref = f32[8,64,128]{2,1,0:T(8,128)S(1)} all-to-all(f32[8,64,128]{2,1,0:T(8,128)S(1)} %entries_up.1), channel_id=1, replica_groups=mesh['z_hi'=8,'z_lo'=2,'x'=4,'head'=8] {'z_lo','x'}, dimensions={0} | all-to-all | bytes 524288 | tf_op jit(solution)/shard_map/all_to_all | solution.py:415
  52.7 1.0 outputs.1
  53.7 14.7 %all_to_all.47.sums_ref = f32[8,8,128]{2,1,0:T(8,128)S(1)} all-to-all(f32[8,8,128]{2,1,0:T(8,128)S(1)} %get-tuple-element.38), channel_id=1, replica_groups=mesh['z_hi'=8,'z_lo'=2,'x'=4,'head'=8] {'head'}, dimensions={0} | all-to-all | bytes 65536 | tf_op jit(solution)/shard_map/all_to_all | solution.py:415
  68.4 1.4 gradients.1
  69.8 19.6 %all_to_all.48.rec_ref = f32[8,320,128]{2,1,0:T(8,128)S(1)} all-to-all(f32[8,320,128]{2,1,0:T(8,128)S(1)} %get-tuple-element.40), channel_id=1, replica_groups=mesh['z_hi'=8,'z_lo'=2,'x'=4,'head'=8] {'z_lo','x'}, dimensions={0} | all-to-all | bytes 2621440 | tf_op jit(solution)/shard_map/all_to_all | solution.py:415
  89.4 0.8 totals_down.1
  90.2 3.4 %all-to-all-start.5 = ((f32[8,64,128]{2,1,0:T(8,128)}), f32[8,64,128]{2,1,0:T(8,128)S(1)}, u32[]{:S(2)}, u32[]{:S(2)}) async-start(f32[8,64,128]{2,1,0:T(8,128)} %totals_down.1), calls=%async_computation.5 | async-start | bytes 524288 | tf_op jit(solution)/shard_map/all_to_all | solution.py:415
  93.6 0.7 gate_gradient.1
  94.4 3.0 %near_gradients.1 = (f32[256,256]{1,0:T(8,128)S(1)}, f32[256,128]{1,0:T(8,128)S(1)}, f32[256,128]{1,0:T(8,128)S(1)}) custom-call(f32[4]{0:T(128)S(1)} %copy-done.9, bf16[256,256]{1,0:T(8,128)(2,1)S(1)} %copy-done.1, bf16[256,128]{1,0:T(8,128)(2,1)S(1)} %copy-done.3, bf16[256,128]{1,0:T(8,128)(2,1)S(1)} %copy-done.4, f32[4,256]{1,0:T(4,128)S(1)} %copy-done.6, ...), custom_call_target="tpu_custom_call" | custom-call | tf_op jit(solution)/shard_map/near_gradients/pallas_call | solution.py:403
  97.4 13.8 %all-to-all-done.5.zrec_ref = f32[8,64,128]{2,1,0:T(8,128)S(1)} async-done(((f32[8,64,128]{2,1,0:T(8,128)}), f32[8,64,128]{2,1,0:T(8,128)S(1)}, u32[]{:S(2)}, u32[]{:S(2)}) %all-to-all-start.5) | async-done | bytes 262176 | tf_op jit(solution)/shard_map/all_to_all | solution.py:415
  111.1 0.7 entries_down.1
  111.8 8.5 %all_to_all.49.exit_ref = f32[8,64,128]{2,1,0:T(8,128)S(1)} all-to-all(f32[8,64,128]{2,1,0:T(8,128)S(1)} %get-tuple-element.47), channel_id=1, replica_groups=mesh['z_hi'=8,'z_lo'=2,'x'=4,'head'=8] {'z_lo','x'}, dimensions={0} | all-to-all | bytes 524288 | tf_op jit(solution)/shard_map/all_to_all | solution.py:415
  120.3 6.3 %all-to-all-start.7 = ((f32[8,32,128]{2,1,0:T(8,128)}), f32[8,32,128]{2,1,0:T(8,128)S(1)}, u32[]{:S(2)}, u32[]{:S(2)}) async-start(f32[8,32,128]{2,1,0:T(8,128)} %get-tuple-element.52), calls=%async_computation.7 | async-start | bytes 262144 | tf_op jit(solution)/shard_map/all_to_all | solution.py:415
  126.6 1.2 finish.1
  127.7 5.0 %collective-permute-start = (f32[256,128]{1,0:T(8,128)S(1)}, f32[256,128]{1,0:T(8,128)S(1)}, u32[]{:S(2)}, u32[]{:S(2)}) collective-permute-start(f32[256,128]{1,0:T(8,128)S(1)} %get-tuple-element.56), channel_id=1, source_target_pairs={{0,1},{1,0},{2,3},{3,2},{4,5},{5,4},{6,7},{7,6},{8,9},{9,8},{10,11... | collective-permute-start | bytes 393224 | tf_op jit(solution)/shard_map/ppermute | solution.py:419
  132.8 1.0 collective-permute-done.b_ref
  133.7 2.2 %collective-permute-start.1 = (f32[256,128]{1,0:T(8,128)S(1)}, f32[256,128]{1,0:T(8,128)S(1)}, u32[]{:S(2)}, u32[]{:S(2)}) collective-permute-start(f32[256,128]{1,0:T(8,128)S(1)} %add_core.1.a_ref), channel_id=1, source_target_pairs={{0,2},{1,3},{2,0},{3,1},{4,6},{5,7},{6,4},{7,5},{8,10},{9,11},{10,... | collective-permute-start | bytes 393224 | tf_op jit(solution)/shard_map/ppermute | solution.py:419
  135.9 4.4 %collective-permute-done.1.b_ref = f32[256,128]{1,0:T(8,128)S(1)} collective-permute-done((f32[256,128]{1,0:T(8,128)S(1)}, f32[256,128]{1,0:T(8,128)S(1)}, u32[]{:S(2)}, u32[]{:S(2)}) %collective-permute-start.1) | collective-permute-done | bytes 131104 | tf_op jit(solution)/shard_map/ppermute | solution.py:419
  140.4 1.0 weight_copy.1
  141.4 3.6 %all-to-all-start.8 = ((f32[8,256,128]{2,1,0:T(8,128)}), f32[8,256,128]{2,1,0:T(8,128)S(1)}, u32[]{:S(2)}, u32[]{:S(2)}) async-start(f32[8,256,128]{2,1,0:T(8,128)} %weight_copy.1), calls=%async_computation.8 | async-start | bytes 2097152 | tf_op jit(solution)/shard_map/all_to_all | solution.py:415
  145.0 2.8 %collective-permute-start.2 = (f32[256,128]{1,0:T(8,128)S(1)}, f32[256,128]{1,0:T(8,128)S(1)}, u32[]{:S(2)}, u32[]{:S(2)}) collective-permute-start(f32[256,128]{1,0:T(8,128)S(1)} %add_y.2.a_ref), channel_id=1, source_target_pairs={{0,6},{1,7},{2,4},{3,5},{4,2},{5,3},{6,0},{7,1},{8,14},{9,15},{10,... | collective-permute-start | bytes 393224 | tf_op jit(solution)/shard_map/ppermute | solution.py:419
  147.8 4.1 %collective-permute-done.2.b_ref = f32[256,128]{1,0:T(8,128)S(1)} collective-permute-done((f32[256,128]{1,0:T(8,128)S(1)}, f32[256,128]{1,0:T(8,128)S(1)}, u32[]{:S(2)}, u32[]{:S(2)}) %collective-permute-start.2) | collective-permute-done | bytes 131104 | tf_op jit(solution)/shard_map/ppermute | solution.py:419
  151.9 6.7 %collective-permute-start.3 = (f32[256,128]{1,0:T(8,128)S(1)}, f32[256,128]{1,0:T(8,128)S(1)}, u32[]{:S(2)}, u32[]{:S(2)}) collective-permute-start(f32[256,128]{1,0:T(8,128)S(1)} %add_y.3.own_ref), channel_id=1, source_target_pairs={{0,1},{1,0},{2,3},{3,2},{4,5},{5,4},{6,7},{7,6},{8,9},{9,8},{10,11... | collective-permute-start | bytes 393224 | tf_op jit(solution)/shard_map/ppermute | solution.py:419
  158.7 1.5 finish_x.1
  160.2 0.7 deal_out.1
  160.9 1.0 weight_rows.1
  (27 shorter events, 0.2 us)
Async XLA Ops:
  0.6 29.5 %copy-start.7 = (f32[4,256]{1,0:T(4,128)S(1)}, f32[4,256]{1,0:T(4,128)}, u32[]{:S(2)}) copy-start(f32[4,256]{1,0:T(4,128)} %db_ref.11) | copy-start | bytes 12292
  0.6 29.5 %copy-start.6 = (f32[4,256]{1,0:T(4,128)S(1)}, f32[4,256]{1,0:T(4,128)}, u32[]{:S(2)}) copy-start(f32[4,256]{1,0:T(4,128)} %df_ref.11) | copy-start | bytes 12292
  0.7 29.5 %copy-start.3 = (bf16[256,128]{1,0:T(8,128)(2,1)S(1)}, bf16[256,128]{1,0:T(8,128)(2,1)}, u32[]{:S(2)}) copy-start(bf16[256,128]{1,0:T(8,128)(2,1)} %b_ref.5) | copy-start | bytes 196612
  0.7 29.5 %copy-start.1 = (bf16[256,256]{1,0:T(8,128)(2,1)S(1)}, bf16[256,256]{1,0:T(8,128)(2,1)}, u32[]{:S(2)}) copy-start(bf16[256,256]{1,0:T(8,128)(2,1)} %x_ref.5) | copy-start | bytes 393220
  0.7 29.5 %copy-start.4 = (bf16[256,128]{1,0:T(8,128)(2,1)S(1)}, bf16[256,128]{1,0:T(8,128)(2,1)}, u32[]{:S(2)}) copy-start(bf16[256,128]{1,0:T(8,128)(2,1)} %c_ref.7) | copy-start | bytes 196612
  0.7 29.5 %copy-start = (bf16[256,1024]{1,0:T(8,128)(2,1)S(1)}, bf16[256,1024]{1,0:T(8,128)(2,1)}, u32[]{:S(2)}) copy-start(bf16[256,1024]{1,0:T(8,128)(2,1)} %do_ref.3) | copy-start | bytes 1572868
  0.7 29.5 %copy-start.9 = (f32[4]{0:T(128)S(1)}, f32[4]{0:T(128)}, u32[]{:S(2)}) copy-start(f32[4]{0:T(128)} %skip_ref.3) | copy-start | bytes 52
  0.7 29.5 %copy-start.5 = (bf16[256,1024]{1,0:T(8,128)(2,1)S(1)}, bf16[256,1024]{1,0:T(8,128)(2,1)}, u32[]{:S(2)}) copy-start(bf16[256,1024]{1,0:T(8,128)(2,1)} %w_ref.1) | copy-start | bytes 1572868
  0.7 29.5 %copy-start.8 = (f32[256]{0:T(256)S(1)}, f32[256]{0:T(256)}, u32[]{:S(2)}) copy-start(f32[256]{0:T(256)} %param.17) | copy-start | bytes 3076
  16.1 27.2 %all-to-all-start.1 = ((f32[8,40,128]{2,1,0:T(8,128)}), f32[8,40,128]{2,1,0:T(8,128)S(1)}, u32[]{:S(2)}, u32[]{:S(2)}) async-start(f32[8,40,128]{2,1,0:T(8,128)} %totals_up.1), calls=%async_computation.1 | async-start | bytes 327680 | tf_op jit(solution)/shard_map/all_to_all | solution.py:415
  30.1 22.6 %copy-start.2 = (bf16[256,256]{1,0:T(8,128)(2,1)S(1)}, bf16[256,256]{1,0:T(8,128)(2,1)}, u32[]{:S(2)}) copy-start(bf16[256,256]{1,0:T(8,128)(2,1)} %z_ref.5) | copy-start | bytes 393220
  90.2 20.9 %all-to-all-start.5 = ((f32[8,64,128]{2,1,0:T(8,128)}), f32[8,64,128]{2,1,0:T(8,128)S(1)}, u32[]{:S(2)}, u32[]{:S(2)}) async-start(f32[8,64,128]{2,1,0:T(8,128)} %totals_down.1), calls=%async_computation.5 | async-start | bytes 524288 | tf_op jit(solution)/shard_map/all_to_all | solution.py:415
  120.3 20.1 %all-to-all-start.7 = ((f32[8,32,128]{2,1,0:T(8,128)}), f32[8,32,128]{2,1,0:T(8,128)S(1)}, u32[]{:S(2)}, u32[]{:S(2)}) async-start(f32[8,32,128]{2,1,0:T(8,128)} %get-tuple-element.52), calls=%async_computation.7 | async-start | bytes 262144 | tf_op jit(solution)/shard_map/all_to_all | solution.py:415
  127.7 6.0 %collective-permute-start = (f32[256,128]{1,0:T(8,128)S(1)}, f32[256,128]{1,0:T(8,128)S(1)}, u32[]{:S(2)}, u32[]{:S(2)}) collective-permute-start(f32[256,128]{1,0:T(8,128)S(1)} %get-tuple-element.56), channel_id=1, source_target_pairs={{0,1},{1,0},{2,3},{3,2},{4,5},{5,4},{6,7},{7,6},{8,9},{9,8},{10,11... | collective-permute-start | bytes 393224 | tf_op jit(solution)/shard_map/ppermute | solution.py:419
  133.7 6.6 %collective-permute-start.1 = (f32[256,128]{1,0:T(8,128)S(1)}, f32[256,128]{1,0:T(8,128)S(1)}, u32[]{:S(2)}, u32[]{:S(2)}) collective-permute-start(f32[256,128]{1,0:T(8,128)S(1)} %add_core.1.a_ref), channel_id=1, source_target_pairs={{0,2},{1,3},{2,0},{3,1},{4,6},{5,7},{6,4},{7,5},{8,10},{9,11},{10,... | collective-permute-start | bytes 393224 | tf_op jit(solution)/shard_map/ppermute | solution.py:419
  141.4 19.5 %all-to-all-start.8 = ((f32[8,256,128]{2,1,0:T(8,128)}), f32[8,256,128]{2,1,0:T(8,128)S(1)}, u32[]{:S(2)}, u32[]{:S(2)}) async-start(f32[8,256,128]{2,1,0:T(8,128)} %weight_copy.1), calls=%async_computation.8 | async-start | bytes 2097152 | tf_op jit(solution)/shard_map/all_to_all | solution.py:415
  145.0 6.9 %collective-permute-start.2 = (f32[256,128]{1,0:T(8,128)S(1)}, f32[256,128]{1,0:T(8,128)S(1)}, u32[]{:S(2)}, u32[]{:S(2)}) collective-permute-start(f32[256,128]{1,0:T(8,128)S(1)} %add_y.2.a_ref), channel_id=1, source_target_pairs={{0,6},{1,7},{2,4},{3,5},{4,2},{5,3},{6,0},{7,1},{8,14},{9,15},{10,... | collective-permute-start | bytes 393224 | tf_op jit(solution)/shard_map/ppermute | solution.py:419
  151.9 8.3 %collective-permute-start.3 = (f32[256,128]{1,0:T(8,128)S(1)}, f32[256,128]{1,0:T(8,128)S(1)}, u32[]{:S(2)}, u32[]{:S(2)}) collective-permute-start(f32[256,128]{1,0:T(8,128)S(1)} %add_y.3.own_ref), channel_id=1, source_target_pairs={{0,1},{1,0},{2,3},{3,2},{4,5},{5,4},{6,7},{7,6},{8,9},{9,8},{10,11... | collective-permute-start | bytes 393224 | tf_op jit(solution)/shard_map/ppermute | solution.py:419

commit v11 on v10

--- a/solution.py
+++ b/solution.py
@@ -357,18 +357,14 @@
     gz_ref[...] = (du_ref[...] * y_ref[...] * sig * (1.0 + z * (1.0 - sig))).astype(BF16)
 
 
-def finish(core_ref, x_ref, df_ref, db_ref, exit_ref, gb_near, gc_near, keep_ref, give_ref):
+def finish(x_ref, df_ref, db_ref, exit_ref, gb_near, gc_near, out_ref):
     cf, be, end_f, end_b = columns(df_ref[...], db_ref[...])
     x = x_ref[...].astype(F32)
     exit_f, exit_b = take_slices(exit_ref)
     grad_b = gb_near[...] + dot_both(x * spread(jnp.exp(end_f - cf)), exit_f, 1, 0)
     grad_b = grad_b + dot_both(x * spread(jnp.exp(be)), exit_b, 1, 0)
-    half = FRAMES // 2
-    first = core_ref[0] == 0
-    for i, grad in enumerate((grad_b, gc_near[...])):
-        at = slice(i * half, (i + 1) * half)
-        keep_ref[at, :] = jnp.where(first, grad[:half, :], grad[half:, :])
-        give_ref[at, :] = jnp.where(first, grad[half:, :], grad[:half, :])
+    out_ref[0, :, :] = grad_b
+    out_ref[1, :, :] = gc_near[...]
 
 
 def finish_x(b_ref, df_ref, db_ref, exit_ref, gx_near, gx_ref):
@@ -383,13 +379,9 @@
     out_ref[...] = a_ref[...] + b_ref[...]
 
 
-def deal_out(core_ref, own_ref, other_ref, gb_ref, gc_ref):
-    half = FRAMES // 2
-    first = core_ref[0] == 0
-    for i, ref in enumerate((gb_ref, gc_ref)):
-        at = slice(i * half, (i + 1) * half)
-        ref[0:half, :] = jnp.where(first, own_ref[at, :], other_ref[at, :])
-        ref[half:, :] = jnp.where(first, other_ref[at, :], own_ref[at, :])
+def add_last(a_ref, b_ref, gb_ref, gc_ref):
+    gb_ref[...] = a_ref[0, :, :] + b_ref[0, :, :]
+    gc_ref[...] = a_ref[1, :, :] + b_ref[1, :, :]
 
 
 VMEM = pl.BlockSpec(memory_space=pltpu.VMEM)
@@ -479,21 +471,19 @@
     exits, weight = lax.optimization_barrier((exits, weight))
     weight = exchange(weight, "z_hi")
 
-    core = (lax.axis_index("head") % 2).astype(jnp.int32).reshape(1)
-    half = [((FRAMES, STATE), F32)]
-    own, give = call(finish, "finish", half * 2, core, x_in, *decays, exits, gb_near, gc_near, scalars=1)
-    own = call(add_two, "add_core", half, own, swapped(give, 1, n_h))
-    own = call(add_two, "add_y", half, own, swapped(own, 2, n_h))
+    both = [((2, FRAMES, STATE), F32)]
+    own = call(finish, "finish", both, x_in, *decays, exits, gb_near, gc_near)
+    own = call(add_two, "add_core", both, own, swapped(own, 1, n_h))
+    own = call(add_two, "add_y", both, own, swapped(own, 2, n_h))
     weight, own = lax.optimization_barrier((weight, own))
 
     weight = call(weight_copy, "weight_copy", [((n, weights, LANES), F32)], weight)
     weight = exchange(weight, group)
     grad_w = call(weight_rows, "weight_rows", [((WIDTH, model), F32)], weight)
 
-    own = call(add_two, "add_y", half, own, swapped(own, 6, n_h))
-    other = swapped(own, 1, n_h)
     grad_x = call(finish_x, "finish_x", [(square, BF16)], b_in, *decays, exits, gx_near)
-    grad_b, grad_c = call(deal_out, "deal_out", half * 2, core, own, other, scalars=1)
+    grads = [((FRAMES, STATE), F32)] * 2
+    grad_b, grad_c = call(add_last, "add_last", grads, own, swapped(own, 6, n_h))
     return grad_x, grad_z, grad_b, grad_c, grad_w
 
 

time: 163 us -> 170 us (1.043)
  waiting for transfers between devices: 34.3 us -> 48.2 us
  starting transfers between devices: 44 us -> 37.3 us
    all_to_all x4, waiting for transfers between devices: 24.8 us -> 34.5 us  [exchange(): return lax.all_to_all(a, axis, 0, 0, tiled=True)]
    ppermute x4 -> x3, waiting for transfers between devices: 9.51 us -> 13.7 us  [swapped(): return lax.ppermute(a, 'head', [(i, i ^ mask) for i in range(n_h)])]
    ppermute x4 -> x3, starting transfers between devices: 16.7 us -> 12.9 us  [swapped(): return lax.ppermute(a, 'head', [(i, i ^ mask) for i in range(n_h)])]
    all_to_all x4, starting transfers between devices: 27.3 us -> 24.4 us  [exchange(): return lax.all_to_all(a, axis, 0, 0, tiled=True)]
    pallas_call x18 -> x17, Pallas kernels: 18.2 us -> 18.2 us  [call(): pl.pallas_call(kernel, name=name, out_shape=shapes[0] if single else tupl...]
  transfers between devices with their start and end apart: 8 -> 7, of which waited for: 5 -> 6; matrix products, arithmetic and copies ran while one was open for 0% -> 0% of each run, Pallas kernels for 6% -> 5%
where the time goes in v11:
time: 170 us; the launch traced here: 169 us
  blocking collectives  64.6 us (38%)
  waiting for transfers between devices  48.2 us (28%)
  starting transfers between devices  37.3 us (22%)
  Pallas kernels  18.2 us (11%)
    all_to_all x5, blocking collectives, exchange(): return lax.all_to_all(a, axis, 0, 0, tiled=True)  64.6 us
    all_to_all x4, waiting for transfers between devices, exchange(): return lax.all_to_all(a, axis, 0, 0, tiled=True)  34.5 us
    all_to_all x4, starting transfers between devices, exchange(): return lax.all_to_all(a, axis, 0, 0, tiled=True)  24.4 us
    pallas_call x17, Pallas kernels, call(): pl.pallas_call(kernel, name=name, out_shape=shapes[0] if single else tupl...  18.2 us
    ppermute x3, waiting for transfers between devices, swapped(): return lax.ppermute(a, 'head', [(i, i ^ mask) for i in range(n_h)])  13.7 us
    ppermute x3, starting transfers between devices, swapped(): return lax.ppermute(a, 'head', [(i, i ^ mask) for i in range(n_h)])  12.9 us
  transfers between devices with their start and end apart: 7, of which 6 were waited for; matrix products, arithmetic and copies ran while one was open for 0% of the time, Pallas kernels for 5%

profile of v11, /device:TPU:1, one launch (start us, length us, event | category | flops | bytes accessed | tf_op | source)
XLA Modules:
  0.0 169.3 jit_solution(6088836874949497014)
XLA Ops:
  0.7 2.1 %local_states.1 = f32[8,72,128]{2,1,0:T(8,128)S(1)} custom-call(s32[1]{0:T(128)} %bitcast._.place_ref, bf16[256,256]{1,0:T(8,128)(2,1)} %x_ref.5, bf16[256,128]{1,0:T(8,128)(2,1)} %b_ref.5, f32[4,256]{1,0:T(4,128)} %df_ref.11, f32[4,256]{1,0:T(4,128)} %db_ref.11), custom_call_target="tpu_custom_call" | custom-call | tf_op jit(solution)/shard_map/local_states/pallas_call | solution.py:395
  2.9 12.5 %all_to_all.45.rec_ref.dec_ref = f32[8,72,128]{2,1,0:T(8,128)S(1)} all-to-all(f32[8,72,128]{2,1,0:T(8,128)S(1)} %local_states.1), channel_id=1, replica_groups=mesh['z_hi'=8,'z_lo'=2,'x'=4,'head'=8] {'z_lo','x'}, dimensions={0} | all-to-all | bytes 589824 | tf_op jit(solution)/shard_map/all_to_all | solution.py:407
  15.4 0.7 totals_up.1
  16.1 14.0 %all-to-all-start.1 = ((f32[8,40,128]{2,1,0:T(8,128)}), f32[8,40,128]{2,1,0:T(8,128)S(1)}, u32[]{:S(2)}, u32[]{:S(2)}) async-start(f32[8,40,128]{2,1,0:T(8,128)} %totals_up.1), calls=%async_computation.1 | async-start | bytes 327680 | tf_op jit(solution)/shard_map/all_to_all | solution.py:407
  30.2 2.1 %near_outputs.1 = (f32[256,256]{1,0:T(8,128)S(1)}, f32[256,256]{1,0:T(8,128)S(1)}) custom-call(f32[4]{0:T(128)S(1)} %copy-done.9, bf16[256,256]{1,0:T(8,128)(2,1)S(1)} %copy-done.1, bf16[256,128]{1,0:T(8,128)(2,1)S(1)} %copy-done.3, bf16[256,128]{1,0:T(8,128)(2,1)S(1)} %copy-done.4, f32[4,256]{1,0:T(4,128)S(1)} %copy-done.6, f32[4,256]{1,0:T(4,128)S(1)} %copy-done.7, ...), custom_call_target="tpu_custom_call" | custom-call | tf_op jit(solution)/shard_map/near_outputs/pallas_call | solution.py:395
  32.3 11.0 %all-to-all-done.1.zrec_ref.zdec_ref = f32[8,40,128]{2,1,0:T(8,128)S(1)} async-done(((f32[8,40,128]{2,1,0:T(8,128)}), f32[8,40,128]{2,1,0:T(8,128)S(1)}, u32[]{:S(2)}, u32[]{:S(2)}) %all-to-all-start.1) | async-done | bytes 163872 | tf_op jit(solution)/shard_map/all_to_all | solution.py:407
  43.4 9.3 %all_to_all.46.ent_ref = f32[8,64,128]{2,1,0:T(8,128)S(1)} all-to-all(f32[8,64,128]{2,1,0:T(8,128)S(1)} %entries_up.1), channel_id=1, replica_groups=mesh['z_hi'=8,'z_lo'=2,'x'=4,'head'=8] {'z_lo','x'}, dimensions={0} | all-to-all | bytes 524288 | tf_op jit(solution)/shard_map/all_to_all | solution.py:407
  52.7 1.0 outputs.1
  53.7 14.7 %all_to_all.47.sums_ref = f32[8,8,128]{2,1,0:T(8,128)S(1)} all-to-all(f32[8,8,128]{2,1,0:T(8,128)S(1)} %get-tuple-element.36), channel_id=1, replica_groups=mesh['z_hi'=8,'z_lo'=2,'x'=4,'head'=8] {'head'}, dimensions={0} | all-to-all | bytes 65536 | tf_op jit(solution)/shard_map/all_to_all | solution.py:407
  68.4 1.4 gradients.1
  69.8 19.6 %all_to_all.48.rec_ref = f32[8,320,128]{2,1,0:T(8,128)S(1)} all-to-all(f32[8,320,128]{2,1,0:T(8,128)S(1)} %get-tuple-element.38), channel_id=1, replica_groups=mesh['z_hi'=8,'z_lo'=2,'x'=4,'head'=8] {'z_lo','x'}, dimensions={0} | all-to-all | bytes 2621440 | tf_op jit(solution)/shard_map/all_to_all | solution.py:407
  89.4 0.8 totals_down.1
  90.2 3.4 %all-to-all-start.5 = ((f32[8,64,128]{2,1,0:T(8,128)}), f32[8,64,128]{2,1,0:T(8,128)S(1)}, u32[]{:S(2)}, u32[]{:S(2)}) async-start(f32[8,64,128]{2,1,0:T(8,128)} %totals_down.1), calls=%async_computation.5 | async-start | bytes 524288 | tf_op jit(solution)/shard_map/all_to_all | solution.py:407
  93.6 0.7 gate_gradient.1
  94.4 3.0 %near_gradients.1 = (f32[256,256]{1,0:T(8,128)S(1)}, f32[256,128]{1,0:T(8,128)S(1)}, f32[256,128]{1,0:T(8,128)S(1)}) custom-call(f32[4]{0:T(128)S(1)} %copy-done.9, bf16[256,256]{1,0:T(8,128)(2,1)S(1)} %copy-done.1, bf16[256,128]{1,0:T(8,128)(2,1)S(1)} %copy-done.3, bf16[256,128]{1,0:T(8,128)(2,1)S(1)} %copy-done.4, f32[4,256]{1,0:T(4,128)S(1)} %copy-done.6, ...), custom_call_target="tpu_custom_call" | custom-call | tf_op jit(solution)/shard_map/near_gradients/pallas_call | solution.py:395
  97.4 13.8 %all-to-all-done.5.zrec_ref = f32[8,64,128]{2,1,0:T(8,128)S(1)} async-done(((f32[8,64,128]{2,1,0:T(8,128)}), f32[8,64,128]{2,1,0:T(8,128)S(1)}, u32[]{:S(2)}, u32[]{:S(2)}) %all-to-all-start.5) | async-done | bytes 262176 | tf_op jit(solution)/shard_map/all_to_all | solution.py:407
  111.1 0.7 entries_down.1
  111.8 8.5 %all_to_all.49.exit_ref = f32[8,64,128]{2,1,0:T(8,128)S(1)} all-to-all(f32[8,64,128]{2,1,0:T(8,128)S(1)} %get-tuple-element.45), channel_id=1, replica_groups=mesh['z_hi'=8,'z_lo'=2,'x'=4,'head'=8] {'z_lo','x'}, dimensions={0} | all-to-all | bytes 524288 | tf_op jit(solution)/shard_map/all_to_all | solution.py:407
  120.3 1.2 finish.1.a_ref
  121.5 7.9 %collective-permute-start = (f32[2,256,128]{2,1,0:T(8,128)S(1)}, f32[2,256,128]{2,1,0:T(8,128)S(1)}, u32[]{:S(2)}, u32[]{:S(2)}) collective-permute-start(f32[2,256,128]{2,1,0:T(8,128)S(1)} %finish.1.a_ref), channel_id=1, source_target_pairs={{0,1},{1,0},{2,3},{3,2},{4,5},{5,4},{6,7},{7,6},{8,9},{9,8},{10,11... | collective-permute-start | bytes 786440 | tf_op jit(solution)/shard_map/ppermute | solution.py:411
  129.4 3.4 %all-to-all-start.7 = ((f32[8,32,128]{2,1,0:T(8,128)}), f32[8,32,128]{2,1,0:T(8,128)S(1)}, u32[]{:S(2)}, u32[]{:S(2)}) async-start(f32[8,32,128]{2,1,0:T(8,128)} %get-tuple-element.50), calls=%async_computation.7 | async-start | bytes 262144 | tf_op jit(solution)/shard_map/all_to_all | solution.py:407
  132.8 2.2 %collective-permute-start.1 = (f32[2,256,128]{2,1,0:T(8,128)S(1)}, f32[2,256,128]{2,1,0:T(8,128)S(1)}, u32[]{:S(2)}, u32[]{:S(2)}) collective-permute-start(f32[2,256,128]{2,1,0:T(8,128)S(1)} %add_core.1.a_ref), channel_id=1, source_target_pairs={{0,2},{1,3},{2,0},{3,1},{4,6},{5,7},{6,4},{7,5},{8,10},{9,11},{10,... | collective-permute-start | bytes 786440 | tf_op jit(solution)/shard_map/ppermute | solution.py:411
  135.0 7.6 %collective-permute-done.1.b_ref = f32[2,256,128]{2,1,0:T(8,128)S(1)} collective-permute-done((f32[2,256,128]{2,1,0:T(8,128)S(1)}, f32[2,256,128]{2,1,0:T(8,128)S(1)}, u32[]{:S(2)}, u32[]{:S(2)}) %collective-permute-start.1) | collective-permute-done | bytes 262176 | tf_op jit(solution)/shard_map/ppermute | solution.py:411
  142.7 6.1 %all-to-all-done.7.rec_ref = f32[8,32,128]{2,1,0:T(8,128)S(1)} async-done(((f32[8,32,128]{2,1,0:T(8,128)}), f32[8,32,128]{2,1,0:T(8,128)S(1)}, u32[]{:S(2)}, u32[]{:S(2)}) %all-to-all-start.7) | async-done | bytes 131104 | tf_op jit(solution)/shard_map/all_to_all | solution.py:407
  148.7 1.0 weight_copy.1
  149.8 3.6 %all-to-all-start.8 = ((f32[8,256,128]{2,1,0:T(8,128)}), f32[8,256,128]{2,1,0:T(8,128)S(1)}, u32[]{:S(2)}, u32[]{:S(2)}) async-start(f32[8,256,128]{2,1,0:T(8,128)} %weight_copy.1), calls=%async_computation.8 | async-start | bytes 2097152 | tf_op jit(solution)/shard_map/all_to_all | solution.py:407
  153.3 2.8 %collective-permute-start.2 = (f32[2,256,128]{2,1,0:T(8,128)S(1)}, f32[2,256,128]{2,1,0:T(8,128)S(1)}, u32[]{:S(2)}, u32[]{:S(2)}) collective-permute-start(f32[2,256,128]{2,1,0:T(8,128)S(1)} %add_y.1.a_ref), channel_id=1, source_target_pairs={{0,6},{1,7},{2,4},{3,5},{4,2},{5,3},{6,0},{7,1},{8,14},{9,15},{10,... | collective-permute-start | bytes 786440 | tf_op jit(solution)/shard_map/ppermute | solution.py:411
  156.1 1.5 finish_x.1
  157.7 6.1 %collective-permute-done.2.b_ref = f32[2,256,128]{2,1,0:T(8,128)S(1)} collective-permute-done((f32[2,256,128]{2,1,0:T(8,128)S(1)}, f32[2,256,128]{2,1,0:T(8,128)S(1)}, u32[]{:S(2)}, u32[]{:S(2)}) %collective-permute-start.2) | collective-permute-done | bytes 262176 | tf_op jit(solution)/shard_map/ppermute | solution.py:411
  163.8 0.7 add_last.1
  164.5 3.7 %all-to-all-done.8.rec_ref = f32[8,256,128]{2,1,0:T(8,128)S(1)} async-done(((f32[8,256,128]{2,1,0:T(8,128)}), f32[8,256,128]{2,1,0:T(8,128)S(1)}, u32[]{:S(2)}, u32[]{:S(2)}) %all-to-all-start.8) | async-done | bytes 1048608 | tf_op jit(solution)/shard_map/all_to_all | solution.py:407
  168.2 1.0 weight_rows.1
  (24 shorter events, 0.2 us)
Async XLA Ops:
  0.6 29.5 %copy-start.7 = (f32[4,256]{1,0:T(4,128)S(1)}, f32[4,256]{1,0:T(4,128)}, u32[]{:S(2)}) copy-start(f32[4,256]{1,0:T(4,128)} %db_ref.11) | copy-start | bytes 12292
  0.6 29.5 %copy-start.6 = (f32[4,256]{1,0:T(4,128)S(1)}, f32[4,256]{1,0:T(4,128)}, u32[]{:S(2)}) copy-start(f32[4,256]{1,0:T(4,128)} %df_ref.11) | copy-start | bytes 12292
  0.7 29.5 %copy-start.3 = (bf16[256,128]{1,0:T(8,128)(2,1)S(1)}, bf16[256,128]{1,0:T(8,128)(2,1)}, u32[]{:S(2)}) copy-start(bf16[256,128]{1,0:T(8,128)(2,1)} %b_ref.5) | copy-start | bytes 196612
  0.7 29.5 %copy-start.1 = (bf16[256,256]{1,0:T(8,128)(2,1)S(1)}, bf16[256,256]{1,0:T(8,128)(2,1)}, u32[]{:S(2)}) copy-start(bf16[256,256]{1,0:T(8,128)(2,1)} %x_ref.5) | copy-start | bytes 393220
  0.7 29.5 %copy-start.4 = (bf16[256,128]{1,0:T(8,128)(2,1)S(1)}, bf16[256,128]{1,0:T(8,128)(2,1)}, u32[]{:S(2)}) copy-start(bf16[256,128]{1,0:T(8,128)(2,1)} %c_ref.7) | copy-start | bytes 196612
  0.7 29.5 %copy-start = (bf16[256,1024]{1,0:T(8,128)(2,1)S(1)}, bf16[256,1024]{1,0:T(8,128)(2,1)}, u32[]{:S(2)}) copy-start(bf16[256,1024]{1,0:T(8,128)(2,1)} %do_ref.3) | copy-start | bytes 1572868
  0.7 29.5 %copy-start.9 = (f32[4]{0:T(128)S(1)}, f32[4]{0:T(128)}, u32[]{:S(2)}) copy-start(f32[4]{0:T(128)} %skip_ref.3) | copy-start | bytes 52
  0.7 29.5 %copy-start.5 = (bf16[256,1024]{1,0:T(8,128)(2,1)S(1)}, bf16[256,1024]{1,0:T(8,128)(2,1)}, u32[]{:S(2)}) copy-start(bf16[256,1024]{1,0:T(8,128)(2,1)} %w_ref.1) | copy-start | bytes 1572868
  0.7 29.5 %copy-start.8 = (f32[256]{0:T(256)S(1)}, f32[256]{0:T(256)}, u32[]{:S(2)}) copy-start(f32[256]{0:T(256)} %param.17) | copy-start | bytes 3076
  16.1 27.2 %all-to-all-start.1 = ((f32[8,40,128]{2,1,0:T(8,128)}), f32[8,40,128]{2,1,0:T(8,128)S(1)}, u32[]{:S(2)}, u32[]{:S(2)}) async-start(f32[8,40,128]{2,1,0:T(8,128)} %totals_up.1), calls=%async_computation.1 | async-start | bytes 327680 | tf_op jit(solution)/shard_map/all_to_all | solution.py:407
  30.1 22.6 %copy-start.2 = (bf16[256,256]{1,0:T(8,128)(2,1)S(1)}, bf16[256,256]{1,0:T(8,128)(2,1)}, u32[]{:S(2)}) copy-start(bf16[256,256]{1,0:T(8,128)(2,1)} %z_ref.5) | copy-start | bytes 393220
  90.2 20.9 %all-to-all-start.5 = ((f32[8,64,128]{2,1,0:T(8,128)}), f32[8,64,128]{2,1,0:T(8,128)S(1)}, u32[]{:S(2)}, u32[]{:S(2)}) async-start(f32[8,64,128]{2,1,0:T(8,128)} %totals_down.1), calls=%async_computation.5 | async-start | bytes 524288 | tf_op jit(solution)/shard_map/all_to_all | solution.py:407
  121.5 11.3 %collective-permute-start = (f32[2,256,128]{2,1,0:T(8,128)S(1)}, f32[2,256,128]{2,1,0:T(8,128)S(1)}, u32[]{:S(2)}, u32[]{:S(2)}) collective-permute-start(f32[2,256,128]{2,1,0:T(8,128)S(1)} %finish.1.a_ref), channel_id=1, source_target_pairs={{0,1},{1,0},{2,3},{3,2},{4,5},{5,4},{6,7},{7,6},{8,9},{9,8},{10,11... | collective-permute-start | bytes 786440 | tf_op jit(solution)/shard_map/ppermute | solution.py:411
  129.4 19.4 %all-to-all-start.7 = ((f32[8,32,128]{2,1,0:T(8,128)}), f32[8,32,128]{2,1,0:T(8,128)S(1)}, u32[]{:S(2)}, u32[]{:S(2)}) async-start(f32[8,32,128]{2,1,0:T(8,128)} %get-tuple-element.50), calls=%async_computation.7 | async-start | bytes 262144 | tf_op jit(solution)/shard_map/all_to_all | solution.py:407
  132.8 9.8 %collective-permute-start.1 = (f32[2,256,128]{2,1,0:T(8,128)S(1)}, f32[2,256,128]{2,1,0:T(8,128)S(1)}, u32[]{:S(2)}, u32[]{:S(2)}) collective-permute-start(f32[2,256,128]{2,1,0:T(8,128)S(1)} %add_core.1.a_ref), channel_id=1, source_target_pairs={{0,2},{1,3},{2,0},{3,1},{4,6},{5,7},{6,4},{7,5},{8,10},{9,11},{10,... | collective-permute-start | bytes 786440 | tf_op jit(solution)/shard_map/ppermute | solution.py:411
  149.8 18.5 %all-to-all-start.8 = ((f32[8,256,128]{2,1,0:T(8,128)}), f32[8,256,128]{2,1,0:T(8,128)S(1)}, u32[]{:S(2)}, u32[]{:S(2)}) async-start(f32[8,256,128]{2,1,0:T(8,128)} %weight_copy.1), calls=%async_computation.8 | async-start | bytes 2097152 | tf_op jit(solution)/shard_map/all_to_all | solution.py:407
  153.3 10.5 %collective-permute-start.2 = (f32[2,256,128]{2,1,0:T(8,128)S(1)}, f32[2,256,128]{2,1,0:T(8,128)S(1)}, u32[]{:S(2)}, u32[]{:S(2)}) collective-permute-start(f32[2,256,128]{2,1,0:T(8,128)S(1)} %add_y.1.a_ref), channel_id=1, source_target_pairs={{0,6},{1,7},{2,4},{3,5},{4,2},{5,3},{6,0},{7,1},{8,14},{9,15},{10,... | collective-permute-start | bytes 786440 | tf_op jit(solution)/shard_map/ppermute | solution.py:411

commit v12 on v10

--- a/solution.py
+++ b/solution.py
@@ -484,7 +484,8 @@
     own, give = call(finish, "finish", half * 2, core, x_in, *decays, exits, gb_near, gc_near, scalars=1)
     own = call(add_two, "add_core", half, own, swapped(give, 1, n_h))
     own = call(add_two, "add_y", half, own, swapped(own, 2, n_h))
-    weight, own = lax.optimization_barrier((weight, own))
+    grad_x = call(finish_x, "finish_x", [(square, BF16)], b_in, *decays, exits, gx_near)
+    weight, own, grad_x = lax.optimization_barrier((weight, own, grad_x))
 
     weight = call(weight_copy, "weight_copy", [((n, weights, LANES), F32)], weight)
     weight = exchange(weight, group)
@@ -492,7 +493,6 @@
 
     own = call(add_two, "add_y", half, own, swapped(own, 6, n_h))
     other = swapped(own, 1, n_h)
-    grad_x = call(finish_x, "finish_x", [(square, BF16)], b_in, *decays, exits, gx_near)
     grad_b, grad_c = call(deal_out, "deal_out", half * 2, core, own, other, scalars=1)
     return grad_x, grad_z, grad_b, grad_c, grad_w
 

time: 163 us -> 162 us (level)
  transfers between devices with their start and end apart: 8 -> 8, of which waited for: 5 -> 6; matrix products, arithmetic and copies ran while one was open for 0% -> 0% of each run, Pallas kernels for 6% -> 6%
where the time goes in v12:
time: 162 us; the launch traced here: 161 us
  blocking collectives  64.6 us (40%)
  starting transfers between devices  44 us (27%)
  waiting for transfers between devices  33.7 us (21%)
  Pallas kernels  18.2 us (11%)
    all_to_all x5, blocking collectives, exchange(): return lax.all_to_all(a, axis, 0, 0, tiled=True)  64.6 us
    all_to_all x4, starting transfers between devices, exchange(): return lax.all_to_all(a, axis, 0, 0, tiled=True)  27.3 us
    all_to_all x4, waiting for transfers between devices, exchange(): return lax.all_to_all(a, axis, 0, 0, tiled=True)  24.8 us
    pallas_call x18, Pallas kernels, call(): pl.pallas_call(kernel, name=name, out_shape=shapes[0] if single else tupl...  18.2 us
    ppermute x4, starting transfers between devices, swapped(): return lax.ppermute(a, 'head', [(i, i ^ mask) for i in range(n_h)])  16.7 us
    ppermute x4, waiting for transfers between devices, swapped(): return lax.ppermute(a, 'head', [(i, i ^ mask) for i in range(n_h)])  8.93 us
  transfers between devices with their start and end apart: 8, of which 6 were waited for; matrix products, arithmetic and copies ran while one was open for 0% of the time, Pallas kernels for 6%

profile of v12, /device:TPU:1, one launch (start us, length us, event | category | flops | bytes accessed | tf_op | source)
XLA Modules:
  0.0 161.4 jit_solution(16666156585938094031)
XLA Ops:
  0.7 2.1 %local_states.1 = f32[8,72,128]{2,1,0:T(8,128)S(1)} custom-call(s32[1]{0:T(128)} %bitcast._.place_ref, bf16[256,256]{1,0:T(8,128)(2,1)} %x_ref.5, bf16[256,128]{1,0:T(8,128)(2,1)} %b_ref.5, f32[4,256]{1,0:T(4,128)} %df_ref.11, f32[4,256]{1,0:T(4,128)} %db_ref.11), custom_call_target="tpu_custom_call" | custom-call | tf_op jit(solution)/shard_map/local_states/pallas_call | solution.py:403
  2.9 12.5 %all_to_all.45.rec_ref.dec_ref = f32[8,72,128]{2,1,0:T(8,128)S(1)} all-to-all(f32[8,72,128]{2,1,0:T(8,128)S(1)} %local_states.1), channel_id=1, replica_groups=mesh['z_hi'=8,'z_lo'=2,'x'=4,'head'=8] {'z_lo','x'}, dimensions={0} | all-to-all | bytes 589824 | tf_op jit(solution)/shard_map/all_to_all | solution.py:415
  15.4 0.7 totals_up.1
  16.1 14.0 %all-to-all-start.1 = ((f32[8,40,128]{2,1,0:T(8,128)}), f32[8,40,128]{2,1,0:T(8,128)S(1)}, u32[]{:S(2)}, u32[]{:S(2)}) async-start(f32[8,40,128]{2,1,0:T(8,128)} %totals_up.1), calls=%async_computation.1 | async-start | bytes 327680 | tf_op jit(solution)/shard_map/all_to_all | solution.py:415
  30.2 2.1 %near_outputs.1 = (f32[256,256]{1,0:T(8,128)S(1)}, f32[256,256]{1,0:T(8,128)S(1)}) custom-call(f32[4]{0:T(128)S(1)} %copy-done.9, bf16[256,256]{1,0:T(8,128)(2,1)S(1)} %copy-done.1, bf16[256,128]{1,0:T(8,128)(2,1)S(1)} %copy-done.3, bf16[256,128]{1,0:T(8,128)(2,1)S(1)} %copy-done.4, f32[4,256]{1,0:T(4,128)S(1)} %copy-done.6, f32[4,256]{1,0:T(4,128)S(1)} %copy-done.7, ...), custom_call_target="tpu_custom_call" | custom-call | tf_op jit(solution)/shard_map/near_outputs/pallas_call | solution.py:403
  32.3 11.0 %all-to-all-done.1.zrec_ref.zdec_ref = f32[8,40,128]{2,1,0:T(8,128)S(1)} async-done(((f32[8,40,128]{2,1,0:T(8,128)}), f32[8,40,128]{2,1,0:T(8,128)S(1)}, u32[]{:S(2)}, u32[]{:S(2)}) %all-to-all-start.1) | async-done | bytes 163872 | tf_op jit(solution)/shard_map/all_to_all | solution.py:415
  43.4 9.3 %all_to_all.46.ent_ref = f32[8,64,128]{2,1,0:T(8,128)S(1)} all-to-all(f32[8,64,128]{2,1,0:T(8,128)S(1)} %entries_up.1), channel_id=1, replica_groups=mesh['z_hi'=8,'z_lo'=2,'x'=4,'head'=8] {'z_lo','x'}, dimensions={0} | all-to-all | bytes 524288 | tf_op jit(solution)/shard_map/all_to_all | solution.py:415
  52.7 1.0 outputs.1
  53.7 14.7 %all_to_all.47.sums_ref = f32[8,8,128]{2,1,0:T(8,128)S(1)} all-to-all(f32[8,8,128]{2,1,0:T(8,128)S(1)} %get-tuple-element.39), channel_id=1, replica_groups=mesh['z_hi'=8,'z_lo'=2,'x'=4,'head'=8] {'head'}, dimensions={0} | all-to-all | bytes 65536 | tf_op jit(solution)/shard_map/all_to_all | solution.py:415
  68.4 1.4 gradients.1
  69.8 19.6 %all_to_all.48.rec_ref = f32[8,320,128]{2,1,0:T(8,128)S(1)} all-to-all(f32[8,320,128]{2,1,0:T(8,128)S(1)} %get-tuple-element.41), channel_id=1, replica_groups=mesh['z_hi'=8,'z_lo'=2,'x'=4,'head'=8] {'z_lo','x'}, dimensions={0} | all-to-all | bytes 2621440 | tf_op jit(solution)/shard_map/all_to_all | solution.py:415
  89.4 0.8 totals_down.1
  90.2 3.4 %all-to-all-start.5 = ((f32[8,64,128]{2,1,0:T(8,128)}), f32[8,64,128]{2,1,0:T(8,128)S(1)}, u32[]{:S(2)}, u32[]{:S(2)}) async-start(f32[8,64,128]{2,1,0:T(8,128)} %totals_down.1), calls=%async_computation.5 | async-start | bytes 524288 | tf_op jit(solution)/shard_map/all_to_all | solution.py:415
  93.6 0.7 gate_gradient.1
  94.4 3.0 %near_gradients.1 = (f32[256,256]{1,0:T(8,128)S(1)}, f32[256,128]{1,0:T(8,128)S(1)}, f32[256,128]{1,0:T(8,128)S(1)}) custom-call(f32[4]{0:T(128)S(1)} %copy-done.9, bf16[256,256]{1,0:T(8,128)(2,1)S(1)} %copy-done.1, bf16[256,128]{1,0:T(8,128)(2,1)S(1)} %copy-done.3, bf16[256,128]{1,0:T(8,128)(2,1)S(1)} %copy-done.4, f32[4,256]{1,0:T(4,128)S(1)} %copy-done.6, ...), custom_call_target="tpu_custom_call" | custom-call | tf_op jit(solution)/shard_map/near_gradients/pallas_call | solution.py:403
  97.4 13.8 %all-to-all-done.5.zrec_ref = f32[8,64,128]{2,1,0:T(8,128)S(1)} async-done(((f32[8,64,128]{2,1,0:T(8,128)}), f32[8,64,128]{2,1,0:T(8,128)S(1)}, u32[]{:S(2)}, u32[]{:S(2)}) %all-to-all-start.5) | async-done | bytes 262176 | tf_op jit(solution)/shard_map/all_to_all | solution.py:415
  111.8 8.5 %all_to_all.49.exit_ref = f32[8,64,128]{2,1,0:T(8,128)S(1)} all-to-all(f32[8,64,128]{2,1,0:T(8,128)S(1)} %get-tuple-element.48), channel_id=1, replica_groups=mesh['z_hi'=8,'z_lo'=2,'x'=4,'head'=8] {'z_lo','x'}, dimensions={0} | all-to-all | bytes 524288 | tf_op jit(solution)/shard_map/all_to_all | solution.py:415
  120.3 6.3 %all-to-all-start.7 = ((f32[8,32,128]{2,1,0:T(8,128)}), f32[8,32,128]{2,1,0:T(8,128)S(1)}, u32[]{:S(2)}, u32[]{:S(2)}) async-start(f32[8,32,128]{2,1,0:T(8,128)} %get-tuple-element.50), calls=%async_computation.7 | async-start | bytes 262144 | tf_op jit(solution)/shard_map/all_to_all | solution.py:415
  126.6 1.2 finish.1
  127.7 5.0 %collective-permute-start = (f32[256,128]{1,0:T(8,128)S(1)}, f32[256,128]{1,0:T(8,128)S(1)}, u32[]{:S(2)}, u32[]{:S(2)}) collective-permute-start(f32[256,128]{1,0:T(8,128)S(1)} %get-tuple-element.55), channel_id=1, source_target_pairs={{0,1},{1,0},{2,3},{3,2},{4,5},{5,4},{6,7},{7,6},{8,9},{9,8},{10,11... | collective-permute-start | bytes 393224 | tf_op jit(solution)/shard_map/ppermute | solution.py:419
  132.8 1.0 collective-permute-done.b_ref
  133.7 2.2 %collective-permute-start.1 = (f32[256,128]{1,0:T(8,128)S(1)}, f32[256,128]{1,0:T(8,128)S(1)}, u32[]{:S(2)}, u32[]{:S(2)}) collective-permute-start(f32[256,128]{1,0:T(8,128)S(1)} %add_core.1.a_ref), channel_id=1, source_target_pairs={{0,2},{1,3},{2,0},{3,1},{4,6},{5,7},{6,4},{7,5},{8,10},{9,11},{10,... | collective-permute-start | bytes 393224 | tf_op jit(solution)/shard_map/ppermute | solution.py:419
  135.9 1.5 finish_x.1
  137.5 2.9 %collective-permute-done.1.b_ref = f32[256,128]{1,0:T(8,128)S(1)} collective-permute-done((f32[256,128]{1,0:T(8,128)S(1)}, f32[256,128]{1,0:T(8,128)S(1)}, u32[]{:S(2)}, u32[]{:S(2)}) %collective-permute-start.1) | collective-permute-done | bytes 131104 | tf_op jit(solution)/shard_map/ppermute | solution.py:419
  140.4 1.0 weight_copy.1
  141.4 3.6 %all-to-all-start.8 = ((f32[8,256,128]{2,1,0:T(8,128)}), f32[8,256,128]{2,1,0:T(8,128)S(1)}, u32[]{:S(2)}, u32[]{:S(2)}) async-start(f32[8,256,128]{2,1,0:T(8,128)} %weight_copy.1), calls=%async_computation.8 | async-start | bytes 2097152 | tf_op jit(solution)/shard_map/all_to_all | solution.py:415
  145.0 2.8 %collective-permute-start.2 = (f32[256,128]{1,0:T(8,128)S(1)}, f32[256,128]{1,0:T(8,128)S(1)}, u32[]{:S(2)}, u32[]{:S(2)}) collective-permute-start(f32[256,128]{1,0:T(8,128)S(1)} %add_y.2.a_ref), channel_id=1, source_target_pairs={{0,6},{1,7},{2,4},{3,5},{4,2},{5,3},{6,0},{7,1},{8,14},{9,15},{10,... | collective-permute-start | bytes 393224 | tf_op jit(solution)/shard_map/ppermute | solution.py:419
  147.8 4.1 %collective-permute-done.2.b_ref = f32[256,128]{1,0:T(8,128)S(1)} collective-permute-done((f32[256,128]{1,0:T(8,128)S(1)}, f32[256,128]{1,0:T(8,128)S(1)}, u32[]{:S(2)}, u32[]{:S(2)}) %collective-permute-start.2) | collective-permute-done | bytes 131104 | tf_op jit(solution)/shard_map/ppermute | solution.py:419
  151.9 6.7 %collective-permute-start.3 = (f32[256,128]{1,0:T(8,128)S(1)}, f32[256,128]{1,0:T(8,128)S(1)}, u32[]{:S(2)}, u32[]{:S(2)}) collective-permute-start(f32[256,128]{1,0:T(8,128)S(1)} %add_y.3.own_ref), channel_id=1, source_target_pairs={{0,1},{1,0},{2,3},{3,2},{4,5},{5,4},{6,7},{7,6},{8,9},{9,8},{10,11... | collective-permute-start | bytes 393224 | tf_op jit(solution)/shard_map/ppermute | solution.py:419
  158.7 1.0 collective-permute-done.3.other_ref
  159.6 0.7 deal_out.1
  160.3 1.0 weight_rows.1
  (27 shorter events, 0.8 us)
Async XLA Ops:
  0.6 29.5 %copy-start.7 = (f32[4,256]{1,0:T(4,128)S(1)}, f32[4,256]{1,0:T(4,128)}, u32[]{:S(2)}) copy-start(f32[4,256]{1,0:T(4,128)} %db_ref.11) | copy-start | bytes 12292
  0.6 29.5 %copy-start.6 = (f32[4,256]{1,0:T(4,128)S(1)}, f32[4,256]{1,0:T(4,128)}, u32[]{:S(2)}) copy-start(f32[4,256]{1,0:T(4,128)} %df_ref.11) | copy-start | bytes 12292
  0.7 29.5 %copy-start.3 = (bf16[256,128]{1,0:T(8,128)(2,1)S(1)}, bf16[256,128]{1,0:T(8,128)(2,1)}, u32[]{:S(2)}) copy-start(bf16[256,128]{1,0:T(8,128)(2,1)} %b_ref.5) | copy-start | bytes 196612
  0.7 29.5 %copy-start.1 = (bf16[256,256]{1,0:T(8,128)(2,1)S(1)}, bf16[256,256]{1,0:T(8,128)(2,1)}, u32[]{:S(2)}) copy-start(bf16[256,256]{1,0:T(8,128)(2,1)} %x_ref.5) | copy-start | bytes 393220
  0.7 29.5 %copy-start.4 = (bf16[256,128]{1,0:T(8,128)(2,1)S(1)}, bf16[256,128]{1,0:T(8,128)(2,1)}, u32[]{:S(2)}) copy-start(bf16[256,128]{1,0:T(8,128)(2,1)} %c_ref.7) | copy-start | bytes 196612
  0.7 29.5 %copy-start = (bf16[256,1024]{1,0:T(8,128)(2,1)S(1)}, bf16[256,1024]{1,0:T(8,128)(2,1)}, u32[]{:S(2)}) copy-start(bf16[256,1024]{1,0:T(8,128)(2,1)} %do_ref.3) | copy-start | bytes 1572868
  0.7 29.5 %copy-start.9 = (f32[4]{0:T(128)S(1)}, f32[4]{0:T(128)}, u32[]{:S(2)}) copy-start(f32[4]{0:T(128)} %skip_ref.3) | copy-start | bytes 52
  0.7 29.5 %copy-start.5 = (bf16[256,1024]{1,0:T(8,128)(2,1)S(1)}, bf16[256,1024]{1,0:T(8,128)(2,1)}, u32[]{:S(2)}) copy-start(bf16[256,1024]{1,0:T(8,128)(2,1)} %w_ref.1) | copy-start | bytes 1572868
  0.7 29.5 %copy-start.8 = (f32[256]{0:T(256)S(1)}, f32[256]{0:T(256)}, u32[]{:S(2)}) copy-start(f32[256]{0:T(256)} %param.17) | copy-start | bytes 3076
  16.1 27.2 %all-to-all-start.1 = ((f32[8,40,128]{2,1,0:T(8,128)}), f32[8,40,128]{2,1,0:T(8,128)S(1)}, u32[]{:S(2)}, u32[]{:S(2)}) async-start(f32[8,40,128]{2,1,0:T(8,128)} %totals_up.1), calls=%async_computation.1 | async-start | bytes 327680 | tf_op jit(solution)/shard_map/all_to_all | solution.py:415
  30.1 22.6 %copy-start.2 = (bf16[256,256]{1,0:T(8,128)(2,1)S(1)}, bf16[256,256]{1,0:T(8,128)(2,1)}, u32[]{:S(2)}) copy-start(bf16[256,256]{1,0:T(8,128)(2,1)} %z_ref.5) | copy-start | bytes 393220
  90.2 20.9 %all-to-all-start.5 = ((f32[8,64,128]{2,1,0:T(8,128)}), f32[8,64,128]{2,1,0:T(8,128)S(1)}, u32[]{:S(2)}, u32[]{:S(2)}) async-start(f32[8,64,128]{2,1,0:T(8,128)} %totals_down.1), calls=%async_computation.5 | async-start | bytes 524288 | tf_op jit(solution)/shard_map/all_to_all | solution.py:415
  120.3 20.1 %all-to-all-start.7 = ((f32[8,32,128]{2,1,0:T(8,128)}), f32[8,32,128]{2,1,0:T(8,128)S(1)}, u32[]{:S(2)}, u32[]{:S(2)}) async-start(f32[8,32,128]{2,1,0:T(8,128)} %get-tuple-element.50), calls=%async_computation.7 | async-start | bytes 262144 | tf_op jit(solution)/shard_map/all_to_all | solution.py:415
  127.7 6.0 %collective-permute-start = (f32[256,128]{1,0:T(8,128)S(1)}, f32[256,128]{1,0:T(8,128)S(1)}, u32[]{:S(2)}, u32[]{:S(2)}) collective-permute-start(f32[256,128]{1,0:T(8,128)S(1)} %get-tuple-element.55), channel_id=1, source_target_pairs={{0,1},{1,0},{2,3},{3,2},{4,5},{5,4},{6,7},{7,6},{8,9},{9,8},{10,11... | collective-permute-start | bytes 393224 | tf_op jit(solution)/shard_map/ppermute | solution.py:419
  133.7 6.6 %collective-permute-start.1 = (f32[256,128]{1,0:T(8,128)S(1)}, f32[256,128]{1,0:T(8,128)S(1)}, u32[]{:S(2)}, u32[]{:S(2)}) collective-permute-start(f32[256,128]{1,0:T(8,128)S(1)} %add_core.1.a_ref), channel_id=1, source_target_pairs={{0,2},{1,3},{2,0},{3,1},{4,6},{5,7},{6,4},{7,5},{8,10},{9,11},{10,... | collective-permute-start | bytes 393224 | tf_op jit(solution)/shard_map/ppermute | solution.py:419
  141.4 18.9 %all-to-all-start.8 = ((f32[8,256,128]{2,1,0:T(8,128)}), f32[8,256,128]{2,1,0:T(8,128)S(1)}, u32[]{:S(2)}, u32[]{:S(2)}) async-start(f32[8,256,128]{2,1,0:T(8,128)} %weight_copy.1), calls=%async_computation.8 | async-start | bytes 2097152 | tf_op jit(solution)/shard_map/all_to_all | solution.py:415
  145.0 6.9 %collective-permute-start.2 = (f32[256,128]{1,0:T(8,128)S(1)}, f32[256,128]{1,0:T(8,128)S(1)}, u32[]{:S(2)}, u32[]{:S(2)}) collective-permute-start(f32[256,128]{1,0:T(8,128)S(1)} %add_y.2.a_ref), channel_id=1, source_target_pairs={{0,6},{1,7},{2,4},{3,5},{4,2},{5,3},{6,0},{7,1},{8,14},{9,15},{10,... | collective-permute-start | bytes 393224 | tf_op jit(solution)/shard_map/ppermute | solution.py:419
  151.9 7.7 %collective-permute-start.3 = (f32[256,128]{1,0:T(8,128)S(1)}, f32[256,128]{1,0:T(8,128)S(1)}, u32[]{:S(2)}, u32[]{:S(2)}) collective-permute-start(f32[256,128]{1,0:T(8,128)S(1)} %add_y.3.own_ref), channel_id=1, source_target_pairs={{0,1},{1,0},{2,3},{3,2},{4,5},{5,4},{6,7},{7,6},{8,9},{9,8},{10,11... | collective-permute-start | bytes 393224 | tf_op jit(solution)/shard_map/ppermute | solution.py:419

commit v13 on v12

--- a/solution.py
+++ b/solution.py
@@ -227,21 +227,11 @@
 
 
 def weight_copy(rec_ref, out_ref):
-    n_g, part = rec_ref.shape[0], rec_ref.shape[1]
+    n_g, size = rec_ref.shape[0], rec_ref.shape[1]
     for k in range(n_g):
-        rows = rec_ref[k, :, :]
-        for i in range(out_ref.shape[0]):
-            out_ref[i, k * part : (k + 1) * part, :] = rows
-
-
-def weight_rows(rec_ref, gw_ref):
-    n = rec_ref.shape[0]
-    size = WIDTH // n
-    for i in range(n):
-        for block in range(gw_ref.shape[1] // LANES):
-            gw_ref[i * size : (i + 1) * size, block * LANES : (block + 1) * LANES] = (
-                rec_ref[i, block * size : (block + 1) * size, :] * WEIGHT_SCALE
-            )
+        rows = rec_ref[k, :, :] * WEIGHT_SCALE
+        for i in range(out_ref.shape[0] // size):
+            out_ref[i * size : (i + 1) * size, k * LANES : (k + 1) * LANES] = rows
 
 
 def across_rows(cols):
@@ -487,9 +477,8 @@
     grad_x = call(finish_x, "finish_x", [(square, BF16)], b_in, *decays, exits, gx_near)
     weight, own, grad_x = lax.optimization_barrier((weight, own, grad_x))
 
-    weight = call(weight_copy, "weight_copy", [((n, weights, LANES), F32)], weight)
-    weight = exchange(weight, group)
-    grad_w = call(weight_rows, "weight_rows", [((WIDTH, model), F32)], weight)
+    weight = weight.reshape(model // LANES, size, LANES)
+    grad_w = exchange(call(weight_copy, "weight_copy", [((WIDTH, model), F32)], weight), group)
 
     own = call(add_two, "add_y", half, own, swapped(own, 6, n_h))
     other = swapped(own, 1, n_h)

time: 162 us -> 162 us (level)
    pallas_call x18 -> x17, Pallas kernels: 18.2 us -> 17.2 us  [call(): pl.pallas_call(kernel, name=name, out_shape=shapes[0] if single else tupl...]
where the time goes in v13:
time: 162 us; the launch traced here: 161 us
  blocking collectives  64.6 us (40%)
  starting transfers between devices  44 us (27%)
  waiting for transfers between devices  33.7 us (21%)
  Pallas kernels  17.2 us (11%)
    all_to_all x5, blocking collectives, exchange(): return lax.all_to_all(a, axis, 0, 0, tiled=True)  64.6 us
    all_to_all x4, starting transfers between devices, exchange(): return lax.all_to_all(a, axis, 0, 0, tiled=True)  27.3 us
    all_to_all x4, waiting for transfers between devices, exchange(): return lax.all_to_all(a, axis, 0, 0, tiled=True)  24.8 us
    pallas_call x17, Pallas kernels, call(): pl.pallas_call(kernel, name=name, out_shape=shapes[0] if single else tupl...  17.2 us
    ppermute x4, starting transfers between devices, swapped(): return lax.ppermute(a, 'head', [(i, i ^ mask) for i in range(n_h)])  16.7 us
    ppermute x4, waiting for transfers between devices, swapped(): return lax.ppermute(a, 'head', [(i, i ^ mask) for i in range(n_h)])  8.93 us
  transfers between devices with their start and end apart: 8, of which 6 were waited for; matrix products, arithmetic and copies ran while one was open for 0% of the time, Pallas kernels for 6%

profile of v13, /device:TPU:1, one launch (start us, length us, event | category | flops | bytes accessed | tf_op | source)
XLA Modules:
  0.0 161.4 jit_solution(7316567404572615307)
XLA Ops:
  0.7 2.1 %local_states.1 = f32[8,72,128]{2,1,0:T(8,128)S(1)} custom-call(s32[1]{0:T(128)} %bitcast._.place_ref, bf16[256,256]{1,0:T(8,128)(2,1)} %x_ref.5, bf16[256,128]{1,0:T(8,128)(2,1)} %b_ref.5, f32[4,256]{1,0:T(4,128)} %df_ref.11, f32[4,256]{1,0:T(4,128)} %db_ref.11), custom_call_target="tpu_custom_call" | custom-call | tf_op jit(solution)/shard_map/local_states/pallas_call | solution.py:393
  2.9 12.5 %all_to_all.52.rec_ref.dec_ref = f32[8,72,128]{2,1,0:T(8,128)S(1)} all-to-all(f32[8,72,128]{2,1,0:T(8,128)S(1)} %local_states.1), channel_id=1, replica_groups=mesh['z_hi'=8,'z_lo'=2,'x'=4,'head'=8] {'z_lo','x'}, dimensions={0} | all-to-all | bytes 589824 | tf_op jit(solution)/shard_map/all_to_all | solution.py:405
  15.4 0.7 totals_up.1
  16.1 14.0 %all-to-all-start.1 = ((f32[8,40,128]{2,1,0:T(8,128)}), f32[8,40,128]{2,1,0:T(8,128)S(1)}, u32[]{:S(2)}, u32[]{:S(2)}) async-start(f32[8,40,128]{2,1,0:T(8,128)} %totals_up.1), calls=%async_computation.1 | async-start | bytes 327680 | tf_op jit(solution)/shard_map/all_to_all | solution.py:405
  30.2 2.1 %near_outputs.1 = (f32[256,256]{1,0:T(8,128)S(1)}, f32[256,256]{1,0:T(8,128)S(1)}) custom-call(f32[4]{0:T(128)S(1)} %copy-done.9, bf16[256,256]{1,0:T(8,128)(2,1)S(1)} %copy-done.1, bf16[256,128]{1,0:T(8,128)(2,1)S(1)} %copy-done.3, bf16[256,128]{1,0:T(8,128)(2,1)S(1)} %copy-done.4, f32[4,256]{1,0:T(4,128)S(1)} %copy-done.6, f32[4,256]{1,0:T(4,128)S(1)} %copy-done.7, ...), custom_call_target="tpu_custom_call" | custom-call | tf_op jit(solution)/shard_map/near_outputs/pallas_call | solution.py:393
  32.3 11.0 %all-to-all-done.1.zrec_ref.zdec_ref = f32[8,40,128]{2,1,0:T(8,128)S(1)} async-done(((f32[8,40,128]{2,1,0:T(8,128)}), f32[8,40,128]{2,1,0:T(8,128)S(1)}, u32[]{:S(2)}, u32[]{:S(2)}) %all-to-all-start.1) | async-done | bytes 163872 | tf_op jit(solution)/shard_map/all_to_all | solution.py:405
  43.4 9.3 %all_to_all.53.ent_ref = f32[8,64,128]{2,1,0:T(8,128)S(1)} all-to-all(f32[8,64,128]{2,1,0:T(8,128)S(1)} %entries_up.1), channel_id=1, replica_groups=mesh['z_hi'=8,'z_lo'=2,'x'=4,'head'=8] {'z_lo','x'}, dimensions={0} | all-to-all | bytes 524288 | tf_op jit(solution)/shard_map/all_to_all | solution.py:405
  52.7 1.0 outputs.1
  53.7 14.7 %all_to_all.54.sums_ref = f32[8,8,128]{2,1,0:T(8,128)S(1)} all-to-all(f32[8,8,128]{2,1,0:T(8,128)S(1)} %get-tuple-element.39), channel_id=1, replica_groups=mesh['z_hi'=8,'z_lo'=2,'x'=4,'head'=8] {'head'}, dimensions={0} | all-to-all | bytes 65536 | tf_op jit(solution)/shard_map/all_to_all | solution.py:405
  68.4 1.4 gradients.1
  69.8 19.6 %all_to_all.55.rec_ref = f32[8,320,128]{2,1,0:T(8,128)S(1)} all-to-all(f32[8,320,128]{2,1,0:T(8,128)S(1)} %get-tuple-element.41), channel_id=1, replica_groups=mesh['z_hi'=8,'z_lo'=2,'x'=4,'head'=8] {'z_lo','x'}, dimensions={0} | all-to-all | bytes 2621440 | tf_op jit(solution)/shard_map/all_to_all | solution.py:405
  89.4 0.8 totals_down.1
  90.2 3.4 %all-to-all-start.5 = ((f32[8,64,128]{2,1,0:T(8,128)}), f32[8,64,128]{2,1,0:T(8,128)S(1)}, u32[]{:S(2)}, u32[]{:S(2)}) async-start(f32[8,64,128]{2,1,0:T(8,128)} %totals_down.1), calls=%async_computation.5 | async-start | bytes 524288 | tf_op jit(solution)/shard_map/all_to_all | solution.py:405
  93.6 0.7 gate_gradient.1
  94.4 3.0 %near_gradients.1 = (f32[256,256]{1,0:T(8,128)S(1)}, f32[256,128]{1,0:T(8,128)S(1)}, f32[256,128]{1,0:T(8,128)S(1)}) custom-call(f32[4]{0:T(128)S(1)} %copy-done.9, bf16[256,256]{1,0:T(8,128)(2,1)S(1)} %copy-done.1, bf16[256,128]{1,0:T(8,128)(2,1)S(1)} %copy-done.3, bf16[256,128]{1,0:T(8,128)(2,1)S(1)} %copy-done.4, f32[4,256]{1,0:T(4,128)S(1)} %copy-done.6, ...), custom_call_target="tpu_custom_call" | custom-call | tf_op jit(solution)/shard_map/near_gradients/pallas_call | solution.py:393
  97.4 13.8 %all-to-all-done.5.zrec_ref = f32[8,64,128]{2,1,0:T(8,128)S(1)} async-done(((f32[8,64,128]{2,1,0:T(8,128)}), f32[8,64,128]{2,1,0:T(8,128)S(1)}, u32[]{:S(2)}, u32[]{:S(2)}) %all-to-all-start.5) | async-done | bytes 262176 | tf_op jit(solution)/shard_map/all_to_all | solution.py:405
  111.8 8.5 %all_to_all.56.exit_ref = f32[8,64,128]{2,1,0:T(8,128)S(1)} all-to-all(f32[8,64,128]{2,1,0:T(8,128)S(1)} %get-tuple-element.48), channel_id=1, replica_groups=mesh['z_hi'=8,'z_lo'=2,'x'=4,'head'=8] {'z_lo','x'}, dimensions={0} | all-to-all | bytes 524288 | tf_op jit(solution)/shard_map/all_to_all | solution.py:405
  120.3 6.3 %all-to-all-start.7 = ((f32[8,32,128]{2,1,0:T(8,128)}), f32[8,32,128]{2,1,0:T(8,128)S(1)}, u32[]{:S(2)}, u32[]{:S(2)}) async-start(f32[8,32,128]{2,1,0:T(8,128)} %get-tuple-element.50), calls=%async_computation.7 | async-start | bytes 262144 | tf_op jit(solution)/shard_map/all_to_all | solution.py:405
  126.6 1.2 finish.1
  127.7 5.0 %collective-permute-start = (f32[256,128]{1,0:T(8,128)S(1)}, f32[256,128]{1,0:T(8,128)S(1)}, u32[]{:S(2)}, u32[]{:S(2)}) collective-permute-start(f32[256,128]{1,0:T(8,128)S(1)} %get-tuple-element.55), channel_id=1, source_target_pairs={{0,1},{1,0},{2,3},{3,2},{4,5},{5,4},{6,7},{7,6},{8,9},{9,8},{10,11... | collective-permute-start | bytes 393224 | tf_op jit(solution)/shard_map/ppermute | solution.py:409
  132.8 1.0 collective-permute-done.b_ref
  133.7 2.2 %collective-permute-start.1 = (f32[256,128]{1,0:T(8,128)S(1)}, f32[256,128]{1,0:T(8,128)S(1)}, u32[]{:S(2)}, u32[]{:S(2)}) collective-permute-start(f32[256,128]{1,0:T(8,128)S(1)} %add_core.1.a_ref), channel_id=1, source_target_pairs={{0,2},{1,3},{2,0},{3,1},{4,6},{5,7},{6,4},{7,5},{8,10},{9,11},{10,... | collective-permute-start | bytes 393224 | tf_op jit(solution)/shard_map/ppermute | solution.py:409
  135.9 1.5 finish_x.1
  137.5 2.9 %collective-permute-done.1.b_ref = f32[256,128]{1,0:T(8,128)S(1)} collective-permute-done((f32[256,128]{1,0:T(8,128)S(1)}, f32[256,128]{1,0:T(8,128)S(1)}, u32[]{:S(2)}, u32[]{:S(2)}) %collective-permute-start.1) | collective-permute-done | bytes 131104 | tf_op jit(solution)/shard_map/ppermute | solution.py:409
  140.4 1.1 weight_copy.1
  141.5 3.6 %all-to-all-start.8 = ((f32[8,32,1024]{2,1,0:T(8,128)}), f32[8,32,1024]{2,1,0:T(8,128)S(1)}, u32[]{:S(2)}, u32[]{:S(2)}) async-start(f32[8,32,1024]{2,1,0:T(8,128)} %bitcast.3), calls=%async_computation.8 | async-start | bytes 2097152 | tf_op jit(solution)/shard_map/all_to_all | solution.py:405
  145.1 2.8 %collective-permute-start.2 = (f32[256,128]{1,0:T(8,128)S(1)}, f32[256,128]{1,0:T(8,128)S(1)}, u32[]{:S(2)}, u32[]{:S(2)}) collective-permute-start(f32[256,128]{1,0:T(8,128)S(1)} %add_y.2.a_ref), channel_id=1, source_target_pairs={{0,6},{1,7},{2,4},{3,5},{4,2},{5,3},{6,0},{7,1},{8,14},{9,15},{10,... | collective-permute-start | bytes 393224 | tf_op jit(solution)/shard_map/ppermute | solution.py:409
  147.9 4.1 %collective-permute-done.2.b_ref = f32[256,128]{1,0:T(8,128)S(1)} collective-permute-done((f32[256,128]{1,0:T(8,128)S(1)}, f32[256,128]{1,0:T(8,128)S(1)}, u32[]{:S(2)}, u32[]{:S(2)}) %collective-permute-start.2) | collective-permute-done | bytes 131104 | tf_op jit(solution)/shard_map/ppermute | solution.py:409
  152.0 6.7 %collective-permute-start.3 = (f32[256,128]{1,0:T(8,128)S(1)}, f32[256,128]{1,0:T(8,128)S(1)}, u32[]{:S(2)}, u32[]{:S(2)}) collective-permute-start(f32[256,128]{1,0:T(8,128)S(1)} %add_y.3.own_ref), channel_id=1, source_target_pairs={{0,1},{1,0},{2,3},{3,2},{4,5},{5,4},{6,7},{7,6},{8,9},{9,8},{10,11... | collective-permute-start | bytes 393224 | tf_op jit(solution)/shard_map/ppermute | solution.py:409
  158.7 1.0 collective-permute-done.3.other_ref
  159.7 0.7 deal_out.1
  160.4 1.0 copy.16
  (27 shorter events, 0.8 us)
Async XLA Ops:
  0.6 29.5 %copy-start.7 = (f32[4,256]{1,0:T(4,128)S(1)}, f32[4,256]{1,0:T(4,128)}, u32[]{:S(2)}) copy-start(f32[4,256]{1,0:T(4,128)} %db_ref.11) | copy-start | bytes 12292
  0.6 29.5 %copy-start.6 = (f32[4,256]{1,0:T(4,128)S(1)}, f32[4,256]{1,0:T(4,128)}, u32[]{:S(2)}) copy-start(f32[4,256]{1,0:T(4,128)} %df_ref.11) | copy-start | bytes 12292
  0.7 29.5 %copy-start.3 = (bf16[256,128]{1,0:T(8,128)(2,1)S(1)}, bf16[256,128]{1,0:T(8,128)(2,1)}, u32[]{:S(2)}) copy-start(bf16[256,128]{1,0:T(8,128)(2,1)} %b_ref.5) | copy-start | bytes 196612
  0.7 29.5 %copy-start.1 = (bf16[256,256]{1,0:T(8,128)(2,1)S(1)}, bf16[256,256]{1,0:T(8,128)(2,1)}, u32[]{:S(2)}) copy-start(bf16[256,256]{1,0:T(8,128)(2,1)} %x_ref.5) | copy-start | bytes 393220
  0.7 29.5 %copy-start.4 = (bf16[256,128]{1,0:T(8,128)(2,1)S(1)}, bf16[256,128]{1,0:T(8,128)(2,1)}, u32[]{:S(2)}) copy-start(bf16[256,128]{1,0:T(8,128)(2,1)} %c_ref.7) | copy-start | bytes 196612
  0.7 29.5 %copy-start = (bf16[256,1024]{1,0:T(8,128)(2,1)S(1)}, bf16[256,1024]{1,0:T(8,128)(2,1)}, u32[]{:S(2)}) copy-start(bf16[256,1024]{1,0:T(8,128)(2,1)} %do_ref.3) | copy-start | bytes 1572868
  0.7 29.5 %copy-start.9 = (f32[4]{0:T(128)S(1)}, f32[4]{0:T(128)}, u32[]{:S(2)}) copy-start(f32[4]{0:T(128)} %skip_ref.3) | copy-start | bytes 52
  0.7 29.5 %copy-start.5 = (bf16[256,1024]{1,0:T(8,128)(2,1)S(1)}, bf16[256,1024]{1,0:T(8,128)(2,1)}, u32[]{:S(2)}) copy-start(bf16[256,1024]{1,0:T(8,128)(2,1)} %w_ref.1) | copy-start | bytes 1572868
  0.7 29.5 %copy-start.8 = (f32[256]{0:T(256)S(1)}, f32[256]{0:T(256)}, u32[]{:S(2)}) copy-start(f32[256]{0:T(256)} %param.17) | copy-start | bytes 3076
  16.1 27.2 %all-to-all-start.1 = ((f32[8,40,128]{2,1,0:T(8,128)}), f32[8,40,128]{2,1,0:T(8,128)S(1)}, u32[]{:S(2)}, u32[]{:S(2)}) async-start(f32[8,40,128]{2,1,0:T(8,128)} %totals_up.1), calls=%async_computation.1 | async-start | bytes 327680 | tf_op jit(solution)/shard_map/all_to_all | solution.py:405
  30.1 22.6 %copy-start.2 = (bf16[256,256]{1,0:T(8,128)(2,1)S(1)}, bf16[256,256]{1,0:T(8,128)(2,1)}, u32[]{:S(2)}) copy-start(bf16[256,256]{1,0:T(8,128)(2,1)} %z_ref.5) | copy-start | bytes 393220
  90.2 20.9 %all-to-all-start.5 = ((f32[8,64,128]{2,1,0:T(8,128)}), f32[8,64,128]{2,1,0:T(8,128)S(1)}, u32[]{:S(2)}, u32[]{:S(2)}) async-start(f32[8,64,128]{2,1,0:T(8,128)} %totals_down.1), calls=%async_computation.5 | async-start | bytes 524288 | tf_op jit(solution)/shard_map/all_to_all | solution.py:405
  120.3 20.1 %all-to-all-start.7 = ((f32[8,32,128]{2,1,0:T(8,128)}), f32[8,32,128]{2,1,0:T(8,128)S(1)}, u32[]{:S(2)}, u32[]{:S(2)}) async-start(f32[8,32,128]{2,1,0:T(8,128)} %get-tuple-element.50), calls=%async_computation.7 | async-start | bytes 262144 | tf_op jit(solution)/shard_map/all_to_all | solution.py:405
  127.7 6.0 %collective-permute-start = (f32[256,128]{1,0:T(8,128)S(1)}, f32[256,128]{1,0:T(8,128)S(1)}, u32[]{:S(2)}, u32[]{:S(2)}) collective-permute-start(f32[256,128]{1,0:T(8,128)S(1)} %get-tuple-element.55), channel_id=1, source_target_pairs={{0,1},{1,0},{2,3},{3,2},{4,5},{5,4},{6,7},{7,6},{8,9},{9,8},{10,11... | collective-permute-start | bytes 393224 | tf_op jit(solution)/shard_map/ppermute | solution.py:409
  133.7 6.6 %collective-permute-start.1 = (f32[256,128]{1,0:T(8,128)S(1)}, f32[256,128]{1,0:T(8,128)S(1)}, u32[]{:S(2)}, u32[]{:S(2)}) collective-permute-start(f32[256,128]{1,0:T(8,128)S(1)} %add_core.1.a_ref), channel_id=1, source_target_pairs={{0,2},{1,3},{2,0},{3,1},{4,6},{5,7},{6,4},{7,5},{8,10},{9,11},{10,... | collective-permute-start | bytes 393224 | tf_op jit(solution)/shard_map/ppermute | solution.py:409
  141.5 18.9 %all-to-all-start.8 = ((f32[8,32,1024]{2,1,0:T(8,128)}), f32[8,32,1024]{2,1,0:T(8,128)S(1)}, u32[]{:S(2)}, u32[]{:S(2)}) async-start(f32[8,32,1024]{2,1,0:T(8,128)} %bitcast.3), calls=%async_computation.8 | async-start | bytes 2097152 | tf_op jit(solution)/shard_map/all_to_all | solution.py:405
  145.1 6.9 %collective-permute-start.2 = (f32[256,128]{1,0:T(8,128)S(1)}, f32[256,128]{1,0:T(8,128)S(1)}, u32[]{:S(2)}, u32[]{:S(2)}) collective-permute-start(f32[256,128]{1,0:T(8,128)S(1)} %add_y.2.a_ref), channel_id=1, source_target_pairs={{0,6},{1,7},{2,4},{3,5},{4,2},{5,3},{6,0},{7,1},{8,14},{9,15},{10,... | collective-permute-start | bytes 393224 | tf_op jit(solution)/shard_map/ppermute | solution.py:409
  152.0 7.7 %collective-permute-start.3 = (f32[256,128]{1,0:T(8,128)S(1)}, f32[256,128]{1,0:T(8,128)S(1)}, u32[]{:S(2)}, u32[]{:S(2)}) collective-permute-start(f32[256,128]{1,0:T(8,128)S(1)} %add_y.3.own_ref), channel_id=1, source_target_pairs={{0,1},{1,0},{2,3},{3,2},{4,5},{5,4},{6,7},{7,6},{8,9},{9,8},{10,11... | collective-permute-start | bytes 393224 | tf_op jit(solution)/shard_map/ppermute | solution.py:409
